TPU v7x, 32 devices: a whole 2x2x4 slice. The times are simulated.
32 devices in a mesh: seq: 16 (over z, y, core), tp: 2 (over x).
Axes of the slice: x: 2, y: 2, z: 4, core: 2. Of those that a mesh axis runs over, the one named last changes fastest.
Arguments:
- state: bfloat16 [2048, 1024], P('seq', 'tp'), may hold values from -16 to 16
- cotangent: float32 [2048, 1024], P('seq', 'tp'), may hold values from -40 to 40
- norm_gain: float32 [1024], replicated, may hold values from 0.5 to 1.5
- w_query: bfloat16 [1024, 1024], P(None, 'tp'), may hold values from -8 to 8
- w_key: bfloat16 [1024, 1024], P(None, 'tp'), may hold values from -1 to 1
- w_value: bfloat16 [1024, 1024], P(None, 'tp'), may hold values from -0.1875 to 0.1875
- w_out: bfloat16 [1024, 1024], P('tp'), may hold values from -1.5 to 1.5
Outputs:
- adjoint: float32 [2048, 1024], P('seq', 'tp')
- residual: float32 [2048, 1024], P('seq', 'tp')
All inputs are finite; a program needn't handle non-finite values.
Results may differ from a plain program's by a relative error of at most 0.025.
The roundings to bfloat16 on the way count: a program that leaves them out, or rounds other values in their place, can miss the bound.
Values may be sent and summed in bfloat16 or wider, within the bound.
No kernel may reach another device: no remote copies, remote signals or barrier semaphores. Data moves between devices by JAX's collectives and lax.ppermute only.
A program may use at most 64 MiB of HBM per device.

v0:
```python
import math

import jax
import jax.numpy as jnp
from jax import lax
from jax.sharding import PartitionSpec as P

HD = 128
WIN = 1024
SSTEP = 4


EPSILON = 1e-05


def shifted(array, axis, by):
    length = lax.axis_size(axis)
    pairs = [(i, i + by) for i in range(length) if 0 <= i + by < length]
    return lax.ppermute(array, axis, pairs)


def lower_solve(factor, values):
    result = []
    for index_i in range(values.shape[0]):
        running = values[index_i]
        for index_j in range(index_i):
            running = running - factor[index_i, index_j] * result[index_j]
        result.append(running / factor[index_i, index_i])
    return jnp.stack(result)


def upper_solve(factor, values):
    length_n = values.shape[0]
    result = [None] * length_n
    for index_i in range(length_n - 1, -1, -1):
        running = values[index_i]
        for index_j in range(index_i + 1, length_n):
            running = running - factor[index_j, index_i] * result[index_j]
        result[index_i] = running / factor[index_i, index_i]
    return jnp.stack(result)


def combine_coefficients(gram_matrix, right_side):
    factor = jnp.linalg.cholesky(gram_matrix)
    return upper_solve(factor, lower_solve(factor, right_side))


def on_device(state, cotangent, norm_gain, w_query, w_key, w_value, w_out):
    tok_rows = state.shape[0]
    cols_local = state.shape[1]
    attn_width = w_query.shape[1]
    heads_local = attn_width // HD
    half_span = WIN // 2
    edge_rows = min(tok_rows, half_span)
    reach_count = (half_span + tok_rows - 1) // tok_rows
    key_count = tok_rows + 2 * half_span
    total_rows = tok_rows * lax.axis_size("seq")
    first_row = lax.axis_index("seq") * tok_rows
    scale_factor = 1.0 / math.sqrt(HD)
    gain_local = lax.dynamic_slice_in_dim(
        norm_gain, lax.axis_index("tp") * cols_local, cols_local, 0
    )
    contract_last = (((1,), (1,)), ((), ()))
    full_state = lax.all_gather(state, "tp", axis=1, tiled=True)
    state_full = full_state.astype(jnp.float32)
    inverse = lax.rsqrt(jnp.mean(state_full * state_full, axis=1, keepdims=True) + EPSILON)
    normed = (state_full * inverse * norm_gain[None, :]).astype(jnp.bfloat16)
    w_inputs = jnp.concatenate([w_query, w_key, w_value], axis=1)
    projected = jnp.dot(normed, w_inputs, preferred_element_type=jnp.float32).astype(jnp.bfloat16)
    queries = projected[:, :attn_width].reshape(tok_rows, heads_local, HD)
    key_vecs = projected[:, attn_width : 2 * attn_width].reshape(tok_rows, heads_local, HD)
    values = projected[:, 2 * attn_width :].reshape(tok_rows, heads_local, HD)
    left_parts = []
    for offset in range(reach_count, 0, -1):
        left_parts.append(shifted((key_vecs, values), "seq", offset))
    right_parts = []
    for offset in range(1, reach_count + 1):
        right_parts.append(shifted((key_vecs, values), "seq", -offset))
    keys_all = jnp.concatenate(
        [received[0] for received in left_parts]
        + [key_vecs]
        + [received[0] for received in right_parts],
        axis=0,
    )
    values_all = jnp.concatenate(
        [received[1] for received in left_parts]
        + [values]
        + [received[1] for received in right_parts],
        axis=0,
    )
    query_pos = first_row + jnp.arange(tok_rows, dtype=jnp.int32)
    key_pos = first_row - half_span + jnp.arange(key_count, dtype=jnp.int32)
    distance = jnp.abs(key_pos[None, :] - query_pos[:, None])
    valid = ((distance <= half_span) & (key_pos[None, :] >= 0) & (key_pos[None, :] < total_rows))[
        None
    ]
    scores = (
        jnp.einsum("rhe,khe->hrk", queries, keys_all, preferred_element_type=jnp.float32)
        * scale_factor
    )
    row_peak = jnp.max(jnp.where(valid, scores, -jnp.inf), axis=2, keepdims=True)
    raw_weights = jnp.where(valid, jnp.exp(scores - row_peak), 0.0)
    row_total = jnp.sum(raw_weights, axis=2, keepdims=True)
    attn_probs = raw_weights / row_total
    probs_low = attn_probs.astype(jnp.bfloat16)
    attended = jnp.einsum("hrk,khe->rhe", probs_low, values_all, preferred_element_type=jnp.float32)
    krylov = [cotangent]
    differences = []
    for index_n in range(SSTEP):
        whole_vec = lax.all_gather(krylov[-1].astype(jnp.bfloat16), "tp", axis=1, tiled=True)
        grad_out = (
            lax.dot_general(whole_vec, w_out, contract_last, preferred_element_type=jnp.float32)
            .astype(jnp.bfloat16)
            .reshape(tok_rows, heads_local, HD)
        )
        row_corr = jnp.sum(grad_out.astype(jnp.float32) * attended, axis=2).T
        grad_prob = jnp.einsum(
            "rhe,khe->hrk", grad_out, values_all, preferred_element_type=jnp.float32
        )
        grad_score = (scale_factor * attn_probs * (grad_prob - row_corr[:, :, None])).astype(
            jnp.bfloat16
        )
        grad_query = jnp.einsum(
            "hrk,khe->rhe", grad_score, keys_all, preferred_element_type=jnp.float32
        ).astype(jnp.bfloat16)
        key_partial = jnp.einsum(
            "hrk,rhe->khe", grad_score, queries, preferred_element_type=jnp.float32
        )
        value_partial = jnp.einsum(
            "hrk,rhe->khe", probs_low, grad_out, preferred_element_type=jnp.float32
        )
        own_key = key_partial[half_span : half_span + tok_rows]
        own_value = value_partial[half_span : half_span + tok_rows]
        for cell_offset in range(1, reach_count + 1):
            lower_row = (reach_count - cell_offset) * edge_rows
            incoming = shifted(
                (
                    key_partial[lower_row : lower_row + edge_rows],
                    value_partial[lower_row : lower_row + edge_rows],
                ),
                "seq",
                -cell_offset,
            )
            own_key = own_key.at[tok_rows - edge_rows :].add(incoming[0])
            own_value = own_value.at[tok_rows - edge_rows :].add(incoming[1])
        for cell_offset in range(1, reach_count + 1):
            upper_row = half_span + tok_rows + (cell_offset - 1) * edge_rows
            incoming = shifted(
                (
                    key_partial[upper_row : upper_row + edge_rows],
                    value_partial[upper_row : upper_row + edge_rows],
                ),
                "seq",
                cell_offset,
            )
            own_key = own_key.at[:edge_rows].add(incoming[0])
            own_value = own_value.at[:edge_rows].add(incoming[1])
        grad_key = own_key.astype(jnp.bfloat16)
        grad_value = own_value.astype(jnp.bfloat16)
        stacked = jnp.concatenate(
            [
                grad_query.reshape(tok_rows, attn_width),
                grad_key.reshape(tok_rows, attn_width),
                grad_value.reshape(tok_rows, attn_width),
            ],
            axis=1,
        )
        partial_sum = lax.dot_general(
            stacked, w_inputs, contract_last, preferred_element_type=jnp.float32
        )
        summed = lax.psum_scatter(partial_sum, "tp", scatter_dimension=1, tiled=True)
        krylov.append(inverse * (gain_local[None, :] * summed))
        differences.append(krylov[index_n] - krylov[index_n + 1])
    diff_stack = jnp.stack(differences)
    local_gram = jnp.einsum("arc,brc->ab", diff_stack, diff_stack, precision=lax.Precision.HIGHEST)
    local_right = jnp.einsum("arc,rc->a", diff_stack, cotangent, precision=lax.Precision.HIGHEST)
    gram_matrix, right_side = lax.psum((local_gram, local_right), ("seq", "tp"))
    coefficients = combine_coefficients(gram_matrix, right_side)
    adjoint = coefficients[0] * krylov[0]
    residual = cotangent - coefficients[0] * differences[0]
    for index_n in range(1, SSTEP):
        adjoint = adjoint + coefficients[index_n] * krylov[index_n]
        residual = residual - coefficients[index_n] * differences[index_n]
    return (adjoint, residual)


def solution(mesh):
    in_specs = (
        P("seq", "tp"),
        P("seq", "tp"),
        P(),
        P(None, "tp"),
        P(None, "tp"),
        P(None, "tp"),
        P("tp", None),
    )
    out_specs = (P("seq", "tp"), P("seq", "tp"))
    return jax.shard_map(
        on_device, mesh=mesh, in_specs=in_specs, out_specs=out_specs, check_vma=False
    )
```

profile of v0, /device:TPU:0, one launch (start us, length us, event | category | flops | bytes accessed | tf_op | source)
XLA Modules:
  0.0 529.8 jit_solution(6957527849341988305)
XLA Ops:
  7.2 7.5 %all_gather.15 = bf16[128,1024]{1,0:T(8,128)(2,1)S(1)} all-gather(bf16[128,512]{1,0:T(8,128)(2,1)} %param.263), channel_id=1, replica_groups=mesh['seq'=16,'tp'=2] {'tp'}, dimensions={1}, use_global_device_ids=true | all-gather | bytes 393216 | tf_op jit(solution)/shard_map/all_gather | solution.py:64
  33.8 6.9 %all_gather.16 = bf16[128,1024]{1,0:T(8,128)(2,1)S(1)} all-gather(bf16[128,512]{1,0:T(8,128)(2,1)S(1)} %convert_element_type.111), channel_id=1, replica_groups=mesh['seq'=16,'tp'=2] {'tp'}, dimensions={1}, use_global_device_ids=true | all-gather | bytes 393216 | tf_op jit(solution)/shard_map/all_gather | solution.py:110
  48.6 7.1 %collective-permute-start.8 = (bf16[128,4,128]{2,0,1:T(8,128)(2,1)}, bf16[128,4,128]{2,0,1:T(8,128)(2,1)S(1)}, u32[]{:S(2)}, u32[]{:S(2)}) collective-permute-start(bf16[128,4,128]{2,0,1:T(8,128)(2,1)} %bitcast.147), channel_id=1, source_target_pairs={{0,8},{2,10},{4,12},{6,14},{8,16},{10,18},{12,20},{14,22},{16,24},... | collective-permute-start | bytes 393224 | tf_op jit(solution)/shard_map/ppermute | solution.py:19
  71.8 6.6 %collective-permute-done.13 = bf16[128,4,128]{2,0,1:T(8,128)(2,1)S(1)} collective-permute-done((bf16[128,4,128]{2,0,1:T(8,128)(2,1)}, bf16[128,4,128]{2,0,1:T(8,128)(2,1)S(1)}, u32[]{:S(2)}, u32[]{:S(2)}) %collective-permute-start.13) | collective-permute-done | bytes 131104 | tf_op jit(solution)/shard_map/ppermute | solution.py:19
  79.3 5.4 %collective-permute-done.15 = bf16[128,4,128]{2,0,1:T(8,128)(2,1)S(1)} collective-permute-done((bf16[128,4,128]{2,0,1:T(8,128)(2,1)}, bf16[128,4,128]{2,0,1:T(8,128)(2,1)S(1)}, u32[]{:S(2)}, u32[]{:S(2)}) %collective-permute-start.15) | collective-permute-done | bytes 131104 | tf_op jit(solution)/shard_map/ppermute | solution.py:19
  96.3 4.9 collective-permute-start.21
  101.5 5.1 collective-permute-start.22
  106.5 9.9 %collective-permute-start.23 = (f32[128,4,128]{0,2,1:T(8,128)S(1)}, f32[128,4,128]{0,2,1:T(8,128)S(1)}, u32[]{:S(2)}, u32[]{:S(2)}) collective-permute-start(f32[128,4,128]{0,2,1:T(8,128)S(1)} %get-tuple-element.1333), channel_id=1, source_target_pairs={{0,8},{2,10},{4,12},{6,14},{8,16},{10,18},{12,20},{14,22},{16,24},... | collective-permute-start | bytes 786440 | tf_op jit(solution)/shard_map/ppermute | solution.py:19
  130.3 5.1 collective-permute-start.30
  146.6 21.6 %reduce-scatter.5.cloned.1.call-done = f32[128,512]{1,0:T(8,128)} async-done(((f32[128,1024]{1,0:T(8,128)}), f32[128,512]{1,0:T(8,128)}) %reduce-scatter.5.cloned.1.call-update) | async-done | bytes 262160 | tf_op jit(solution)/shard_map/reduce_scatter | solution.py:171
  170.0 5.9 %all_gather.17 = bf16[128,1024]{1,0:T(8,128)(2,1)S(1)} all-gather(bf16[128,512]{1,0:T(8,128)(2,1)S(1)} %get-tuple-element.1354), channel_id=1, replica_groups=mesh['seq'=16,'tp'=2] {'tp'}, dimensions={1}, use_global_device_ids=true | all-gather | bytes 393216 | tf_op jit(solution)/shard_map/all_gather | solution.py:110
  202.3 9.8 %collective-permute-start.39 = (f32[128,4,128]{0,2,1:T(8,128)S(1)}, f32[128,4,128]{0,2,1:T(8,128)S(1)}, u32[]{:S(2)}, u32[]{:S(2)}) collective-permute-start(f32[128,4,128]{0,2,1:T(8,128)S(1)} %get-tuple-element.1317), channel_id=1, source_target_pairs={{0,8},{2,10},{4,12},{6,14},{8,16},{10,18},{12,20},{14,22},{16,24},... | collective-permute-start | bytes 786440 | tf_op jit(solution)/shard_map/ppermute | solution.py:19
  226.0 5.1 collective-permute-start.46
  242.9 20.4 %reduce-scatter.7.cloned.1.call-done = f32[128,512]{1,0:T(8,128)} async-done(((f32[128,1024]{1,0:T(8,128)}), f32[128,512]{1,0:T(8,128)}) %reduce-scatter.7.cloned.1.call-update) | async-done | bytes 262160 | tf_op jit(solution)/shard_map/reduce_scatter | solution.py:171
  265.2 5.7 %all_gather.18 = bf16[128,1024]{1,0:T(8,128)(2,1)S(1)} all-gather(bf16[128,512]{1,0:T(8,128)(2,1)S(1)} %get-tuple-element.1356), channel_id=1, replica_groups=mesh['seq'=16,'tp'=2] {'tp'}, dimensions={1}, use_global_device_ids=true | all-gather | bytes 393216 | tf_op jit(solution)/shard_map/all_gather | solution.py:110
  297.3 9.8 %collective-permute-start.55 = (f32[128,4,128]{0,2,1:T(8,128)S(1)}, f32[128,4,128]{0,2,1:T(8,128)S(1)}, u32[]{:S(2)}, u32[]{:S(2)}) collective-permute-start(f32[128,4,128]{0,2,1:T(8,128)S(1)} %get-tuple-element.1301), channel_id=1, source_target_pairs={{0,8},{2,10},{4,12},{6,14},{8,16},{10,18},{12,20},{14,22},{16,24},... | collective-permute-start | bytes 786440 | tf_op jit(solution)/shard_map/ppermute | solution.py:19
  316.0 4.9 collective-permute-start.61
  320.9 5.1 collective-permute-start.62
  337.9 20.4 %reduce-scatter.9.cloned.1.call-done = f32[128,512]{1,0:T(8,128)} async-done(((f32[128,1024]{1,0:T(8,128)}), f32[128,512]{1,0:T(8,128)}) %reduce-scatter.9.cloned.1.call-update) | async-done | bytes 262160 | tf_op jit(solution)/shard_map/reduce_scatter | solution.py:171
  360.2 6.0 %all_gather.19 = bf16[128,1024]{1,0:T(8,128)(2,1)S(1)} all-gather(bf16[128,512]{1,0:T(8,128)(2,1)S(1)} %get-tuple-element.1358), channel_id=1, replica_groups=mesh['seq'=16,'tp'=2] {'tp'}, dimensions={1}, use_global_device_ids=true | all-gather | bytes 393216 | tf_op jit(solution)/shard_map/all_gather | solution.py:110
  392.4 9.9 %collective-permute-start.71 = (f32[128,4,128]{0,2,1:T(8,128)S(1)}, f32[128,4,128]{0,2,1:T(8,128)S(1)}, u32[]{:S(2)}, u32[]{:S(2)}) collective-permute-start(f32[128,4,128]{0,2,1:T(8,128)S(1)} %get-tuple-element.1285), channel_id=1, source_target_pairs={{0,8},{2,10},{4,12},{6,14},{8,16},{10,18},{12,20},{14,22},{16,24},... | collective-permute-start | bytes 786440 | tf_op jit(solution)/shard_map/ppermute | solution.py:19
  416.2 5.1 collective-permute-start.78
  434.0 19.6 %reduce-scatter.11.cloned.1.call-done = f32[128,512]{1,0:T(8,128)} async-done(((f32[128,1024]{1,0:T(8,128)}), f32[128,512]{1,0:T(8,128)}) %reduce-scatter.11.cloned.1.call-update) | async-done | bytes 262160 | tf_op jit(solution)/shard_map/reduce_scatter | solution.py:171
  464.4 39.3 %all-reduce = (f32[4]{0:T(128)S(1)}, f32[4,4]{0,1:T(4,128)S(1)}) all-reduce(f32[4]{0:T(128)S(1)} %convolution_bitcast_fusion.10, f32[4,4]{0,1:T(4,128)S(1)} %convolution_bitcast_fusion.9), channel_id=1, replica_groups=mesh['seq'=16,'tp'=2] {'seq','tp'}, use_global_device_ids=true, to_apply=%region_11.12 | all-reduce | flops 20 | bytes 160 | tf_op jit(solution)/shard_map/psum | solution.py:177
  (315 shorter events, 252.1 us)
Async XLA Ops:
  7.2 161.0 %reduce-scatter.5.cloned.1.call-start = ((), (), s32[]{:S(2)}) async-start(), calls=%async_computation.4 | async-start | bytes 786432 | tf_op jit(solution)/shard_map/reduce_scatter | solution.py:171
  19.9 23.1 %collective-permute-start = (bf16[128,4,128]{2,0,1:T(8,128)(2,1)S(1)}, bf16[128,4,128]{2,0,1:T(8,128)(2,1)S(1)}, u32[]{:S(2)}, u32[]{:S(2)}) collective-permute-start(bf16[128,4,128]{2,0,1:T(8,128)(2,1)S(1)} %bitcast.175), channel_id=1, source_target_pairs={{0,8},{2,10},{4,12},{6,14},{8,16},{10,18},{12,20},{14,22},{16,24},... | collective-permute-start | bytes 393224 | tf_op jit(solution)/shard_map/ppermute | solution.py:19
  23.7 22.2 %collective-permute-start.1 = (bf16[128,4,128]{2,0,1:T(8,128)(2,1)S(1)}, bf16[128,4,128]{2,0,1:T(8,128)(2,1)S(1)}, u32[]{:S(2)}, u32[]{:S(2)}) collective-permute-start(bf16[128,4,128]{2,0,1:T(8,128)(2,1)S(1)} %bitcast.176), channel_id=1, source_target_pairs={{0,6},{2,8},{4,10},{6,12},{8,14},{10,16},{12,18},{14,20},{16,22},{... | collective-permute-start | bytes 393224 | tf_op jit(solution)/shard_map/ppermute | solution.py:19
  25.5 21.8 %collective-permute-start.2 = (bf16[128,4,128]{2,0,1:T(8,128)(2,1)S(1)}, bf16[128,4,128]{2,0,1:T(8,128)(2,1)S(1)}, u32[]{:S(2)}, u32[]{:S(2)}) collective-permute-start(bf16[128,4,128]{2,0,1:T(8,128)(2,1)S(1)} %bitcast.177), channel_id=1, source_target_pairs={{0,4},{2,6},{4,8},{6,10},{8,12},{10,14},{12,16},{14,18},{16,20},{1... | collective-permute-start | bytes 393224 | tf_op jit(solution)/shard_map/ppermute | solution.py:19
  28.9 19.7 %collective-permute-start.3 = (bf16[128,4,128]{2,0,1:T(8,128)(2,1)S(1)}, bf16[128,4,128]{2,0,1:T(8,128)(2,1)S(1)}, u32[]{:S(2)}, u32[]{:S(2)}) collective-permute-start(bf16[128,4,128]{2,0,1:T(8,128)(2,1)S(1)} %bitcast.178), channel_id=1, source_target_pairs={{0,2},{2,4},{4,6},{6,8},{8,10},{10,12},{12,14},{14,16},{16,18},{18... | collective-permute-start | bytes 393224 | tf_op jit(solution)/shard_map/ppermute | solution.py:19
  32.4 23.3 %collective-permute-start.4 = (bf16[128,4,128]{2,0,1:T(8,128)(2,1)S(1)}, bf16[128,4,128]{2,0,1:T(8,128)(2,1)S(1)}, u32[]{:S(2)}, u32[]{:S(2)}) collective-permute-start(bf16[128,4,128]{2,0,1:T(8,128)(2,1)S(1)} %bitcast.179), channel_id=1, source_target_pairs={{2,0},{4,2},{6,4},{8,6},{10,8},{12,10},{14,12},{16,14},{18,16},{20... | collective-permute-start | bytes 393224 | tf_op jit(solution)/shard_map/ppermute | solution.py:19
  91.4 25.0 %collective-permute-start.19 = (f32[128,4,128]{0,2,1:T(8,128)S(1)}, f32[128,4,128]{0,2,1:T(8,128)S(1)}, u32[]{:S(2)}, u32[]{:S(2)}) collective-permute-start(f32[128,4,128]{0,2,1:T(8,128)S(1)} %get-tuple-element.1337), channel_id=1, source_target_pairs={{8,0},{10,2},{12,4},{14,6},{16,8},{18,10},{20,12},{22,14},{24,16},... | collective-permute-start | bytes 786440 | tf_op jit(solution)/shard_map/ppermute | solution.py:19
  92.7 25.0 %collective-permute-start.20 = (f32[128,4,128]{0,2,1:T(8,128)S(1)}, f32[128,4,128]{0,2,1:T(8,128)S(1)}, u32[]{:S(2)}, u32[]{:S(2)}) collective-permute-start(f32[128,4,128]{0,2,1:T(8,128)S(1)} %get-tuple-element.1336), channel_id=1, source_target_pairs={{0,2},{2,4},{4,6},{6,8},{8,10},{10,12},{12,14},{14,16},{16,18},{18... | collective-permute-start | bytes 786440 | tf_op jit(solution)/shard_map/ppermute | solution.py:19
  96.3 22.8 %collective-permute-start.21 = (f32[128,4,128]{0,2,1:T(8,128)S(1)}, f32[128,4,128]{0,2,1:T(8,128)S(1)}, u32[]{:S(2)}, u32[]{:S(2)}) collective-permute-start(f32[128,4,128]{0,2,1:T(8,128)S(1)} %get-tuple-element.1335), channel_id=1, source_target_pairs={{0,4},{2,6},{4,8},{6,10},{8,12},{10,14},{12,16},{14,18},{16,20},{1... | collective-permute-start | bytes 786440 | tf_op jit(solution)/shard_map/ppermute | solution.py:19
  146.4 116.9 %reduce-scatter.7.cloned.1.call-start = ((), (), s32[]{:S(2)}) async-start(), calls=%async_computation.5 | async-start | bytes 786432 | tf_op jit(solution)/shard_map/reduce_scatter | solution.py:171
  187.2 25.0 %collective-permute-start.35 = (f32[128,4,128]{0,2,1:T(8,128)S(1)}, f32[128,4,128]{0,2,1:T(8,128)S(1)}, u32[]{:S(2)}, u32[]{:S(2)}) collective-permute-start(f32[128,4,128]{0,2,1:T(8,128)S(1)} %get-tuple-element.1321), channel_id=1, source_target_pairs={{8,0},{10,2},{12,4},{14,6},{16,8},{18,10},{20,12},{22,14},{24,16},... | collective-permute-start | bytes 786440 | tf_op jit(solution)/shard_map/ppermute | solution.py:19
  188.5 25.0 %collective-permute-start.36 = (f32[128,4,128]{0,2,1:T(8,128)S(1)}, f32[128,4,128]{0,2,1:T(8,128)S(1)}, u32[]{:S(2)}, u32[]{:S(2)}) collective-permute-start(f32[128,4,128]{0,2,1:T(8,128)S(1)} %get-tuple-element.1320), channel_id=1, source_target_pairs={{0,2},{2,4},{4,6},{6,8},{8,10},{10,12},{12,14},{14,16},{16,18},{18... | collective-permute-start | bytes 786440 | tf_op jit(solution)/shard_map/ppermute | solution.py:19
  192.0 22.7 %collective-permute-start.37 = (f32[128,4,128]{0,2,1:T(8,128)S(1)}, f32[128,4,128]{0,2,1:T(8,128)S(1)}, u32[]{:S(2)}, u32[]{:S(2)}) collective-permute-start(f32[128,4,128]{0,2,1:T(8,128)S(1)} %get-tuple-element.1319), channel_id=1, source_target_pairs={{0,4},{2,6},{4,8},{6,10},{8,12},{10,14},{12,16},{14,18},{16,20},{1... | collective-permute-start | bytes 786440 | tf_op jit(solution)/shard_map/ppermute | solution.py:19
  216.7 19.6 %collective-permute-start.43 = (f32[128,4,128]{0,2,1:T(8,128)S(1)}, f32[128,4,128]{0,2,1:T(8,128)S(1)}, u32[]{:S(2)}, u32[]{:S(2)}) collective-permute-start(f32[128,4,128]{0,2,1:T(8,128)S(1)} %get-tuple-element.1329), channel_id=1, source_target_pairs={{8,0},{10,2},{12,4},{14,6},{16,8},{18,10},{20,12},{22,14},{24,16},... | collective-permute-start | bytes 786440 | tf_op jit(solution)/shard_map/ppermute | solution.py:19
  242.9 115.4 %reduce-scatter.9.cloned.1.call-start = ((), (), s32[]{:S(2)}) async-start(), calls=%async_computation.6 | async-start | bytes 786432 | tf_op jit(solution)/shard_map/reduce_scatter | solution.py:171
  282.2 24.9 %collective-permute-start.51 = (f32[128,4,128]{0,2,1:T(8,128)S(1)}, f32[128,4,128]{0,2,1:T(8,128)S(1)}, u32[]{:S(2)}, u32[]{:S(2)}) collective-permute-start(f32[128,4,128]{0,2,1:T(8,128)S(1)} %get-tuple-element.1305), channel_id=1, source_target_pairs={{8,0},{10,2},{12,4},{14,6},{16,8},{18,10},{20,12},{22,14},{24,16},... | collective-permute-start | bytes 786440 | tf_op jit(solution)/shard_map/ppermute | solution.py:19
  283.5 24.9 %collective-permute-start.52 = (f32[128,4,128]{0,2,1:T(8,128)S(1)}, f32[128,4,128]{0,2,1:T(8,128)S(1)}, u32[]{:S(2)}, u32[]{:S(2)}) collective-permute-start(f32[128,4,128]{0,2,1:T(8,128)S(1)} %get-tuple-element.1304), channel_id=1, source_target_pairs={{0,2},{2,4},{4,6},{6,8},{8,10},{10,12},{12,14},{14,16},{16,18},{18... | collective-permute-start | bytes 786440 | tf_op jit(solution)/shard_map/ppermute | solution.py:19
  287.0 22.7 %collective-permute-start.53 = (f32[128,4,128]{0,2,1:T(8,128)S(1)}, f32[128,4,128]{0,2,1:T(8,128)S(1)}, u32[]{:S(2)}, u32[]{:S(2)}) collective-permute-start(f32[128,4,128]{0,2,1:T(8,128)S(1)} %get-tuple-element.1303), channel_id=1, source_target_pairs={{0,4},{2,6},{4,8},{6,10},{8,12},{10,14},{12,16},{14,18},{16,20},{1... | collective-permute-start | bytes 786440 | tf_op jit(solution)/shard_map/ppermute | solution.py:19
  311.6 19.6 %collective-permute-start.59 = (f32[128,4,128]{0,2,1:T(8,128)S(1)}, f32[128,4,128]{0,2,1:T(8,128)S(1)}, u32[]{:S(2)}, u32[]{:S(2)}) collective-permute-start(f32[128,4,128]{0,2,1:T(8,128)S(1)} %get-tuple-element.1313), channel_id=1, source_target_pairs={{8,0},{10,2},{12,4},{14,6},{16,8},{18,10},{20,12},{22,14},{24,16},... | collective-permute-start | bytes 786440 | tf_op jit(solution)/shard_map/ppermute | solution.py:19
  337.9 115.7 %reduce-scatter.11.cloned.1.call-start = ((), (), s32[]{:S(2)}) async-start(), calls=%async_computation.7 | async-start | bytes 786432 | tf_op jit(solution)/shard_map/reduce_scatter | solution.py:171
  377.4 24.9 %collective-permute-start.67 = (f32[128,4,128]{0,2,1:T(8,128)S(1)}, f32[128,4,128]{0,2,1:T(8,128)S(1)}, u32[]{:S(2)}, u32[]{:S(2)}) collective-permute-start(f32[128,4,128]{0,2,1:T(8,128)S(1)} %get-tuple-element.1289), channel_id=1, source_target_pairs={{8,0},{10,2},{12,4},{14,6},{16,8},{18,10},{20,12},{22,14},{24,16},... | collective-permute-start | bytes 786440 | tf_op jit(solution)/shard_map/ppermute | solution.py:19
  378.7 24.9 %collective-permute-start.68 = (f32[128,4,128]{0,2,1:T(8,128)S(1)}, f32[128,4,128]{0,2,1:T(8,128)S(1)}, u32[]{:S(2)}, u32[]{:S(2)}) collective-permute-start(f32[128,4,128]{0,2,1:T(8,128)S(1)} %get-tuple-element.1288), channel_id=1, source_target_pairs={{0,2},{2,4},{4,6},{6,8},{8,10},{10,12},{12,14},{14,16},{16,18},{18... | collective-permute-start | bytes 786440 | tf_op jit(solution)/shard_map/ppermute | solution.py:19
  382.3 22.7 %collective-permute-start.69 = (f32[128,4,128]{0,2,1:T(8,128)S(1)}, f32[128,4,128]{0,2,1:T(8,128)S(1)}, u32[]{:S(2)}, u32[]{:S(2)}) collective-permute-start(f32[128,4,128]{0,2,1:T(8,128)S(1)} %get-tuple-element.1287), channel_id=1, source_target_pairs={{0,4},{2,6},{4,8},{6,10},{8,12},{10,14},{12,16},{14,18},{16,20},{1... | collective-permute-start | bytes 786440 | tf_op jit(solution)/shard_map/ppermute | solution.py:19
  406.9 19.7 %collective-permute-start.75 = (f32[128,4,128]{0,2,1:T(8,128)S(1)}, f32[128,4,128]{0,2,1:T(8,128)S(1)}, u32[]{:S(2)}, u32[]{:S(2)}) collective-permute-start(f32[128,4,128]{0,2,1:T(8,128)S(1)} %get-tuple-element.1297), channel_id=1, source_target_pairs={{8,0},{10,2},{12,4},{14,6},{16,8},{18,10},{20,12},{22,14},{24,16},... | collective-permute-start | bytes 786440 | tf_op jit(solution)/shard_map/ppermute | solution.py:19
  (89 other events, 1331.9 us)
Sparse Core Ops, SparseCore 0:
  146.6 21.5 reduce-scatter.4
  243.0 20.2 reduce-scatter.6
  338.0 20.3 reduce-scatter.8
  433.3 20.2 reduce-scatter.10
where the time goes:
time: 533 us; the launch traced here: 530 us
  starting transfers between devices  238 us (45%)
  waiting for transfers between devices  117 us (22%)
  blocking collectives  71.3 us (13%)
  matrix products  38.8 us (7%)
  between operations  31.1 us (6%)
  local copies, waits for them, and re-layouts  17.7 us (3%)
  other arithmetic  15.5 us (3%)
    ppermute x80, starting transfers between devices, shifted(): return lax.ppermute(array, axis, pairs)  238 us
    reduce_scatter x4, waiting for transfers between devices, on_device(): lax.psum_scatter(partial_sum, 'tp', scatter_dimension=1, tiled=True)  82 us
    psum x1, blocking collectives, on_device(): gram_matrix, right_side = lax.psum((local_gram, local_right), ('seq', 'tp'))  39.3 us
    ppermute x80, waiting for transfers between devices, shifted(): return lax.ppermute(array, axis, pairs)  35.2 us
    all_gather x4, blocking collectives, on_device(): lax.all_gather(krylov[-1].astype(jnp.bfloat16), 'tp', axis=1, tiled=True)  24.5 us
  transfers between devices with their start and end apart: 84, of which 22 were waited for; matrix products, arithmetic and copies ran while one was open for 2% of the time, Pallas kernels for 0%

commit v1 on v0

v1 whole, which is shorter than its diff:
```python
import functools
import math

import jax
import jax.numpy as jnp
from jax import lax
from jax.experimental import pallas as pl
from jax.experimental.pallas import tpu as pltpu
from jax.sharding import PartitionSpec as P

HD = 128
WIN = 1024
SSTEP = 4
EPSILON = 1e-05
PAD = 16
NEG = -1e30
SCALE = 1.0 / math.sqrt(HD)
NT = (((1,), (1,)), ((), ()))
NN = (((1,), (0,)), ((), ()))
F32 = jnp.float32
BF16 = jnp.bfloat16


def mm(a, b, dims=NN):
    return lax.dot_general(a, b, dims, preferred_element_type=F32)


def col(h):
    return slice(h * HD, (h + 1) * HD)


def kernel_call(body, outs, ins, n_smem=0, scratch=(), flops=10**8, limit=24 << 20):
    in_specs = [pl.BlockSpec(memory_space=pltpu.SMEM)] * n_smem
    in_specs += [pl.BlockSpec(memory_space=pltpu.VMEM)] * (len(ins) - n_smem)
    moved = sum(math.prod(a.shape) * a.dtype.itemsize for a in list(ins) + list(outs))
    return pl.pallas_call(
        body,
        out_shape=[jax.ShapeDtypeStruct(o.shape, o.dtype) for o in outs],
        in_specs=in_specs,
        out_specs=[pl.BlockSpec(memory_space=pltpu.VMEM)] * len(outs),
        scratch_shapes=list(scratch),
        compiler_params=pltpu.CompilerParams(vmem_limit_bytes=limit),
        cost_estimate=pl.CostEstimate(flops=flops, bytes_accessed=moved, transcendentals=0),
    )(*ins)


def sds(*shape, dtype=F32):
    return jax.ShapeDtypeStruct(shape, dtype)


def parts_of(x):
    hi = x.astype(BF16).astype(F32)
    rest = x - hi
    mid = rest.astype(BF16).astype(F32)
    low = (rest - mid).astype(BF16).astype(F32)
    return [hi, mid, low]


def pack_rows(out_ref, rows, heads, columns):
    lane = lax.broadcasted_iota(jnp.int32, (rows, HD), 1)
    mat = jnp.zeros((rows, HD), F32)
    for i, c in enumerate(columns):
        mat = jnp.where(lane == i, c, mat)
    pieces = parts_of(mat.T)
    sub = lax.broadcasted_iota(jnp.int32, (PAD, rows), 0)
    for h in range(heads):
        tile = jnp.zeros((PAD, rows), F32)
        for kind in range(len(columns) // heads):
            r = kind * heads + h
            for i, piece in enumerate(pieces):
                tile = jnp.where(sub == 3 * kind + i, piece[r : r + 1, :], tile)
        out_ref[rows : rows + PAD, col(h)] = tile.astype(BF16)


def unpack_row(slots, rows, h, kind):
    pieces = []
    for s in slots:
        t = s[rows : rows + PAD, col(h)].astype(F32)
        k = 3 * kind
        pieces.append(t[k : k + 1] + t[k + 1 : k + 2] + t[k + 2 : k + 3])
    return jnp.concatenate(pieces, axis=1)


def project_body(x_ref, gain_ref, wq_ref, wk_ref, wv_ref, wo_ref, q_ref, kv_ref, go_ref, inv_ref):
    tps, _, rows, cols = x_ref.shape
    width = wq_ref.shape[1]
    xs = [x_ref[t, 0].astype(F32) for t in range(tps)]
    total = jnp.zeros((rows, 1), F32)
    for x in xs:
        total = total + jnp.sum(x * x, axis=1, keepdims=True)
    inverse = lax.rsqrt(total / (tps * cols) + EPSILON)
    inv_ref[...] = jnp.broadcast_to(inverse, inv_ref.shape)
    normed = jnp.concatenate(
        [
            (x * inverse * gain_ref[:, t * cols : (t + 1) * cols]).astype(BF16)
            for t, x in enumerate(xs)
        ],
        axis=1,
    )
    kv_ref[:, :width] = mm(normed, wk_ref[...]).astype(BF16)
    kv_ref[:, width:] = mm(normed, wv_ref[...]).astype(BF16)
    q_ref[...] = mm(normed, wq_ref[...]).astype(BF16)
    cot = jnp.concatenate([x_ref[t, 1] for t in range(tps)], axis=1)
    go_ref[...] = mm(cot, wo_ref[...], NT).astype(BF16)


def mask_of(start_ref, rows, slots, half):
    own = start_ref[0] + lax.broadcasted_iota(jnp.int32, (rows, rows), 0)
    lane = lax.broadcasted_iota(jnp.int32, (rows, rows), 1)
    pieces = []
    for b in range(slots):
        pieces.append(jnp.abs(start_ref[b] + lane - own) <= half)
    return pieces


def stats_body(slots, half, start_ref, *refs):
    kv = refs[:slots]
    q_ref, go_ref = refs[slots : slots + 2]
    p_ref, att_ref, packed_ref, kw_ref, vw_ref = refs[slots + 2 :]
    rows, width = q_ref.shape
    heads = width // HD
    for b in range(slots):
        kw_ref[b * rows : (b + 1) * rows, :] = kv[b][:, :width]
        vw_ref[b * rows : (b + 1) * rows, :] = kv[b][:, width:]
    masks = mask_of(start_ref, rows, slots, half)
    packed_ref[:rows, :] = go_ref[...]
    lse, corr = [], []
    for h in range(heads):
        s = mm(q_ref[:, col(h)], kw_ref[:, col(h)], NT) * SCALE
        s = jnp.concatenate(
            [
                jnp.where(masks[b], s[:, b * rows : (b + 1) * rows], NEG)
                for b in range(slots)
            ],
            axis=1,
        )
        peak = jnp.max(s, axis=1, keepdims=True)
        raw = jnp.exp(s - peak)
        total = jnp.sum(raw, axis=1, keepdims=True)
        probs = raw / total
        p_ref[h] = probs
        att = mm(probs.astype(BF16), vw_ref[:, col(h)])
        att_ref[:, col(h)] = att
        lse.append(peak + jnp.log(total))
        corr.append(jnp.sum(go_ref[:, col(h)].astype(F32) * att, axis=1, keepdims=True))
    pack_rows(packed_ref, rows, heads, corr + lse)


def scores_t_body(slots, half, start_ref, *refs):
    qs = refs[:slots]
    kv_ref = refs[slots]
    st_ref, qw_ref = refs[slots + 1 :]
    rows, width = qs[0].shape
    for b in range(slots):
        qw_ref[b * rows : (b + 1) * rows, :] = qs[b][...]
    masks = mask_of(start_ref, rows, slots, half)
    for h in range(width // HD):
        s = mm(kv_ref[:, col(h)], qw_ref[:, col(h)], NT) * SCALE
        for b in range(slots):
            st_ref[h, :, b * rows : (b + 1) * rows] = jnp.where(
                masks[b], s[:, b * rows : (b + 1) * rows], NEG
            )


def query_body(packed_ref, att_ref, p_ref, kw_ref, vw_ref, wq_ref, part_ref):
    rows, width = att_ref.shape
    grads = []
    for h in range(width // HD):
        go = packed_ref[:rows, col(h)]
        corr = jnp.sum(go.astype(F32) * att_ref[:, col(h)], axis=1, keepdims=True)
        gp = mm(go, vw_ref[:, col(h)], NT)
        gs = (SCALE * p_ref[h] * (gp - corr)).astype(BF16)
        grads.append(mm(gs, kw_ref[:, col(h)]).astype(BF16))
    part_ref[...] = mm(jnp.concatenate(grads, axis=1), wq_ref[...], NT)


def key_body(slots, first, *refs):
    got = refs[:slots]
    pt_in, kv_ref, qw_ref, wk_ref, wv_ref, partq_ref = refs[slots : slots + 6]
    if first:
        part_ref, send_ref, pt_ref, gow_ref = refs[slots + 6 :]
    else:
        part_ref, send_ref, gow_ref = refs[slots + 6 :]
        pt_ref = pt_in
    rows = kv_ref.shape[0]
    width = qw_ref.shape[1]
    for b in range(slots):
        gow_ref[b * rows : (b + 1) * rows, :] = got[b][:rows, :]
    gks, gvs = [], []
    for h in range(width // HD):
        corr = unpack_row(got, rows, h, 0)
        if first:
            pt = jnp.exp(pt_in[h] - unpack_row(got, rows, h, 1))
            pt_ref[h] = pt
        else:
            pt = pt_ref[h]
        go = gow_ref[:, col(h)]
        gp = mm(kv_ref[:, width + h * HD : width + (h + 1) * HD], go, NT)
        gs = (SCALE * pt * (gp - corr)).astype(BF16)
        gks.append(mm(gs, qw_ref[:, col(h)]).astype(BF16))
        gvs.append(mm(pt.astype(BF16), go).astype(BF16))
    part = partq_ref[...] + mm(jnp.concatenate(gks, axis=1), wk_ref[...], NT)
    part = part + mm(jnp.concatenate(gvs, axis=1), wv_ref[...], NT)
    part_ref[...] = part
    send_ref[...] = part.astype(BF16)


def combine_body(where_ref, part_ref, recv_ref, inv_ref, gain_ref, wo_ref, att_ref, *refs):
    kry_ref, packed_ref, vec_ref = refs
    rows, width = att_ref.shape
    cols = kry_ref.shape[1]
    inverse = inv_ref[:, :1]
    vec = inverse * (gain_ref[...] * (part_ref[...] + recv_ref[...].astype(F32)))
    vec_ref[...] = vec
    off = pl.multiple_of(where_ref[0], HD)
    kry_ref[...] = vec_ref[:, pl.ds(off, cols)]
    go = mm(vec.astype(BF16), wo_ref[...], NT).astype(BF16)
    packed_ref[:rows, :] = go
    corr = [
        jnp.sum(go[:, col(h)].astype(F32) * att_ref[:, col(h)], axis=1, keepdims=True)
        for h in range(width // HD)
    ]
    pack_rows(packed_ref, rows, width // HD, corr)


def gram_body(where_ref, part_ref, recv_ref, inv_ref, gain_ref, *refs):
    kry = refs[:SSTEP]
    last_ref, sums_ref, vec_ref = refs[SSTEP:]
    rows, cols = last_ref.shape
    inverse = inv_ref[:, :1]
    vec_ref[...] = inverse * (gain_ref[...] * (part_ref[...] + recv_ref[...].astype(F32)))
    off = pl.multiple_of(where_ref[0], HD)
    last_ref[...] = vec_ref[:, pl.ds(off, cols)]
    all_k = list(kry) + [last_ref]
    count = SSTEP * (SSTEP + 1) // 2 + SSTEP
    acc = [jnp.zeros((8, HD), F32) for _ in range(count)]
    for r in range(0, rows, 8):
        for c in range(0, cols, HD):
            ks = [k[r : r + 8, c : c + HD] for k in all_k]
            ds = [ks[i] - ks[i + 1] for i in range(SSTEP)]
            i = 0
            for a in range(SSTEP):
                for b in range(a + 1):
                    acc[i] = acc[i] + ds[a] * ds[b]
                    i += 1
            for a in range(SSTEP):
                acc[i] = acc[i] + ds[a] * ks[0]
                i += 1
    sub = lax.broadcasted_iota(jnp.int32, sums_ref.shape, 0)
    out = jnp.zeros(sums_ref.shape, F32)
    for i in range(count):
        out = jnp.where(sub == i, jnp.sum(acc[i], axis=0, keepdims=True), out)
    sums_ref[...] = out


def solve(gram, right):
    n = len(right)
    low = [[None] * n for _ in range(n)]
    for i in range(n):
        for j in range(i + 1):
            run = gram[i][j]
            for k in range(j):
                run = run - low[i][k] * low[j][k]
            low[i][j] = jnp.sqrt(run) if i == j else run / low[j][j]
    mid = []
    for i in range(n):
        run = right[i]
        for j in range(i):
            run = run - low[i][j] * mid[j]
        mid.append(run / low[i][i])
    out = [None] * n
    for i in range(n - 1, -1, -1):
        run = mid[i]
        for j in range(i + 1, n):
            run = run - low[j][i] * out[j]
        out[i] = run / low[i][i]
    return out


def finish_body(sums_ref, *refs):
    kry = refs[: SSTEP + 1]
    adj_ref, res_ref = refs[SSTEP + 1 :]
    total = jnp.sum(sums_ref[...], axis=0)
    vals = jnp.sum(total, axis=1, keepdims=True)
    idx = 0
    gram = [[None] * SSTEP for _ in range(SSTEP)]
    for a in range(SSTEP):
        for b in range(a + 1):
            gram[a][b] = vals[idx : idx + 1, :]
            idx += 1
    right = [vals[idx + a : idx + a + 1, :] for a in range(SSTEP)]
    coef = solve(gram, right)
    ks = [k[...] for k in kry]
    adj = coef[0] * ks[0]
    res = ks[0] - coef[0] * (ks[0] - ks[1])
    for i in range(1, SSTEP):
        adj = adj + coef[i] * ks[i]
        res = res - coef[i] * (ks[i] - ks[i + 1])
    adj_ref[...] = adj
    res_ref[...] = res


def swap_partner(c, d, odd):
    return c + d if (c // d) % 2 == odd else c - d


def on_device(state, cotangent, norm_gain, w_query, w_key, w_value, w_out):
    rows, cols = state.shape
    width = w_query.shape[1]
    heads = width // HD
    half = WIN // 2
    seq = lax.axis_size("seq")
    tps = lax.axis_size("tp")
    chips = seq // 2
    reach = (half + rows - 1) // rows
    chip_reach = (reach + 1) // 2
    me = lax.axis_index("seq")
    chip, core = me // 2, me % 2
    hops = [(d, odd) for d in range(1, chip_reach + 1) for odd in (1, 0)]
    ids = [chip]
    for d, odd in hops:
        ids.append(jnp.where((chip // d) % 2 == odd, chip + d, chip - d))
    starts = []
    for k in (core, 1 - core):
        for q in ids:
            starts.append(
                jnp.where((q >= 0) & (q < chips), (2 * q + k) * rows, -(1 << 24))
            )
    starts = jnp.stack(starts).astype(jnp.int32)
    slots = 2 * len(ids)
    nwin = slots * rows
    gain = norm_gain[None, :]
    where = (lax.axis_index("tp") * cols).astype(jnp.int32)[None]

    def swap_core(x):
        return lax.ppermute(x, "seq", [(i, i ^ 1) for i in range(seq)])

    def fetch(x):
        got = []
        for d, odd in hops:
            pairs = []
            for c in range(chips):
                q = swap_partner(c, d, odd)
                if 0 <= q < chips:
                    pairs += [(2 * c, 2 * q), (2 * c + 1, 2 * q + 1)]
            got.append(lax.ppermute(x, "seq", pairs))
        mine = [x] + got
        return mine + [swap_core(y) for y in mine]

    both = jnp.stack([state, cotangent.astype(BF16)])
    both = lax.all_gather(both, "tp", axis=0, tiled=False)
    q_own, kv_own, go0, inv = kernel_call(
        project_body,
        [
            sds(rows, width, dtype=BF16),
            sds(rows, 2 * width, dtype=BF16),
            sds(rows, width, dtype=BF16),
            sds(rows, HD),
        ],
        [both, gain, w_query, w_key, w_value, w_out],
    )
    kv_slots = fetch(kv_own)
    q_slots = fetch(q_own)
    probs, att, packed, k_win, v_win = kernel_call(
        functools.partial(stats_body, slots, half),
        [
            sds(heads, rows, nwin),
            sds(rows, width),
            sds(rows + PAD, width, dtype=BF16),
            sds(nwin, width, dtype=BF16),
            sds(nwin, width, dtype=BF16),
        ],
        [starts] + kv_slots + [q_own, go0],
        n_smem=1,
    )
    probs_t, q_win = kernel_call(
        functools.partial(scores_t_body, slots, half),
        [sds(heads, rows, nwin), sds(nwin, width, dtype=BF16)],
        [starts] + q_slots + [kv_own],
        n_smem=1,
    )
    krylov = [cotangent]
    for n in range(SSTEP):
        got = fetch(packed)
        (part_q,) = kernel_call(
            query_body,
            [sds(rows, tps * cols)],
            [packed, att, probs, k_win, v_win, w_query],
        )
        outs = [sds(rows, tps * cols), sds(rows, tps * cols, dtype=BF16)]
        if n == 0:
            outs.append(sds(heads, rows, nwin))
        res = kernel_call(
            functools.partial(key_body, slots, n == 0),
            outs,
            got + [probs_t, kv_own, q_win, w_key, w_value, part_q],
            scratch=[pltpu.VMEM((nwin, width), BF16)],
        )
        part, send = res[:2]
        if n == 0:
            probs_t = res[2]
        k = 1
        while True:
            recv = lax.ppermute(send, "tp", [(i, i ^ k) for i in range(tps)])
            k *= 2
            if k >= tps:
                break
            part = part + recv.astype(F32)
            send = part.astype(BF16)
        if n < SSTEP - 1:
            kry, packed = kernel_call(
                combine_body,
                [sds(rows, cols), sds(rows + PAD, width, dtype=BF16)],
                [where, part, recv, inv, gain, w_out, att],
                n_smem=1,
                scratch=[pltpu.VMEM((rows, tps * cols), F32)],
            )
            krylov.append(kry)
        else:
            last, sums = kernel_call(
                gram_body,
                [sds(rows, cols), sds(PAD, HD)],
                [where, part, recv, inv, gain] + krylov,
                n_smem=1,
                scratch=[pltpu.VMEM((rows, tps * cols), F32)],
            )
            krylov.append(last)
    ranks = seq * tps
    sums = lax.all_to_all(
        jnp.broadcast_to(sums[None], (ranks,) + sums.shape), ("seq", "tp"), 0, 0
    )
    adjoint, residual = kernel_call(
        finish_body,
        [sds(rows, cols), sds(rows, cols)],
        [sums] + krylov,
    )
    return (adjoint, residual)


def solution(mesh):
    in_specs = (
        P("seq", "tp"),
        P("seq", "tp"),
        P(),
        P(None, "tp"),
        P(None, "tp"),
        P(None, "tp"),
        P("tp", None),
    )
    out_specs = (P("seq", "tp"), P("seq", "tp"))
    return jax.shard_map(
        on_device, mesh=mesh, in_specs=in_specs, out_specs=out_specs, check_vma=False
    )
```

time: 533 us -> 198 us (0.37)
  starting transfers between devices: 238 us -> 63.6 us
  waiting for transfers between devices: 117 us -> 45.6 us
  blocking collectives: 71.3 us -> 28.7 us
  matrix products: 38.8 us -> 0 us
  between operations: 31.1 us -> 1.28 us
  Pallas kernels: 0 us -> 24.8 us
  other arithmetic: 15.5 us -> 1.9 us
  local copies, waits for them, and re-layouts: 17.7 us -> 31.2 us
    ppermute x80 -> x58, starting transfers between devices: 238 us -> 63.6 us  [the longest x24 50.8 us: fetch(): got.append(lax.ppermute(x, 'seq', pairs))]
    reduce_scatter x4 -> x0, waiting for transfers between devices: 82 us -> none  [on_device(): lax.psum_scatter(partial_sum, 'tp', scatter_dimension=1, tiled=True)]
    psum x1 -> x0, blocking collectives: 39.3 us -> none  [on_device(): gram_matrix, right_side = lax.psum((local_gram, local_right), ('seq', 'tp'))]
    dot_general x29 -> x0, matrix products: 38.8 us -> none  [the longest x4 9.07 us: on_device(): jnp.einsum('rhe,khe->hrk', grad_out, values_all, preferred_element_type=j...]
    pallas_call x0 -> x16, Pallas kernels: none -> 24.8 us  [kernel_call(): pl.pallas_call(body, out_shape=[jax.ShapeDtypeStruct(o.shape, o.dtype) fo...]
    unnamed x78 -> x90, local copies, waits for them, and re-layouts: 7.11 us -> 31.1 us
    all_gather x5 -> x1, blocking collectives: 32 us -> 9.94 us  [on_device(): both = lax.all_gather(both, 'tp', axis=0, tiled=False)]
    all_to_all x0 -> x1, blocking collectives: none -> 18.7 us  [on_device(): lax.all_to_all(jnp.broadcast_to(sums[None], (ranks,) + sums.shape), ('seq...]
  transfers between devices with their start and end apart: 84 -> 58, of which waited for: 22 -> 13; matrix products, arithmetic and copies ran while one was open for 2% -> 0% of each run, Pallas kernels for 0% -> 5%
where the time goes in v1:
time: 198 us; the launch traced here: 197 us
  starting transfers between devices  63.6 us (32%)
  waiting for transfers between devices  45.6 us (23%)
  local copies, waits for them, and re-layouts  31.2 us (16%)
  blocking collectives  28.7 us (14%)
  Pallas kernels  24.8 us (13%)
    ppermute x24, starting transfers between devices, fetch(): got.append(lax.ppermute(x, 'seq', pairs))  50.8 us
    unnamed x90, local copies, waits for them, and re-layouts  31.1 us
    ppermute x4, waiting for transfers between devices, on_device(): recv = lax.ppermute(send, 'tp', [(i, i ^ k) for i in range(tps)])  27.1 us
    pallas_call x16, Pallas kernels, kernel_call(): pl.pallas_call(body, out_shape=[jax.ShapeDtypeStruct(o.shape, o.dtype) fo...  24.8 us
    all_to_all x1, blocking collectives, on_device(): lax.all_to_all(jnp.broadcast_to(sums[None], (ranks,) + sums.shape), ('seq...  18.7 us
    ppermute x24, waiting for transfers between devices, fetch(): got.append(lax.ppermute(x, 'seq', pairs))  16.8 us
    all_gather x1, blocking collectives, on_device(): both = lax.all_gather(both, 'tp', axis=0, tiled=False)  9.94 us
    ppermute x30, starting transfers between devices, swap_core(): return lax.ppermute(x, 'seq', [(i, i ^ 1) for i in range(seq)])  6.56 us
  transfers between devices with their start and end apart: 58, of which 13 were waited for; matrix products, arithmetic and copies ran while one was open for 0% of the time, Pallas kernels for 5%

profile of v1, /device:TPU:0, one launch (start us, length us, event | category | flops | bytes accessed | tf_op | source)
XLA Modules:
  0.0 197.0 jit_solution(4884683831239859751)
XLA Ops:
  2.5 9.9 %all-gather = bf16[4,128,512]{2,1,0:T(8,128)(2,1)S(1)} all-gather(bf16[2,128,512]{2,1,0:T(8,128)(2,1)S(1)} %pad_maximum_fusion), channel_id=2, replica_groups=mesh['seq'=16,'tp'=2] {'tp'}, dimensions={0}, use_global_device_ids=true | all-gather | bytes 786432 | tf_op jit(solution)/shard_map/all_gather | solution.py:351
  19.7 1.8 collective-permute-start.21
  22.8 3.8 %collective-permute-start.3 = (bf16[128,1024]{1,0:T(8,128)(2,1)S(1)}, bf16[128,1024]{1,0:T(8,128)(2,1)S(1)}, u32[]{:S(2)}, u32[]{:S(2)}) collective-permute-start(bf16[128,1024]{1,0:T(8,128)(2,1)S(1)} %get-tuple-element.30.refs_0_.refs_10_.refs_11_), channel_id=1, source_target_pairs={{0,8},{2,10},{4,12},{6,14},{8,0},{10,2},{12,4},{14,6},{16,24},{18,... | collective-permute-start | bytes 786440 | tf_op jit(solution)/shard_map/ppermute | solution.py:346
  29.6 4.0 %collective-permute-start.19 = (bf16[128,512]{1,0:T(8,128)(2,1)S(1)}, bf16[128,512]{1,0:T(8,128)(2,1)}, u32[]{:S(2)}, u32[]{:S(2)}) collective-permute-start(bf16[128,512]{1,0:T(8,128)(2,1)S(1)} %get-tuple-element.31.refs_10_.refs_0_), channel_id=1, source_target_pairs={{0,4},{2,6},{4,0},{6,2},{8,12},{10,14},{12,8},{14,10},{16,20},{18,... | collective-permute-start | bytes 393224 | tf_op jit(solution)/shard_map/ppermute | solution.py:346
  33.6 7.6 %collective-permute-done.19.refs_2_ = bf16[128,512]{1,0:T(8,128)(2,1)} collective-permute-done((bf16[128,512]{1,0:T(8,128)(2,1)S(1)}, bf16[128,512]{1,0:T(8,128)(2,1)}, u32[]{:S(2)}, u32[]{:S(2)}) %collective-permute-start.19) | collective-permute-done | bytes 131104 | tf_op jit(solution)/shard_map/ppermute | solution.py:346
  60.6 3.1 %shard_map.87 = (f32[4,128,1280]{2,1,0:T(8,128)S(1)}, f32[128,512]{1,0:T(8,128)S(1)}, bf16[144,512]{1,0:T(8,128)(2,1)S(1)}, bf16[1280,512]{1,0:T(8,128)(2,1)S(1)}, bf16[1280,512]{1,0:T(8,128)(2,1)S(1)}) custom-call(s32[10]{0:T(128)S(1)} %stack.52.start_ref, bf16[128,1024]{1,0:T(8,128)(2,1)S(1)} %get-tuple-element.30.refs_0_.refs_10_.refs_11_, ...), custom_call_target="tpu_custom_call" | custom-call | flops 100000000 | bytes 8536104 | tf_op jit(solution)/shard_map/pallas_call | solution.py:36
  63.7 4.7 %collective-permute-start.12 = (bf16[144,512]{1,0:T(8,128)(2,1)S(1)}, bf16[144,512]{1,0:T(8,128)(2,1)S(1)}, u32[]{:S(2)}, u32[]{:S(2)}) collective-permute-start(bf16[144,512]{1,0:T(8,128)(2,1)S(1)} %get-tuple-element.33.packed_ref.refs_0_), channel_id=1, source_target_pairs={{0,8},{2,10},{4,12},{6,14},{8,0},{10,2},{12,4},{14,6},{16,24},{18,... | collective-permute-start | bytes 442376 | tf_op jit(solution)/shard_map/ppermute | solution.py:346
  69.1 1.8 collective-permute-start.10
  75.7 2.0 shard_map.88
  77.7 1.7 copy-done.1
  80.9 2.9 %shard_map.90 = (f32[128,1024]{1,0:T(8,128)S(1)}, bf16[128,1024]{1,0:T(8,128)(2,1)}, f32[4,128,1280]{2,1,0:T(8,128)S(1)}) custom-call(bf16[144,512]{1,0:T(8,128)(2,1)S(1)} %get-tuple-element.33.packed_ref.refs_0_, bf16[144,512]{1,0:T(8,128)(2,1)S(1)} %collective-permute-done.9.refs_1_, bf16[144,512]{1,0:T(8,128)(2,1)S(1)} %collective-permute-done.10.refs_2_, ...), custom_call_target="tpu_custom_call" | custom-call | flops 100000000 | bytes 11698176 | tf_op jit(solution)/shard_map/pallas_call | solution.py:36
  87.6 6.9 %collective-permute-done.27.recv_ref = bf16[128,1024]{1,0:T(8,128)(2,1)S(1)} collective-permute-done((bf16[128,1024]{1,0:T(8,128)(2,1)}, bf16[128,1024]{1,0:T(8,128)(2,1)S(1)}, u32[]{:S(2)}, u32[]{:S(2)}) %collective-permute-start.27) | collective-permute-done | bytes 262176 | tf_op jit(solution)/shard_map/ppermute | solution.py:404
  97.6 7.4 %collective-permute-start.31 = (bf16[144,512]{1,0:T(8,128)(2,1)S(1)}, bf16[144,512]{1,0:T(8,128)(2,1)S(1)}, u32[]{:S(2)}, u32[]{:S(2)}) collective-permute-start(bf16[144,512]{1,0:T(8,128)(2,1)S(1)} %get-tuple-element.43.packed_ref.refs_0_), channel_id=1, source_target_pairs={{0,8},{2,10},{4,12},{6,14},{8,0},{10,2},{12,4},{14,6},{16,24},{18,... | collective-permute-start | bytes 442376 | tf_op jit(solution)/shard_map/ppermute | solution.py:346
  108.7 2.2 %collective-permute-done.29.refs_2_ = bf16[144,512]{1,0:T(8,128)(2,1)S(1)} collective-permute-done((bf16[144,512]{1,0:T(8,128)(2,1)S(1)}, bf16[144,512]{1,0:T(8,128)(2,1)S(1)}, u32[]{:S(2)}, u32[]{:S(2)}) %collective-permute-start.29) | collective-permute-done | bytes 147488 | tf_op jit(solution)/shard_map/ppermute | solution.py:346
  115.6 2.1 %shard_map.93 = (f32[128,1024]{1,0:T(8,128)S(1)}, bf16[128,1024]{1,0:T(8,128)(2,1)S(1)}) custom-call(bf16[144,512]{1,0:T(8,128)(2,1)S(1)} %get-tuple-element.43.packed_ref.refs_0_, bf16[144,512]{1,0:T(8,128)(2,1)S(1)} %collective-permute-done.28.refs_1_, bf16[144,512]{1,0:T(8,128)(2,1)S(1)} %collective-permute-done.29.refs_2_, ...), custom_call_target="tpu_custom_call" | custom-call | flops 100000000 | bytes 9076736 | tf_op jit(solution)/shard_map/pallas_call | solution.py:36
  119.3 6.7 %collective-permute-done.37.recv_ref = bf16[128,1024]{1,0:T(8,128)(2,1)S(1)} collective-permute-done((bf16[128,1024]{1,0:T(8,128)(2,1)S(1)}, bf16[128,1024]{1,0:T(8,128)(2,1)S(1)}, u32[]{:S(2)}, u32[]{:S(2)}) %collective-permute-start.37) | collective-permute-done | bytes 262176 | tf_op jit(solution)/shard_map/ppermute | solution.py:404
  126.8 6.0 %collective-permute-start.41 = (bf16[144,512]{1,0:T(8,128)(2,1)S(1)}, bf16[144,512]{1,0:T(8,128)(2,1)S(1)}, u32[]{:S(2)}, u32[]{:S(2)}) collective-permute-start(bf16[144,512]{1,0:T(8,128)(2,1)S(1)} %get-tuple-element.47.packed_ref.refs_0_), channel_id=1, source_target_pairs={{0,8},{2,10},{4,12},{6,14},{8,0},{10,2},{12,4},{14,6},{16,24},{18,... | collective-permute-start | bytes 442376 | tf_op jit(solution)/shard_map/ppermute | solution.py:346
  140.6 2.1 %shard_map.96 = (f32[128,1024]{1,0:T(8,128)S(1)}, bf16[128,1024]{1,0:T(8,128)(2,1)S(1)}) custom-call(bf16[144,512]{1,0:T(8,128)(2,1)S(1)} %get-tuple-element.47.packed_ref.refs_0_, bf16[144,512]{1,0:T(8,128)(2,1)S(1)} %collective-permute-done.38.refs_1_, bf16[144,512]{1,0:T(8,128)(2,1)S(1)} %collective-permute-done.39.refs_2_, ...), custom_call_target="tpu_custom_call" | custom-call | flops 100000000 | bytes 9076736 | tf_op jit(solution)/shard_map/pallas_call | solution.py:36
  144.3 6.7 %collective-permute-done.47.recv_ref = bf16[128,1024]{1,0:T(8,128)(2,1)S(1)} collective-permute-done((bf16[128,1024]{1,0:T(8,128)(2,1)S(1)}, bf16[128,1024]{1,0:T(8,128)(2,1)S(1)}, u32[]{:S(2)}, u32[]{:S(2)}) %collective-permute-start.47) | collective-permute-done | bytes 262176 | tf_op jit(solution)/shard_map/ppermute | solution.py:404
  151.8 6.5 %collective-permute-start.51 = (bf16[144,512]{1,0:T(8,128)(2,1)S(1)}, bf16[144,512]{1,0:T(8,128)(2,1)S(1)}, u32[]{:S(2)}, u32[]{:S(2)}) collective-permute-start(bf16[144,512]{1,0:T(8,128)(2,1)S(1)} %get-tuple-element.50.packed_ref.refs_0_), channel_id=1, source_target_pairs={{0,8},{2,10},{4,12},{6,14},{8,0},{10,2},{12,4},{14,6},{16,24},{18,... | collective-permute-start | bytes 442376 | tf_op jit(solution)/shard_map/ppermute | solution.py:346
  162.5 1.7 collective-permute-done.49.refs_2_
  166.1 2.1 %shard_map.99 = (f32[128,1024]{1,0:T(8,128)S(1)}, bf16[128,1024]{1,0:T(8,128)(2,1)S(1)}) custom-call(bf16[144,512]{1,0:T(8,128)(2,1)S(1)} %get-tuple-element.50.packed_ref.refs_0_, bf16[144,512]{1,0:T(8,128)(2,1)S(1)} %collective-permute-done.48.refs_1_, bf16[144,512]{1,0:T(8,128)(2,1)S(1)} %collective-permute-done.49.refs_2_, ...), custom_call_target="tpu_custom_call" | custom-call | flops 100000000 | bytes 9076736 | tf_op jit(solution)/shard_map/pallas_call | solution.py:36
  169.8 6.7 %collective-permute-done.57.recv_ref = bf16[128,1024]{1,0:T(8,128)(2,1)S(1)} collective-permute-done((bf16[128,1024]{1,0:T(8,128)(2,1)S(1)}, bf16[128,1024]{1,0:T(8,128)(2,1)S(1)}, u32[]{:S(2)}, u32[]{:S(2)}) %collective-permute-start.57) | collective-permute-done | bytes 262176 | tf_op jit(solution)/shard_map/ppermute | solution.py:404
  177.0 18.7 %all_to_all.5.sums_ref = f32[32,16,128]{2,1,0:T(8,128)S(1)} all-to-all(f32[32,16,128]{2,1,0:T(8,128)S(1)} %broadcast_in_dim.14), channel_id=1, replica_groups=mesh['seq'=16,'tp'=2] {'seq','tp'}, dimensions={0} | all-to-all | bytes 524288 | tf_op jit(solution)/shard_map/all_to_all | solution.py:429
  (204 shorter events, 76.3 us)
Async XLA Ops:
  19.7 9.2 %collective-permute-start.21 = (bf16[128,512]{1,0:T(8,128)(2,1)S(1)}, bf16[128,512]{1,0:T(8,128)(2,1)S(1)}, u32[]{:S(2)}, u32[]{:S(2)}) collective-permute-start(bf16[128,512]{1,0:T(8,128)(2,1)S(1)} %get-tuple-element.31.refs_10_.refs_0_), channel_id=1, source_target_pairs={{0,8},{2,10},{4,12},{6,14},{8,0},{10,2},{12,4},{14,6},{16,24},{18,... | collective-permute-start | bytes 393224 | tf_op jit(solution)/shard_map/ppermute | solution.py:346
  21.5 8.1 %collective-permute-start.20 = (bf16[128,512]{1,0:T(8,128)(2,1)S(1)}, bf16[128,512]{1,0:T(8,128)(2,1)}, u32[]{:S(2)}, u32[]{:S(2)}) collective-permute-start(bf16[128,512]{1,0:T(8,128)(2,1)S(1)} %get-tuple-element.31.refs_10_.refs_0_), channel_id=1, source_target_pairs={{8,16},{10,18},{12,20},{14,22},{16,8},{18,10},{20,12},{22,14},{9,1... | collective-permute-start | bytes 393224 | tf_op jit(solution)/shard_map/ppermute | solution.py:346
  22.8 18.4 %collective-permute-start.3 = (bf16[128,1024]{1,0:T(8,128)(2,1)S(1)}, bf16[128,1024]{1,0:T(8,128)(2,1)S(1)}, u32[]{:S(2)}, u32[]{:S(2)}) collective-permute-start(bf16[128,1024]{1,0:T(8,128)(2,1)S(1)} %get-tuple-element.30.refs_0_.refs_10_.refs_11_), channel_id=1, source_target_pairs={{0,8},{2,10},{4,12},{6,14},{8,0},{10,2},{12,4},{14,6},{16,24},{18,... | collective-permute-start | bytes 786440 | tf_op jit(solution)/shard_map/ppermute | solution.py:346
  26.7 15.8 %collective-permute-start.2 = (bf16[128,1024]{1,0:T(8,128)(2,1)S(1)}, bf16[128,1024]{1,0:T(8,128)(2,1)S(1)}, u32[]{:S(2)}, u32[]{:S(2)}) collective-permute-start(bf16[128,1024]{1,0:T(8,128)(2,1)S(1)} %get-tuple-element.30.refs_0_.refs_10_.refs_11_), channel_id=1, source_target_pairs={{8,16},{10,18},{12,20},{14,22},{16,8},{18,10},{20,12},{22,14},{9,1... | collective-permute-start | bytes 786440 | tf_op jit(solution)/shard_map/ppermute | solution.py:346
  27.3 15.9 %collective-permute-start.1 = (bf16[128,1024]{1,0:T(8,128)(2,1)S(1)}, bf16[128,1024]{1,0:T(8,128)(2,1)S(1)}, u32[]{:S(2)}, u32[]{:S(2)}) collective-permute-start(bf16[128,1024]{1,0:T(8,128)(2,1)S(1)} %get-tuple-element.30.refs_0_.refs_10_.refs_11_), channel_id=1, source_target_pairs={{0,4},{2,6},{4,0},{6,2},{8,12},{10,14},{12,8},{14,10},{16,20},{18,... | collective-permute-start | bytes 786440 | tf_op jit(solution)/shard_map/ppermute | solution.py:346
  28.9 15.5 %collective-permute-start = (bf16[128,1024]{1,0:T(8,128)(2,1)S(1)}, bf16[128,1024]{1,0:T(8,128)(2,1)S(1)}, u32[]{:S(2)}, u32[]{:S(2)}) collective-permute-start(bf16[128,1024]{1,0:T(8,128)(2,1)S(1)} %get-tuple-element.30.refs_0_.refs_10_.refs_11_), channel_id=1, source_target_pairs={{4,8},{6,10},{8,4},{10,6},{12,16},{14,18},{16,12},{18,14},{20,24},... | collective-permute-start | bytes 786440 | tf_op jit(solution)/shard_map/ppermute | solution.py:346
  29.6 11.6 %collective-permute-start.19 = (bf16[128,512]{1,0:T(8,128)(2,1)S(1)}, bf16[128,512]{1,0:T(8,128)(2,1)}, u32[]{:S(2)}, u32[]{:S(2)}) collective-permute-start(bf16[128,512]{1,0:T(8,128)(2,1)S(1)} %get-tuple-element.31.refs_10_.refs_0_), channel_id=1, source_target_pairs={{0,4},{2,6},{4,0},{6,2},{8,12},{10,14},{12,8},{14,10},{16,20},{18,... | collective-permute-start | bytes 393224 | tf_op jit(solution)/shard_map/ppermute | solution.py:346
  45.8 17.8 %collective-permute-start.22 = (bf16[128,512]{1,0:T(8,128)(2,1)S(1)}, bf16[128,512]{1,0:T(8,128)(2,1)}, u32[]{:S(2)}, u32[]{:S(2)}) collective-permute-start(bf16[128,512]{1,0:T(8,128)(2,1)S(1)} %get-tuple-element.31.refs_10_.refs_0_), channel_id=1, source_target_pairs={{0,2},{2,0},{4,6},{6,4},{8,10},{10,8},{12,14},{14,12},{16,18},{18,... | collective-permute-start | bytes 393224 | tf_op jit(solution)/shard_map/ppermute | solution.py:336
  47.1 21.4 %collective-permute-start.18 = (bf16[128,512]{1,0:T(8,128)(2,1)S(1)}, bf16[128,512]{1,0:T(8,128)(2,1)}, u32[]{:S(2)}, u32[]{:S(2)}) collective-permute-start(bf16[128,512]{1,0:T(8,128)(2,1)S(1)} %get-tuple-element.31.refs_10_.refs_0_), channel_id=1, source_target_pairs={{4,8},{6,10},{8,4},{10,6},{12,16},{14,18},{16,12},{18,14},{20,24},... | collective-permute-start | bytes 393224 | tf_op jit(solution)/shard_map/ppermute | solution.py:346
  49.1 20.0 %collective-permute-start.26 = (bf16[128,512]{1,0:T(8,128)(2,1)S(1)}, bf16[128,512]{1,0:T(8,128)(2,1)}, u32[]{:S(2)}, u32[]{:S(2)}) collective-permute-start(bf16[128,512]{1,0:T(8,128)(2,1)S(1)} %collective-permute-done.21.refs_4_), channel_id=1, source_target_pairs={{0,2},{2,0},{4,6},{6,4},{8,10},{10,8},{12,14},{14,12},{16,18},{18,... | collective-permute-start | bytes 393224 | tf_op jit(solution)/shard_map/ppermute | solution.py:336
  49.8 21.1 %collective-permute-start.25 = (bf16[128,512]{1,0:T(8,128)(2,1)}, bf16[128,512]{1,0:T(8,128)(2,1)}, u32[]{:S(2)}, u32[]{:S(2)}) collective-permute-start(bf16[128,512]{1,0:T(8,128)(2,1)} %collective-permute-done.20.refs_3_), channel_id=1, source_target_pairs={{0,2},{2,0},{4,6},{6,4},{8,10},{10,8},{12,14},{14,12},{16,18},{18,... | collective-permute-start | bytes 393224 | tf_op jit(solution)/shard_map/ppermute | solution.py:336
  51.0 20.6 %collective-permute-start.24 = (bf16[128,512]{1,0:T(8,128)(2,1)}, bf16[128,512]{1,0:T(8,128)(2,1)}, u32[]{:S(2)}, u32[]{:S(2)}) collective-permute-start(bf16[128,512]{1,0:T(8,128)(2,1)} %collective-permute-done.19.refs_2_), channel_id=1, source_target_pairs={{0,2},{2,0},{4,6},{6,4},{8,10},{10,8},{12,14},{14,12},{16,18},{18,... | collective-permute-start | bytes 393224 | tf_op jit(solution)/shard_map/ppermute | solution.py:336
  63.7 9.7 %collective-permute-start.12 = (bf16[144,512]{1,0:T(8,128)(2,1)S(1)}, bf16[144,512]{1,0:T(8,128)(2,1)S(1)}, u32[]{:S(2)}, u32[]{:S(2)}) collective-permute-start(bf16[144,512]{1,0:T(8,128)(2,1)S(1)} %get-tuple-element.33.packed_ref.refs_0_), channel_id=1, source_target_pairs={{0,8},{2,10},{4,12},{6,14},{8,0},{10,2},{12,4},{14,6},{16,24},{18,... | collective-permute-start | bytes 442376 | tf_op jit(solution)/shard_map/ppermute | solution.py:346
  73.2 7.6 %collective-permute-start.13 = (bf16[144,512]{1,0:T(8,128)(2,1)S(1)}, bf16[144,512]{1,0:T(8,128)(2,1)S(1)}, u32[]{:S(2)}, u32[]{:S(2)}) collective-permute-start(bf16[144,512]{1,0:T(8,128)(2,1)S(1)} %get-tuple-element.33.packed_ref.refs_0_), channel_id=1, source_target_pairs={{0,2},{2,0},{4,6},{6,4},{8,10},{10,8},{12,14},{14,12},{16,18},{18,... | collective-permute-start | bytes 442376 | tf_op jit(solution)/shard_map/ppermute | solution.py:336
  73.4 7.4 %collective-permute-start.17 = (bf16[144,512]{1,0:T(8,128)(2,1)S(1)}, bf16[144,512]{1,0:T(8,128)(2,1)S(1)}, u32[]{:S(2)}, u32[]{:S(2)}) collective-permute-start(bf16[144,512]{1,0:T(8,128)(2,1)S(1)} %collective-permute-done.12.refs_4_), channel_id=1, source_target_pairs={{0,2},{2,0},{4,6},{6,4},{8,10},{10,8},{12,14},{14,12},{16,18},{18,... | collective-permute-start | bytes 442376 | tf_op jit(solution)/shard_map/ppermute | solution.py:336
  86.1 8.4 %collective-permute-start.27 = (bf16[128,1024]{1,0:T(8,128)(2,1)}, bf16[128,1024]{1,0:T(8,128)(2,1)S(1)}, u32[]{:S(2)}, u32[]{:S(2)}) collective-permute-start(bf16[128,1024]{1,0:T(8,128)(2,1)} %get-tuple-element.41), channel_id=1, source_target_pairs={{0,1},{1,0},{2,3},{3,2},{4,5},{5,4},{6,7},{7,6},{8,9},{9,8},{10,11... | collective-permute-start | bytes 786440 | tf_op jit(solution)/shard_map/ppermute | solution.py:404
  97.6 10.6 %collective-permute-start.31 = (bf16[144,512]{1,0:T(8,128)(2,1)S(1)}, bf16[144,512]{1,0:T(8,128)(2,1)S(1)}, u32[]{:S(2)}, u32[]{:S(2)}) collective-permute-start(bf16[144,512]{1,0:T(8,128)(2,1)S(1)} %get-tuple-element.43.packed_ref.refs_0_), channel_id=1, source_target_pairs={{0,8},{2,10},{4,12},{6,14},{8,0},{10,2},{12,4},{14,6},{16,24},{18,... | collective-permute-start | bytes 442376 | tf_op jit(solution)/shard_map/ppermute | solution.py:346
  108.0 7.5 %collective-permute-start.32 = (bf16[144,512]{1,0:T(8,128)(2,1)S(1)}, bf16[144,512]{1,0:T(8,128)(2,1)S(1)}, u32[]{:S(2)}, u32[]{:S(2)}) collective-permute-start(bf16[144,512]{1,0:T(8,128)(2,1)S(1)} %get-tuple-element.43.packed_ref.refs_0_), channel_id=1, source_target_pairs={{0,2},{2,0},{4,6},{6,4},{8,10},{10,8},{12,14},{14,12},{16,18},{18,... | collective-permute-start | bytes 442376 | tf_op jit(solution)/shard_map/ppermute | solution.py:336
  108.2 7.3 %collective-permute-start.36 = (bf16[144,512]{1,0:T(8,128)(2,1)S(1)}, bf16[144,512]{1,0:T(8,128)(2,1)S(1)}, u32[]{:S(2)}, u32[]{:S(2)}) collective-permute-start(bf16[144,512]{1,0:T(8,128)(2,1)S(1)} %collective-permute-done.31.refs_4_), channel_id=1, source_target_pairs={{0,2},{2,0},{4,6},{6,4},{8,10},{10,8},{12,14},{14,12},{16,18},{18,... | collective-permute-start | bytes 442376 | tf_op jit(solution)/shard_map/ppermute | solution.py:336
  117.7 8.3 %collective-permute-start.37 = (bf16[128,1024]{1,0:T(8,128)(2,1)S(1)}, bf16[128,1024]{1,0:T(8,128)(2,1)S(1)}, u32[]{:S(2)}, u32[]{:S(2)}) collective-permute-start(bf16[128,1024]{1,0:T(8,128)(2,1)S(1)} %get-tuple-element.46), channel_id=1, source_target_pairs={{0,1},{1,0},{2,3},{3,2},{4,5},{5,4},{6,7},{7,6},{8,9},{9,8},{10,11... | collective-permute-start | bytes 786440 | tf_op jit(solution)/shard_map/ppermute | solution.py:404
  126.8 9.7 %collective-permute-start.41 = (bf16[144,512]{1,0:T(8,128)(2,1)S(1)}, bf16[144,512]{1,0:T(8,128)(2,1)S(1)}, u32[]{:S(2)}, u32[]{:S(2)}) collective-permute-start(bf16[144,512]{1,0:T(8,128)(2,1)S(1)} %get-tuple-element.47.packed_ref.refs_0_), channel_id=1, source_target_pairs={{0,8},{2,10},{4,12},{6,14},{8,0},{10,2},{12,4},{14,6},{16,24},{18,... | collective-permute-start | bytes 442376 | tf_op jit(solution)/shard_map/ppermute | solution.py:346
  142.8 8.3 %collective-permute-start.47 = (bf16[128,1024]{1,0:T(8,128)(2,1)S(1)}, bf16[128,1024]{1,0:T(8,128)(2,1)S(1)}, u32[]{:S(2)}, u32[]{:S(2)}) collective-permute-start(bf16[128,1024]{1,0:T(8,128)(2,1)S(1)} %get-tuple-element.49), channel_id=1, source_target_pairs={{0,1},{1,0},{2,3},{3,2},{4,5},{5,4},{6,7},{7,6},{8,9},{9,8},{10,11... | collective-permute-start | bytes 786440 | tf_op jit(solution)/shard_map/ppermute | solution.py:404
  151.8 10.2 %collective-permute-start.51 = (bf16[144,512]{1,0:T(8,128)(2,1)S(1)}, bf16[144,512]{1,0:T(8,128)(2,1)S(1)}, u32[]{:S(2)}, u32[]{:S(2)}) collective-permute-start(bf16[144,512]{1,0:T(8,128)(2,1)S(1)} %get-tuple-element.50.packed_ref.refs_0_), channel_id=1, source_target_pairs={{0,8},{2,10},{4,12},{6,14},{8,0},{10,2},{12,4},{14,6},{16,24},{18,... | collective-permute-start | bytes 442376 | tf_op jit(solution)/shard_map/ppermute | solution.py:346
  168.3 8.3 %collective-permute-start.57 = (bf16[128,1024]{1,0:T(8,128)(2,1)S(1)}, bf16[128,1024]{1,0:T(8,128)(2,1)S(1)}, u32[]{:S(2)}, u32[]{:S(2)}) collective-permute-start(bf16[128,1024]{1,0:T(8,128)(2,1)S(1)} %get-tuple-element.52), channel_id=1, source_target_pairs={{0,1},{1,0},{2,3},{3,2},{4,5},{5,4},{6,7},{7,6},{8,9},{9,8},{10,11... | collective-permute-start | bytes 786440 | tf_op jit(solution)/shard_map/ppermute | solution.py:404
  (79 other events, 347.8 us)

commit v2 on v1

v2 whole, which is shorter than its diff:
```python
import functools
import math

import jax
import jax.numpy as jnp
from jax import lax
from jax.experimental import pallas as pl
from jax.experimental.pallas import tpu as pltpu
from jax.sharding import PartitionSpec as P

HD = 128
WIN = 1024
SSTEP = 4
EPSILON = 1e-05
PAD = 16
NEG = -1e30
SCALE = 1.0 / math.sqrt(HD)
NT = (((1,), (1,)), ((), ()))
NN = (((1,), (0,)), ((), ()))
F32 = jnp.float32
BF16 = jnp.bfloat16


def mm(a, b, dims=NN):
    return lax.dot_general(a, b, dims, preferred_element_type=F32)


def col(h):
    return slice(h * HD, (h + 1) * HD)


def kernel_call(body, outs, ins, scratch=(), flops=10**8, limit=12 << 20):
    in_specs = [pl.BlockSpec(memory_space=pltpu.VMEM)] * len(ins)
    moved = sum(math.prod(a.shape) * a.dtype.itemsize for a in list(ins) + list(outs))
    return pl.pallas_call(
        body,
        out_shape=[jax.ShapeDtypeStruct(o.shape, o.dtype) for o in outs],
        in_specs=in_specs,
        out_specs=[pl.BlockSpec(memory_space=pltpu.VMEM)] * len(outs),
        scratch_shapes=list(scratch),
        compiler_params=pltpu.CompilerParams(vmem_limit_bytes=limit),
        cost_estimate=pl.CostEstimate(flops=flops, bytes_accessed=moved, transcendentals=0),
    )(*ins)


def sds(*shape, dtype=F32):
    return jax.ShapeDtypeStruct(shape, dtype)


def parts_of(x):
    hi = x.astype(BF16).astype(F32)
    rest = x - hi
    mid = rest.astype(BF16).astype(F32)
    low = (rest - mid).astype(BF16).astype(F32)
    return [hi, mid, low]


def pack_rows(out_ref, rows, heads, columns):
    lane = lax.broadcasted_iota(jnp.int32, (rows, HD), 1)
    mat = jnp.zeros((rows, HD), F32)
    for i, c in enumerate(columns):
        mat = jnp.where(lane == i, c, mat)
    pieces = parts_of(mat.T)
    sub = lax.broadcasted_iota(jnp.int32, (PAD, rows), 0)
    for h in range(heads):
        tile = jnp.zeros((PAD, rows), F32)
        for kind in range(len(columns) // heads):
            r = kind * heads + h
            for i, piece in enumerate(pieces):
                tile = jnp.where(sub == 3 * kind + i, piece[r : r + 1, :], tile)
        out_ref[rows : rows + PAD, col(h)] = tile.astype(BF16)


def unpack_row(slots, rows, h, kind):
    pieces = []
    for s in slots:
        t = s[rows : rows + PAD, col(h)].astype(F32)
        k = 3 * kind
        pieces.append(t[k : k + 1] + t[k + 1 : k + 2] + t[k + 2 : k + 3])
    return jnp.concatenate(pieces, axis=1)


def slot_starts(half, rows):
    me, seq = lax.axis_index("seq"), lax.axis_size("seq")
    chip, core = me // 2, me % 2
    ids = [chip]
    for d, odd in hops_of(half, rows):
        ids.append(jnp.where((chip // d) % 2 == odd, chip + d, chip - d))
    out = []
    for k in (core, 1 - core):
        for q in ids:
            inside = (q >= 0) & (q < seq // 2)
            out.append(jnp.where(inside, (2 * q + k) * rows, -(1 << 24)))
    return out


def hops_of(half, rows):
    reach = (half + rows - 1) // rows
    return [(d, odd) for d in range(1, (reach + 1) // 2 + 1) for odd in (1, 0)]


def masks_of(half, rows):
    starts = slot_starts(half, rows)
    sub = lax.broadcasted_iota(jnp.int32, (rows, rows), 0)
    lane = lax.broadcasted_iota(jnp.int32, (rows, rows), 1)
    return [jnp.abs(lane - sub + (st - starts[0])) <= half for st in starts]


def masked(s, masks):
    rows = s.shape[0]
    pieces = [
        jnp.where(m, s[:, b * rows : (b + 1) * rows], NEG) for b, m in enumerate(masks)
    ]
    return jnp.concatenate(pieces, axis=1)


def feature_slices(tps, cols):
    me = lax.axis_index("tp")
    return [pl.ds(pl.multiple_of(((me + k) % tps) * cols, HD), cols) for k in range(tps)]


def round_body(x_ref, o_ref):
    o_ref[...] = x_ref[...].astype(o_ref.dtype)


def norm_body(tps, *refs):
    xs = refs[:tps]
    gain_ref, normed_ref, inv_ref = refs[tps:]
    rows, cols = xs[0].shape
    vals = [x[...].astype(F32) for x in xs]
    total = jnp.zeros((rows, 1), F32)
    for x in vals:
        total = total + jnp.sum(x * x, axis=1, keepdims=True)
    inverse = lax.rsqrt(total / (tps * cols) + EPSILON)
    inv_ref[...] = jnp.broadcast_to(inverse, inv_ref.shape)
    for x, at in zip(vals, feature_slices(tps, cols)):
        normed_ref[:, at] = (x * inverse * gain_ref[:, at]).astype(BF16)


def kv_body(blocks, *refs):
    xs = refs[:blocks]
    wk_ref, wv_ref, kv_ref = refs[blocks:]
    rows = xs[0].shape[0]
    width = wk_ref.shape[1]
    x = jnp.concatenate([r[...] for r in xs], axis=0)
    kv_ref[:, :width] = mm(x, wk_ref[...]).astype(BF16)
    kv_ref[:, width:] = mm(x, wv_ref[...]).astype(BF16)


def q_body(blocks, tps, *refs):
    xs = refs[:blocks]
    cots = refs[blocks : blocks + tps]
    wq_ref, wo_ref, q_ref, go_ref, cot_ref = refs[blocks + tps :]
    x = jnp.concatenate([r[...] for r in xs], axis=0)
    q_ref[...] = mm(x, wq_ref[...]).astype(BF16)
    for c, at in zip(cots, feature_slices(tps, cots[0].shape[1])):
        cot_ref[:, at] = c[...]
    go_ref[...] = mm(cot_ref[...], wo_ref[...], NT).astype(BF16)


def stats_body(half, kvm_ref, kvo_ref, q_ref, go_ref, p_ref, att_ref, packed_ref):
    rows, width = go_ref.shape
    heads = width // HD
    near = kvm_ref.shape[0]
    masks = masks_of(half, rows)
    packed_ref[:rows, :] = go_ref[...]
    lse, corr = [], []
    for h in range(heads):
        q = q_ref[:rows, col(h)]
        s = jnp.concatenate(
            [mm(q, kvm_ref[:, col(h)], NT), mm(q, kvo_ref[:, col(h)], NT)], axis=1
        )
        s = masked(s * SCALE, masks)
        peak = jnp.max(s, axis=1, keepdims=True)
        raw = jnp.exp(s - peak)
        total = jnp.sum(raw, axis=1, keepdims=True)
        probs = raw / total
        p_ref[h] = probs
        low = probs.astype(BF16)
        att = mm(low[:, :near], kvm_ref[:, col(heads + h)])
        att = att + mm(low[:, near:], kvo_ref[:, col(heads + h)])
        att_ref[:, col(h)] = att
        lse.append(peak + jnp.log(total))
        corr.append(jnp.sum(go_ref[:, col(h)].astype(F32) * att, axis=1, keepdims=True))
    pack_rows(packed_ref, rows, heads, corr + lse)


def scores_t_body(half, qm_ref, qo_ref, kv_ref, st_ref):
    rows = st_ref.shape[1]
    masks = masks_of(half, rows)
    for h in range(st_ref.shape[0]):
        k = kv_ref[:rows, col(h)]
        s = jnp.concatenate(
            [mm(k, qm_ref[:, col(h)], NT), mm(k, qo_ref[:, col(h)], NT)], axis=1
        )
        st_ref[h] = masked(s * SCALE, masks)


def query_body(packed_ref, att_ref, p_ref, kvm_ref, kvo_ref, wq_ref, part_ref):
    rows, width = att_ref.shape
    heads = width // HD
    near = kvm_ref.shape[0]
    grads = []
    for h in range(heads):
        go = packed_ref[:rows, col(h)]
        corr = jnp.sum(go.astype(F32) * att_ref[:, col(h)], axis=1, keepdims=True)
        v = col(heads + h)
        gp = jnp.concatenate([mm(go, kvm_ref[:, v], NT), mm(go, kvo_ref[:, v], NT)], axis=1)
        gs = (SCALE * p_ref[h] * (gp - corr)).astype(BF16)
        gq = mm(gs[:, :near], kvm_ref[:, col(h)]) + mm(gs[:, near:], kvo_ref[:, col(h)])
        grads.append(gq.astype(BF16))
    part_ref[...] = mm(jnp.concatenate(grads, axis=1), wq_ref[...], NT)


def key_body(slots, first, *refs):
    got = refs[:slots]
    pt_in, kv_ref, qm_ref, qo_ref, wk_ref, wv_ref, partq_ref = refs[slots : slots + 7]
    if first:
        part_ref, send_ref, pt_ref, gow_ref = refs[slots + 7 :]
    else:
        part_ref, send_ref, gow_ref = refs[slots + 7 :]
        pt_ref = pt_in
    rows, width = got[0].shape[0] - PAD, got[0].shape[1]
    heads = width // HD
    near = qm_ref.shape[0]
    for b in range(slots):
        gow_ref[b * rows : (b + 1) * rows, :] = got[b][:rows, :]
    gks, gvs = [], []
    for h in range(heads):
        corr = unpack_row(got, rows, h, 0)
        if first:
            pt = jnp.exp(pt_in[h] - unpack_row(got, rows, h, 1))
            pt_ref[h] = pt
        else:
            pt = pt_ref[h]
        go = gow_ref[:, col(h)]
        gp = mm(kv_ref[:rows, col(heads + h)], go, NT)
        gs = (SCALE * pt * (gp - corr)).astype(BF16)
        gk = mm(gs[:, :near], qm_ref[:, col(h)]) + mm(gs[:, near:], qo_ref[:, col(h)])
        gks.append(gk.astype(BF16))
        gvs.append(mm(pt.astype(BF16), go).astype(BF16))
    part = partq_ref[...] + mm(jnp.concatenate(gks, axis=1), wk_ref[...], NT)
    part = part + mm(jnp.concatenate(gvs, axis=1), wv_ref[...], NT)
    part_ref[...] = part
    send_ref[...] = part.astype(BF16)


def combine_body(part_ref, recv_ref, inv_ref, gain_ref, wo_ref, att_ref, *refs):
    kry_ref, packed_ref, vec_ref = refs
    rows, width = att_ref.shape
    cols = kry_ref.shape[1]
    inverse = inv_ref[:, :1]
    vec = inverse * (gain_ref[...] * (part_ref[...] + recv_ref[...].astype(F32)))
    vec_ref[...] = vec
    off = pl.multiple_of(lax.axis_index("tp") * cols, HD)
    kry_ref[...] = vec_ref[:, pl.ds(off, cols)]
    go = mm(vec.astype(BF16), wo_ref[...], NT).astype(BF16)
    packed_ref[:rows, :] = go
    corr = [
        jnp.sum(go[:, col(h)].astype(F32) * att_ref[:, col(h)], axis=1, keepdims=True)
        for h in range(width // HD)
    ]
    pack_rows(packed_ref, rows, width // HD, corr)


def gram_body(part_ref, recv_ref, inv_ref, gain_ref, *refs):
    kry = refs[:SSTEP]
    last_ref, sums_ref, vec_ref = refs[SSTEP:]
    rows, cols = last_ref.shape
    inverse = inv_ref[:, :1]
    vec_ref[...] = inverse * (gain_ref[...] * (part_ref[...] + recv_ref[...].astype(F32)))
    off = pl.multiple_of(lax.axis_index("tp") * cols, HD)
    last_ref[...] = vec_ref[:, pl.ds(off, cols)]
    all_k = list(kry) + [last_ref]
    count = SSTEP * (SSTEP + 1) // 2 + SSTEP
    acc = [jnp.zeros((8, HD), F32) for _ in range(count)]
    for r in range(0, rows, 8):
        for c in range(0, cols, HD):
            ks = [k[r : r + 8, c : c + HD] for k in all_k]
            ds = [ks[i] - ks[i + 1] for i in range(SSTEP)]
            i = 0
            for a in range(SSTEP):
                for b in range(a + 1):
                    acc[i] = acc[i] + ds[a] * ds[b]
                    i += 1
            for a in range(SSTEP):
                acc[i] = acc[i] + ds[a] * ks[0]
                i += 1
    sub = lax.broadcasted_iota(jnp.int32, (PAD, HD), 0)
    out = jnp.zeros((PAD, HD), F32)
    for i in range(count):
        out = jnp.where(sub == i, jnp.sum(acc[i], axis=0, keepdims=True), out)
    for r in range(sums_ref.shape[0]):
        sums_ref[r] = out


def solve(gram, right):
    n = len(right)
    low = [[None] * n for _ in range(n)]
    for i in range(n):
        for j in range(i + 1):
            run = gram[i][j]
            for k in range(j):
                run = run - low[i][k] * low[j][k]
            low[i][j] = jnp.sqrt(run) if i == j else run / low[j][j]
    mid = []
    for i in range(n):
        run = right[i]
        for j in range(i):
            run = run - low[i][j] * mid[j]
        mid.append(run / low[i][i])
    out = [None] * n
    for i in range(n - 1, -1, -1):
        run = mid[i]
        for j in range(i + 1, n):
            run = run - low[j][i] * out[j]
        out[i] = run / low[i][i]
    return out


def finish_body(sums_ref, *refs):
    kry = refs[: SSTEP + 1]
    adj_ref, res_ref = refs[SSTEP + 1 :]
    total = jnp.sum(sums_ref[...], axis=0)
    vals = jnp.sum(total, axis=1, keepdims=True)
    idx = 0
    gram = [[None] * SSTEP for _ in range(SSTEP)]
    for a in range(SSTEP):
        for b in range(a + 1):
            gram[a][b] = vals[idx : idx + 1, :]
            idx += 1
    right = [vals[idx + a : idx + a + 1, :] for a in range(SSTEP)]
    coef = solve(gram, right)
    ks = [k[...] for k in kry]
    adj = coef[0] * ks[0]
    res = ks[0] - coef[0] * (ks[0] - ks[1])
    for i in range(1, SSTEP):
        adj = adj + coef[i] * ks[i]
        res = res - coef[i] * (ks[i] - ks[i + 1])
    adj_ref[...] = adj
    res_ref[...] = res


def swap_partner(c, d, odd):
    return c + d if (c // d) % 2 == odd else c - d


def on_device(state, cotangent, norm_gain, w_query, w_key, w_value, w_out):
    rows, cols = state.shape
    width = w_query.shape[1]
    heads = width // HD
    half = WIN // 2
    seq = lax.axis_size("seq")
    tps = lax.axis_size("tp")
    chips = seq // 2
    hops = hops_of(half, rows)
    blocks = 1 + len(hops)
    slots = 2 * blocks
    nwin = slots * rows
    gain = norm_gain[None, :]

    def swap_core(x):
        return lax.ppermute(x, "seq", [(i, i ^ 1) for i in range(seq)])

    def tp_blocks(x):
        return [x] + [
            lax.ppermute(x, "tp", [((i + k) % tps, i) for i in range(tps)]) for k in range(1, tps)
        ]

    def fetch(x):
        got = [x]
        for d, odd in hops:
            pairs = []
            for c in range(chips):
                q = swap_partner(c, d, odd)
                if 0 <= q < chips:
                    pairs += [(2 * c, 2 * q), (2 * c + 1, 2 * q + 1)]
            got.append(lax.ppermute(x, "seq", pairs))
        return got

    states = tp_blocks(state)
    (cot_low,) = kernel_call(round_body, [sds(rows, cols, dtype=BF16)], [cotangent])
    cots = tp_blocks(cot_low)
    normed, inv = kernel_call(
        functools.partial(norm_body, tps),
        [sds(rows, tps * cols, dtype=BF16), sds(rows, HD)],
        states + [gain],
    )
    near = fetch(normed)
    (kv_mine,) = kernel_call(
        functools.partial(kv_body, blocks),
        [sds(blocks * rows, 2 * width, dtype=BF16)],
        near + [w_key, w_value],
    )
    kv_other = swap_core(kv_mine)
    q_mine, go0 = kernel_call(
        functools.partial(q_body, blocks, tps),
        [sds(blocks * rows, width, dtype=BF16), sds(rows, width, dtype=BF16)],
        near + cots + [w_query, w_out],
        scratch=[pltpu.VMEM((rows, tps * cols), BF16)],
    )
    q_other = swap_core(q_mine)
    probs, att, packed = kernel_call(
        functools.partial(stats_body, half),
        [
            sds(heads, rows, nwin),
            sds(rows, width),
            sds(rows + PAD, width, dtype=BF16),
        ],
        [kv_mine, kv_other, q_mine, go0],
    )
    (probs_t,) = kernel_call(
        functools.partial(scores_t_body, half),
        [sds(heads, rows, nwin)],
        [q_mine, q_other, kv_mine],
    )
    krylov = [cotangent]
    ranks = seq * tps
    for n in range(SSTEP):
        got = fetch(packed)
        got = got + [swap_core(x) for x in got]
        (part_q,) = kernel_call(
            query_body,
            [sds(rows, tps * cols)],
            [packed, att, probs, kv_mine, kv_other, w_query],
        )
        outs = [sds(rows, tps * cols), sds(rows, tps * cols, dtype=BF16)]
        if n == 0:
            outs.append(sds(heads, rows, nwin))
        res = kernel_call(
            functools.partial(key_body, slots, n == 0),
            outs,
            got + [probs_t, kv_mine, q_mine, q_other, w_key, w_value, part_q],
            scratch=[pltpu.VMEM((nwin, width), BF16)],
        )
        part, send = res[:2]
        if n == 0:
            probs_t = res[2]
        k = 1
        while True:
            recv = lax.ppermute(send, "tp", [(i, i ^ k) for i in range(tps)])
            k *= 2
            if k >= tps:
                break
            part = part + recv.astype(F32)
            send = part.astype(BF16)
        if n < SSTEP - 1:
            kry, packed = kernel_call(
                combine_body,
                [sds(rows, cols), sds(rows + PAD, width, dtype=BF16)],
                [part, recv, inv, gain, w_out, att],
                scratch=[pltpu.VMEM((rows, tps * cols), F32)],
            )
            krylov.append(kry)
        else:
            last, sums = kernel_call(
                gram_body,
                [sds(rows, cols), sds(ranks, PAD, HD)],
                [part, recv, inv, gain] + krylov,
                scratch=[pltpu.VMEM((rows, tps * cols), F32)],
            )
            krylov.append(last)
    sums = lax.all_to_all(sums, ("seq", "tp"), 0, 0)
    adjoint, residual = kernel_call(
        finish_body,
        [sds(rows, cols), sds(rows, cols)],
        [sums] + krylov,
    )
    return (adjoint, residual)


def solution(mesh):
    in_specs = (
        P("seq", "tp"),
        P("seq", "tp"),
        P(),
        P(None, "tp"),
        P(None, "tp"),
        P(None, "tp"),
        P("tp", None),
    )
    out_specs = (P("seq", "tp"), P("seq", "tp"))
    return jax.shard_map(
        on_device, mesh=mesh, in_specs=in_specs, out_specs=out_specs, check_vma=False
    )
```

time: 198 us -> 160 us (0.81)
  local copies, waits for them, and re-layouts: 31.2 us -> 4.07 us
  blocking collectives: 28.7 us -> 19 us
  waiting for transfers between devices: 45.6 us -> 50.1 us
  starting transfers between devices: 63.6 us -> 59.4 us
    unnamed x90 -> x20, local copies, waits for them, and re-layouts: 31.1 us -> 4.07 us
    all_gather x1 -> x0, blocking collectives: 9.94 us -> none  [on_device(): both = lax.all_gather(both, 'tp', axis=0, tiled=False)]
    ppermute x0 -> x2, waiting for transfers between devices: none -> 8.1 us  [tp_blocks(): lax.ppermute(x, 'tp', [((i + k) % tps, i) for i in range(tps)])]
    ppermute x24 -> x20, starting transfers between devices: 50.8 us -> 44 us  [fetch(): got.append(lax.ppermute(x, 'seq', pairs))]
    ppermute x0 -> x2, starting transfers between devices: none -> 4.59 us  [tp_blocks(): lax.ppermute(x, 'tp', [((i + k) % tps, i) for i in range(tps)])]
    ppermute x30 -> x22, starting transfers between devices: 6.56 us -> 4.51 us  [swap_core(): return lax.ppermute(x, 'seq', [(i, i ^ 1) for i in range(seq)])]
    ppermute x24 -> x20, waiting for transfers between devices: 16.8 us -> 15.1 us  [fetch(): got.append(lax.ppermute(x, 'seq', pairs))]
    pallas_call x16 -> x19, Pallas kernels: 24.8 us -> 25.7 us  [kernel_call(): pl.pallas_call(body, out_shape=[jax.ShapeDtypeStruct(o.shape, o.dtype) fo...]
  transfers between devices with their start and end apart: 58 -> 48, of which waited for: 13 -> 16; matrix products, arithmetic and copies ran while one was open for 0% -> 0% of each run, Pallas kernels for 5% -> 7%
where the time goes in v2:
time: 160 us; the launch traced here: 159 us
  starting transfers between devices  59.4 us (37%)
  waiting for transfers between devices  50.1 us (31%)
  Pallas kernels  25.7 us (16%)
  blocking collectives  19 us (12%)
  local copies, waits for them, and re-layouts  4.07 us (3%)
    ppermute x20, starting transfers between devices, fetch(): got.append(lax.ppermute(x, 'seq', pairs))  44 us
    ppermute x4, waiting for transfers between devices, on_device(): recv = lax.ppermute(send, 'tp', [(i, i ^ k) for i in range(tps)])  26.9 us
    pallas_call x19, Pallas kernels, kernel_call(): pl.pallas_call(body, out_shape=[jax.ShapeDtypeStruct(o.shape, o.dtype) fo...  25.7 us
    all_to_all x1, blocking collectives, on_device(): sums = lax.all_to_all(sums, ('seq', 'tp'), 0, 0)  19 us
    ppermute x20, waiting for transfers between devices, fetch(): got.append(lax.ppermute(x, 'seq', pairs))  15.1 us
    ppermute x2, waiting for transfers between devices, tp_blocks(): lax.ppermute(x, 'tp', [((i + k) % tps, i) for i in range(tps)])  8.1 us
    ppermute x4, starting transfers between devices, on_device(): recv = lax.ppermute(send, 'tp', [(i, i ^ k) for i in range(tps)])  6.23 us
    ppermute x2, starting transfers between devices, tp_blocks(): lax.ppermute(x, 'tp', [((i + k) % tps, i) for i in range(tps)])  4.59 us
  transfers between devices with their start and end apart: 48, of which 16 were waited for; matrix products, arithmetic and copies ran while one was open for 0% of the time, Pallas kernels for 7%

profile of v2, /device:TPU:0, one launch (start us, length us, event | category | flops | bytes accessed | tf_op | source)
XLA Modules:
  0.0 159.4 jit_solution(14617356949632657591)
XLA Ops:
  0.6 3.0 %collective-permute-start = (bf16[128,512]{1,0:T(8,128)(2,1)}, bf16[128,512]{1,0:T(8,128)(2,1)S(1)}, u32[]{:S(2)}, u32[]{:S(2)}) collective-permute-start(bf16[128,512]{1,0:T(8,128)(2,1)} %refs_0_.3), channel_id=1, source_target_pairs={{1,0},{0,1},{3,2},{2,3},{5,4},{4,5},{7,6},{6,7},{9,8},{8,9},{11,10... | collective-permute-start | bytes 393224 | tf_op jit(solution)/shard_map/ppermute | solution.py:367
  3.7 3.7 %collective-permute-done.refs_1_ = bf16[128,512]{1,0:T(8,128)(2,1)S(1)} collective-permute-done((bf16[128,512]{1,0:T(8,128)(2,1)}, bf16[128,512]{1,0:T(8,128)(2,1)S(1)}, u32[]{:S(2)}, u32[]{:S(2)}) %collective-permute-start) | collective-permute-done | bytes 131104 | tf_op jit(solution)/shard_map/ppermute | solution.py:367
  9.1 1.9 %collective-permute-start.4 = (bf16[128,1024]{1,0:T(8,128)(2,1)S(1)}, bf16[128,1024]{1,0:T(8,128)(2,1)S(1)}, u32[]{:S(2)}, u32[]{:S(2)}) collective-permute-start(bf16[128,1024]{1,0:T(8,128)(2,1)S(1)} %get-tuple-element.26.refs_0_), channel_id=1, source_target_pairs={{0,8},{2,10},{4,12},{6,14},{8,0},{10,2},{12,4},{14,6},{16,24},{18,... | collective-permute-start | bytes 786440 | tf_op jit(solution)/shard_map/ppermute | solution.py:378
  14.0 2.7 %collective-permute-done.4.refs_4_ = bf16[128,1024]{1,0:T(8,128)(2,1)S(1)} collective-permute-done((bf16[128,1024]{1,0:T(8,128)(2,1)S(1)}, bf16[128,1024]{1,0:T(8,128)(2,1)S(1)}, u32[]{:S(2)}, u32[]{:S(2)}) %collective-permute-start.4) | collective-permute-done | bytes 262176 | tf_op jit(solution)/shard_map/ppermute | solution.py:378
  16.7 2.0 %collective-permute-done.2.refs_2_ = bf16[128,1024]{1,0:T(8,128)(2,1)S(1)} collective-permute-done((bf16[128,1024]{1,0:T(8,128)(2,1)S(1)}, bf16[128,1024]{1,0:T(8,128)(2,1)S(1)}, u32[]{:S(2)}, u32[]{:S(2)}) %collective-permute-start.2) | collective-permute-done | bytes 262176 | tf_op jit(solution)/shard_map/ppermute | solution.py:378
  24.3 4.4 %collective-permute-done.6.refs_6_ = bf16[128,512]{1,0:T(8,128)(2,1)S(1)} collective-permute-done((bf16[128,512]{1,0:T(8,128)(2,1)S(1)}, bf16[128,512]{1,0:T(8,128)(2,1)S(1)}, u32[]{:S(2)}, u32[]{:S(2)}) %collective-permute-start.6) | collective-permute-done | bytes 131104 | tf_op jit(solution)/shard_map/ppermute | solution.py:367
  30.0 2.6 %shard_map.90 = (f32[4,128,1280]{2,1,0:T(8,128)S(1)}, f32[128,512]{1,0:T(8,128)S(1)}, bf16[144,512]{1,0:T(8,128)(2,1)S(1)}) custom-call(bf16[640,1024]{1,0:T(8,128)(2,1)S(1)} %shard_map.87.kvm_ref.kv_ref.refs_11_, bf16[640,1024]{1,0:T(8,128)(2,1)S(1)} %collective-permute-done.5.kvo_ref, bf16[640,512]{1,0:T(8,128)(2,1)S(1)} %get-tuple-element.27.q_ref.qm_ref.refs_12_, ...), custom_call_target="tpu_custom_call" | custom-call | flops 100000000 | bytes 6438912 | tf_op jit(solution)/shard_map/pallas_call | solution.py:35
  32.6 9.8 %collective-permute-start.10 = (bf16[144,512]{1,0:T(8,128)(2,1)S(1)}, bf16[144,512]{1,0:T(8,128)(2,1)S(1)}, u32[]{:S(2)}, u32[]{:S(2)}) collective-permute-start(bf16[144,512]{1,0:T(8,128)(2,1)S(1)} %get-tuple-element.29.packed_ref.refs_0_), channel_id=1, source_target_pairs={{0,8},{2,10},{4,12},{6,14},{8,0},{10,2},{12,4},{14,6},{16,24},{18,... | collective-permute-start | bytes 442376 | tf_op jit(solution)/shard_map/ppermute | solution.py:378
  47.4 1.7 %collective-permute-done.8.refs_2_ = bf16[144,512]{1,0:T(8,128)(2,1)S(1)} collective-permute-done((bf16[144,512]{1,0:T(8,128)(2,1)S(1)}, bf16[144,512]{1,0:T(8,128)(2,1)S(1)}, u32[]{:S(2)}, u32[]{:S(2)}) %collective-permute-start.8) | collective-permute-done | bytes 147488 | tf_op jit(solution)/shard_map/ppermute | solution.py:378
  52.0 2.3 %shard_map.93 = (f32[128,1024]{1,0:T(8,128)S(1)}, bf16[128,1024]{1,0:T(8,128)(2,1)S(1)}, f32[4,128,1280]{2,1,0:T(8,128)S(1)}) custom-call(bf16[144,512]{1,0:T(8,128)(2,1)S(1)} %get-tuple-element.29.packed_ref.refs_0_, bf16[144,512]{1,0:T(8,128)(2,1)S(1)} %collective-permute-done.7.refs_1_, bf16[144,512]{1,0:T(8,128)(2,1)S(1)} %collective-permute-done.8.refs_2_, ...), custom_call_target="tpu_custom_call" | custom-call | flops 100000000 | bytes 12746752 | tf_op jit(solution)/shard_map/pallas_call | solution.py:35
  55.9 6.7 %collective-permute-done.17.recv_ref = bf16[128,1024]{1,0:T(8,128)(2,1)S(1)} collective-permute-done((bf16[128,1024]{1,0:T(8,128)(2,1)S(1)}, bf16[128,1024]{1,0:T(8,128)(2,1)S(1)}, u32[]{:S(2)}, u32[]{:S(2)}) %collective-permute-start.17) | collective-permute-done | bytes 262176 | tf_op jit(solution)/shard_map/ppermute | solution.py:441
  63.4 5.6 %collective-permute-start.21 = (bf16[144,512]{1,0:T(8,128)(2,1)S(1)}, bf16[144,512]{1,0:T(8,128)(2,1)S(1)}, u32[]{:S(2)}, u32[]{:S(2)}) collective-permute-start(bf16[144,512]{1,0:T(8,128)(2,1)S(1)} %get-tuple-element.35.packed_ref.refs_0_), channel_id=1, source_target_pairs={{0,8},{2,10},{4,12},{6,14},{8,0},{10,2},{12,4},{14,6},{16,24},{18,... | collective-permute-start | bytes 442376 | tf_op jit(solution)/shard_map/ppermute | solution.py:378
  73.2 1.7 %collective-permute-done.19.refs_2_ = bf16[144,512]{1,0:T(8,128)(2,1)S(1)} collective-permute-done((bf16[144,512]{1,0:T(8,128)(2,1)S(1)}, bf16[144,512]{1,0:T(8,128)(2,1)S(1)}, u32[]{:S(2)}, u32[]{:S(2)}) %collective-permute-start.19) | collective-permute-done | bytes 147488 | tf_op jit(solution)/shard_map/ppermute | solution.py:378
  77.1 2.3 %shard_map.96 = (f32[128,1024]{1,0:T(8,128)S(1)}, bf16[128,1024]{1,0:T(8,128)(2,1)S(1)}) custom-call(bf16[144,512]{1,0:T(8,128)(2,1)S(1)} %get-tuple-element.35.packed_ref.refs_0_, bf16[144,512]{1,0:T(8,128)(2,1)S(1)} %collective-permute-done.18.refs_1_, bf16[144,512]{1,0:T(8,128)(2,1)S(1)} %collective-permute-done.19.refs_2_, ...), custom_call_target="tpu_custom_call" | custom-call | flops 100000000 | bytes 10125312 | tf_op jit(solution)/shard_map/pallas_call | solution.py:35
  80.9 6.7 %collective-permute-done.27.recv_ref = bf16[128,1024]{1,0:T(8,128)(2,1)S(1)} collective-permute-done((bf16[128,1024]{1,0:T(8,128)(2,1)S(1)}, bf16[128,1024]{1,0:T(8,128)(2,1)S(1)}, u32[]{:S(2)}, u32[]{:S(2)}) %collective-permute-start.27) | collective-permute-done | bytes 262176 | tf_op jit(solution)/shard_map/ppermute | solution.py:441
  88.4 6.5 %collective-permute-start.31 = (bf16[144,512]{1,0:T(8,128)(2,1)S(1)}, bf16[144,512]{1,0:T(8,128)(2,1)S(1)}, u32[]{:S(2)}, u32[]{:S(2)}) collective-permute-start(bf16[144,512]{1,0:T(8,128)(2,1)S(1)} %get-tuple-element.39.packed_ref.refs_0_), channel_id=1, source_target_pairs={{0,8},{2,10},{4,12},{6,14},{8,0},{10,2},{12,4},{14,6},{16,24},{18,... | collective-permute-start | bytes 442376 | tf_op jit(solution)/shard_map/ppermute | solution.py:378
  99.1 1.7 %collective-permute-done.29.refs_2_ = bf16[144,512]{1,0:T(8,128)(2,1)S(1)} collective-permute-done((bf16[144,512]{1,0:T(8,128)(2,1)S(1)}, bf16[144,512]{1,0:T(8,128)(2,1)S(1)}, u32[]{:S(2)}, u32[]{:S(2)}) %collective-permute-start.29) | collective-permute-done | bytes 147488 | tf_op jit(solution)/shard_map/ppermute | solution.py:378
  103.0 2.3 %shard_map.99 = (f32[128,1024]{1,0:T(8,128)S(1)}, bf16[128,1024]{1,0:T(8,128)(2,1)S(1)}) custom-call(bf16[144,512]{1,0:T(8,128)(2,1)S(1)} %get-tuple-element.39.packed_ref.refs_0_, bf16[144,512]{1,0:T(8,128)(2,1)S(1)} %collective-permute-done.28.refs_1_, bf16[144,512]{1,0:T(8,128)(2,1)S(1)} %collective-permute-done.29.refs_2_, ...), custom_call_target="tpu_custom_call" | custom-call | flops 100000000 | bytes 10125312 | tf_op jit(solution)/shard_map/pallas_call | solution.py:35
  106.8 6.7 %collective-permute-done.37.recv_ref = bf16[128,1024]{1,0:T(8,128)(2,1)S(1)} collective-permute-done((bf16[128,1024]{1,0:T(8,128)(2,1)S(1)}, bf16[128,1024]{1,0:T(8,128)(2,1)S(1)}, u32[]{:S(2)}, u32[]{:S(2)}) %collective-permute-start.37) | collective-permute-done | bytes 262176 | tf_op jit(solution)/shard_map/ppermute | solution.py:441
  114.2 5.8 %collective-permute-start.41 = (bf16[144,512]{1,0:T(8,128)(2,1)S(1)}, bf16[144,512]{1,0:T(8,128)(2,1)S(1)}, u32[]{:S(2)}, u32[]{:S(2)}) collective-permute-start(bf16[144,512]{1,0:T(8,128)(2,1)S(1)} %get-tuple-element.42.packed_ref.refs_0_), channel_id=1, source_target_pairs={{0,8},{2,10},{4,12},{6,14},{8,0},{10,2},{12,4},{14,6},{16,24},{18,... | collective-permute-start | bytes 442376 | tf_op jit(solution)/shard_map/ppermute | solution.py:378
  124.2 1.7 %collective-permute-done.39.refs_2_ = bf16[144,512]{1,0:T(8,128)(2,1)S(1)} collective-permute-done((bf16[144,512]{1,0:T(8,128)(2,1)S(1)}, bf16[144,512]{1,0:T(8,128)(2,1)S(1)}, u32[]{:S(2)}, u32[]{:S(2)}) %collective-permute-start.39) | collective-permute-done | bytes 147488 | tf_op jit(solution)/shard_map/ppermute | solution.py:378
  128.1 2.3 %shard_map.102 = (f32[128,1024]{1,0:T(8,128)S(1)}, bf16[128,1024]{1,0:T(8,128)(2,1)S(1)}) custom-call(bf16[144,512]{1,0:T(8,128)(2,1)S(1)} %get-tuple-element.42.packed_ref.refs_0_, bf16[144,512]{1,0:T(8,128)(2,1)S(1)} %collective-permute-done.38.refs_1_, bf16[144,512]{1,0:T(8,128)(2,1)S(1)} %collective-permute-done.39.refs_2_, ...), custom_call_target="tpu_custom_call" | custom-call | flops 100000000 | bytes 10125312 | tf_op jit(solution)/shard_map/pallas_call | solution.py:35
  131.9 6.7 %collective-permute-done.47.recv_ref = bf16[128,1024]{1,0:T(8,128)(2,1)S(1)} collective-permute-done((bf16[128,1024]{1,0:T(8,128)(2,1)S(1)}, bf16[128,1024]{1,0:T(8,128)(2,1)S(1)}, u32[]{:S(2)}, u32[]{:S(2)}) %collective-permute-start.47) | collective-permute-done | bytes 262176 | tf_op jit(solution)/shard_map/ppermute | solution.py:441
  139.1 19.0 %all_to_all.5.sums_ref = f32[32,16,128]{2,1,0:T(8,128)S(1)} all-to-all(f32[32,16,128]{2,1,0:T(8,128)S(1)} %get-tuple-element.48), channel_id=1, replica_groups=mesh['seq'=16,'tp'=2] {'seq','tp'}, dimensions={0} | all-to-all | bytes 524288 | tf_op jit(solution)/shard_map/all_to_all | solution.py:463
  (112 shorter events, 48.5 us)
Async XLA Ops:
  0.6 6.7 %collective-permute-start = (bf16[128,512]{1,0:T(8,128)(2,1)}, bf16[128,512]{1,0:T(8,128)(2,1)S(1)}, u32[]{:S(2)}, u32[]{:S(2)}) collective-permute-start(bf16[128,512]{1,0:T(8,128)(2,1)} %refs_0_.3), channel_id=1, source_target_pairs={{1,0},{0,1},{3,2},{2,3},{5,4},{4,5},{7,6},{6,7},{9,8},{8,9},{11,10... | collective-permute-start | bytes 393224 | tf_op jit(solution)/shard_map/ppermute | solution.py:367
  9.1 7.5 %collective-permute-start.4 = (bf16[128,1024]{1,0:T(8,128)(2,1)S(1)}, bf16[128,1024]{1,0:T(8,128)(2,1)S(1)}, u32[]{:S(2)}, u32[]{:S(2)}) collective-permute-start(bf16[128,1024]{1,0:T(8,128)(2,1)S(1)} %get-tuple-element.26.refs_0_), channel_id=1, source_target_pairs={{0,8},{2,10},{4,12},{6,14},{8,0},{10,2},{12,4},{14,6},{16,24},{18,... | collective-permute-start | bytes 786440 | tf_op jit(solution)/shard_map/ppermute | solution.py:378
  11.0 5.6 %collective-permute-start.3 = (bf16[128,1024]{1,0:T(8,128)(2,1)S(1)}, bf16[128,1024]{1,0:T(8,128)(2,1)S(1)}, u32[]{:S(2)}, u32[]{:S(2)}) collective-permute-start(bf16[128,1024]{1,0:T(8,128)(2,1)S(1)} %get-tuple-element.26.refs_0_), channel_id=1, source_target_pairs={{8,16},{10,18},{12,20},{14,22},{16,8},{18,10},{20,12},{22,14},{9,1... | collective-permute-start | bytes 786440 | tf_op jit(solution)/shard_map/ppermute | solution.py:378
  11.7 7.0 %collective-permute-start.2 = (bf16[128,1024]{1,0:T(8,128)(2,1)S(1)}, bf16[128,1024]{1,0:T(8,128)(2,1)S(1)}, u32[]{:S(2)}, u32[]{:S(2)}) collective-permute-start(bf16[128,1024]{1,0:T(8,128)(2,1)S(1)} %get-tuple-element.26.refs_0_), channel_id=1, source_target_pairs={{0,4},{2,6},{4,0},{6,2},{8,12},{10,14},{12,8},{14,10},{16,20},{18,... | collective-permute-start | bytes 786440 | tf_op jit(solution)/shard_map/ppermute | solution.py:378
  13.3 5.4 %collective-permute-start.1 = (bf16[128,1024]{1,0:T(8,128)(2,1)S(1)}, bf16[128,1024]{1,0:T(8,128)(2,1)S(1)}, u32[]{:S(2)}, u32[]{:S(2)}) collective-permute-start(bf16[128,1024]{1,0:T(8,128)(2,1)S(1)} %get-tuple-element.26.refs_0_), channel_id=1, source_target_pairs={{4,8},{6,10},{8,4},{10,6},{12,16},{14,18},{16,12},{18,14},{20,24},... | collective-permute-start | bytes 786440 | tf_op jit(solution)/shard_map/ppermute | solution.py:378
  22.7 7.3 %collective-permute-start.5 = (bf16[640,1024]{1,0:T(8,128)(2,1)S(1)}, bf16[640,1024]{1,0:T(8,128)(2,1)S(1)}, u32[]{:S(2)}, u32[]{:S(2)}) collective-permute-start(bf16[640,1024]{1,0:T(8,128)(2,1)S(1)} %shard_map.87.kvm_ref.kv_ref.refs_11_), channel_id=1, source_target_pairs={{0,2},{2,0},{4,6},{6,4},{8,10},{10,8},{12,14},{14,12},{16,18},{18,... | collective-permute-start | bytes 3932168 | tf_op jit(solution)/shard_map/ppermute | solution.py:363
  22.8 6.0 %collective-permute-start.6 = (bf16[128,512]{1,0:T(8,128)(2,1)S(1)}, bf16[128,512]{1,0:T(8,128)(2,1)S(1)}, u32[]{:S(2)}, u32[]{:S(2)}) collective-permute-start(bf16[128,512]{1,0:T(8,128)(2,1)S(1)} %shard_map.88.refs_5_), channel_id=1, source_target_pairs={{1,0},{0,1},{3,2},{2,3},{5,4},{4,5},{7,6},{6,7},{9,8},{8,9},{11,10... | collective-permute-start | bytes 393224 | tf_op jit(solution)/shard_map/ppermute | solution.py:367
  29.9 15.4 %collective-permute-start.16 = (bf16[640,512]{1,0:T(8,128)(2,1)S(1)}, bf16[640,512]{1,0:T(8,128)(2,1)S(1)}, u32[]{:S(2)}, u32[]{:S(2)}) collective-permute-start(bf16[640,512]{1,0:T(8,128)(2,1)S(1)} %get-tuple-element.27.q_ref.qm_ref.refs_12_), channel_id=1, source_target_pairs={{0,2},{2,0},{4,6},{6,4},{8,10},{10,8},{12,14},{14,12},{16,18},{18,... | collective-permute-start | bytes 1966088 | tf_op jit(solution)/shard_map/ppermute | solution.py:363
  32.6 14.3 %collective-permute-start.10 = (bf16[144,512]{1,0:T(8,128)(2,1)S(1)}, bf16[144,512]{1,0:T(8,128)(2,1)S(1)}, u32[]{:S(2)}, u32[]{:S(2)}) collective-permute-start(bf16[144,512]{1,0:T(8,128)(2,1)S(1)} %get-tuple-element.29.packed_ref.refs_0_), channel_id=1, source_target_pairs={{0,8},{2,10},{4,12},{6,14},{8,0},{10,2},{12,4},{14,6},{16,24},{18,... | collective-permute-start | bytes 442376 | tf_op jit(solution)/shard_map/ppermute | solution.py:378
  43.0 6.0 %collective-permute-start.8 = (bf16[144,512]{1,0:T(8,128)(2,1)S(1)}, bf16[144,512]{1,0:T(8,128)(2,1)S(1)}, u32[]{:S(2)}, u32[]{:S(2)}) collective-permute-start(bf16[144,512]{1,0:T(8,128)(2,1)S(1)} %get-tuple-element.29.packed_ref.refs_0_), channel_id=1, source_target_pairs={{0,4},{2,6},{4,0},{6,2},{8,12},{10,14},{12,8},{14,10},{16,20},{18,... | collective-permute-start | bytes 442376 | tf_op jit(solution)/shard_map/ppermute | solution.py:378
  45.3 6.7 %collective-permute-start.11 = (bf16[144,512]{1,0:T(8,128)(2,1)S(1)}, bf16[144,512]{1,0:T(8,128)(2,1)S(1)}, u32[]{:S(2)}, u32[]{:S(2)}) collective-permute-start(bf16[144,512]{1,0:T(8,128)(2,1)S(1)} %get-tuple-element.29.packed_ref.refs_0_), channel_id=1, source_target_pairs={{0,2},{2,0},{4,6},{6,4},{8,10},{10,8},{12,14},{14,12},{16,18},{18,... | collective-permute-start | bytes 442376 | tf_op jit(solution)/shard_map/ppermute | solution.py:363
  46.9 5.1 %collective-permute-start.15 = (bf16[144,512]{1,0:T(8,128)(2,1)S(1)}, bf16[144,512]{1,0:T(8,128)(2,1)S(1)}, u32[]{:S(2)}, u32[]{:S(2)}) collective-permute-start(bf16[144,512]{1,0:T(8,128)(2,1)S(1)} %collective-permute-done.10.refs_4_), channel_id=1, source_target_pairs={{0,2},{2,0},{4,6},{6,4},{8,10},{10,8},{12,14},{14,12},{16,18},{18,... | collective-permute-start | bytes 442376 | tf_op jit(solution)/shard_map/ppermute | solution.py:363
  46.9 5.1 %collective-permute-start.14 = (bf16[144,512]{1,0:T(8,128)(2,1)S(1)}, bf16[144,512]{1,0:T(8,128)(2,1)S(1)}, u32[]{:S(2)}, u32[]{:S(2)}) collective-permute-start(bf16[144,512]{1,0:T(8,128)(2,1)S(1)} %collective-permute-done.9.refs_3_), channel_id=1, source_target_pairs={{0,2},{2,0},{4,6},{6,4},{8,10},{10,8},{12,14},{14,12},{16,18},{18,... | collective-permute-start | bytes 442376 | tf_op jit(solution)/shard_map/ppermute | solution.py:363
  54.4 8.3 %collective-permute-start.17 = (bf16[128,1024]{1,0:T(8,128)(2,1)S(1)}, bf16[128,1024]{1,0:T(8,128)(2,1)S(1)}, u32[]{:S(2)}, u32[]{:S(2)}) collective-permute-start(bf16[128,1024]{1,0:T(8,128)(2,1)S(1)} %get-tuple-element.33), channel_id=1, source_target_pairs={{0,1},{1,0},{2,3},{3,2},{4,5},{5,4},{6,7},{7,6},{8,9},{9,8},{10,11... | collective-permute-start | bytes 786440 | tf_op jit(solution)/shard_map/ppermute | solution.py:441
  63.4 9.3 %collective-permute-start.21 = (bf16[144,512]{1,0:T(8,128)(2,1)S(1)}, bf16[144,512]{1,0:T(8,128)(2,1)S(1)}, u32[]{:S(2)}, u32[]{:S(2)}) collective-permute-start(bf16[144,512]{1,0:T(8,128)(2,1)S(1)} %get-tuple-element.35.packed_ref.refs_0_), channel_id=1, source_target_pairs={{0,8},{2,10},{4,12},{6,14},{8,0},{10,2},{12,4},{14,6},{16,24},{18,... | collective-permute-start | bytes 442376 | tf_op jit(solution)/shard_map/ppermute | solution.py:378
  69.7 5.2 %collective-permute-start.19 = (bf16[144,512]{1,0:T(8,128)(2,1)S(1)}, bf16[144,512]{1,0:T(8,128)(2,1)S(1)}, u32[]{:S(2)}, u32[]{:S(2)}) collective-permute-start(bf16[144,512]{1,0:T(8,128)(2,1)S(1)} %get-tuple-element.35.packed_ref.refs_0_), channel_id=1, source_target_pairs={{0,4},{2,6},{4,0},{6,2},{8,12},{10,14},{12,8},{14,10},{16,20},{18,... | collective-permute-start | bytes 442376 | tf_op jit(solution)/shard_map/ppermute | solution.py:378
  79.4 8.3 %collective-permute-start.27 = (bf16[128,1024]{1,0:T(8,128)(2,1)S(1)}, bf16[128,1024]{1,0:T(8,128)(2,1)S(1)}, u32[]{:S(2)}, u32[]{:S(2)}) collective-permute-start(bf16[128,1024]{1,0:T(8,128)(2,1)S(1)} %get-tuple-element.38), channel_id=1, source_target_pairs={{0,1},{1,0},{2,3},{3,2},{4,5},{5,4},{6,7},{7,6},{8,9},{9,8},{10,11... | collective-permute-start | bytes 786440 | tf_op jit(solution)/shard_map/ppermute | solution.py:441
  88.4 10.2 %collective-permute-start.31 = (bf16[144,512]{1,0:T(8,128)(2,1)S(1)}, bf16[144,512]{1,0:T(8,128)(2,1)S(1)}, u32[]{:S(2)}, u32[]{:S(2)}) collective-permute-start(bf16[144,512]{1,0:T(8,128)(2,1)S(1)} %get-tuple-element.39.packed_ref.refs_0_), channel_id=1, source_target_pairs={{0,8},{2,10},{4,12},{6,14},{8,0},{10,2},{12,4},{14,6},{16,24},{18,... | collective-permute-start | bytes 442376 | tf_op jit(solution)/shard_map/ppermute | solution.py:378
  95.5 5.2 %collective-permute-start.29 = (bf16[144,512]{1,0:T(8,128)(2,1)S(1)}, bf16[144,512]{1,0:T(8,128)(2,1)S(1)}, u32[]{:S(2)}, u32[]{:S(2)}) collective-permute-start(bf16[144,512]{1,0:T(8,128)(2,1)S(1)} %get-tuple-element.39.packed_ref.refs_0_), channel_id=1, source_target_pairs={{0,4},{2,6},{4,0},{6,2},{8,12},{10,14},{12,8},{14,10},{16,20},{18,... | collective-permute-start | bytes 442376 | tf_op jit(solution)/shard_map/ppermute | solution.py:378
  97.6 5.3 %collective-permute-start.32 = (bf16[144,512]{1,0:T(8,128)(2,1)S(1)}, bf16[144,512]{1,0:T(8,128)(2,1)S(1)}, u32[]{:S(2)}, u32[]{:S(2)}) collective-permute-start(bf16[144,512]{1,0:T(8,128)(2,1)S(1)} %get-tuple-element.39.packed_ref.refs_0_), channel_id=1, source_target_pairs={{0,2},{2,0},{4,6},{6,4},{8,10},{10,8},{12,14},{14,12},{16,18},{18,... | collective-permute-start | bytes 442376 | tf_op jit(solution)/shard_map/ppermute | solution.py:363
  105.2 8.3 %collective-permute-start.37 = (bf16[128,1024]{1,0:T(8,128)(2,1)S(1)}, bf16[128,1024]{1,0:T(8,128)(2,1)S(1)}, u32[]{:S(2)}, u32[]{:S(2)}) collective-permute-start(bf16[128,1024]{1,0:T(8,128)(2,1)S(1)} %get-tuple-element.41), channel_id=1, source_target_pairs={{0,1},{1,0},{2,3},{3,2},{4,5},{5,4},{6,7},{7,6},{8,9},{9,8},{10,11... | collective-permute-start | bytes 786440 | tf_op jit(solution)/shard_map/ppermute | solution.py:441
  114.2 9.4 %collective-permute-start.41 = (bf16[144,512]{1,0:T(8,128)(2,1)S(1)}, bf16[144,512]{1,0:T(8,128)(2,1)S(1)}, u32[]{:S(2)}, u32[]{:S(2)}) collective-permute-start(bf16[144,512]{1,0:T(8,128)(2,1)S(1)} %get-tuple-element.42.packed_ref.refs_0_), channel_id=1, source_target_pairs={{0,8},{2,10},{4,12},{6,14},{8,0},{10,2},{12,4},{14,6},{16,24},{18,... | collective-permute-start | bytes 442376 | tf_op jit(solution)/shard_map/ppermute | solution.py:378
  120.7 5.2 %collective-permute-start.39 = (bf16[144,512]{1,0:T(8,128)(2,1)S(1)}, bf16[144,512]{1,0:T(8,128)(2,1)S(1)}, u32[]{:S(2)}, u32[]{:S(2)}) collective-permute-start(bf16[144,512]{1,0:T(8,128)(2,1)S(1)} %get-tuple-element.42.packed_ref.refs_0_), channel_id=1, source_target_pairs={{0,4},{2,6},{4,0},{6,2},{8,12},{10,14},{12,8},{14,10},{16,20},{18,... | collective-permute-start | bytes 442376 | tf_op jit(solution)/shard_map/ppermute | solution.py:378
  130.3 8.3 %collective-permute-start.47 = (bf16[128,1024]{1,0:T(8,128)(2,1)S(1)}, bf16[128,1024]{1,0:T(8,128)(2,1)S(1)}, u32[]{:S(2)}, u32[]{:S(2)}) collective-permute-start(bf16[128,1024]{1,0:T(8,128)(2,1)S(1)} %get-tuple-element.44), channel_id=1, source_target_pairs={{0,1},{1,0},{2,3},{3,2},{4,5},{5,4},{6,7},{7,6},{8,9},{9,8},{10,11... | collective-permute-start | bytes 786440 | tf_op jit(solution)/shard_map/ppermute | solution.py:441
  (34 other events, 154.5 us)

commit v3 on v2

--- a/solution.py
+++ b/solution.py
@@ -7,6 +7,7 @@
 from jax.experimental import pallas as pl
 from jax.experimental.pallas import tpu as pltpu
 from jax.sharding import PartitionSpec as P
+
 
 HD = 128
 WIN = 1024
@@ -29,8 +30,9 @@
     return slice(h * HD, (h + 1) * HD)
 
 
-def kernel_call(body, outs, ins, scratch=(), flops=10**8, limit=12 << 20):
-    in_specs = [pl.BlockSpec(memory_space=pltpu.VMEM)] * len(ins)
+def kernel_call(body, outs, ins, scratch=(), hbm=0, flops=10**8, limit=12 << 20):
+    in_specs = [pl.BlockSpec(memory_space=pltpu.HBM)] * hbm
+    in_specs += [pl.BlockSpec(memory_space=pltpu.VMEM)] * (len(ins) - hbm)
     moved = sum(math.prod(a.shape) * a.dtype.itemsize for a in list(ins) + list(outs))
     return pl.pallas_call(
         body,
@@ -96,7 +98,7 @@
 
 def hops_of(half, rows):
     reach = (half + rows - 1) // rows
-    return [(d, odd) for d in range(1, (reach + 1) // 2 + 1) for odd in (1, 0)]
+    return [(d, odd) for odd in (1, 0) for d in range(1, (reach + 1) // 2 + 1)]
 
 
 def masks_of(half, rows):
@@ -119,40 +121,47 @@
     return [pl.ds(pl.multiple_of(((me + k) % tps) * cols, HD), cols) for k in range(tps)]
 
 
-def round_body(x_ref, o_ref):
-    o_ref[...] = x_ref[...].astype(o_ref.dtype)
-
-
-def norm_body(tps, *refs):
-    xs = refs[:tps]
-    gain_ref, normed_ref, inv_ref = refs[tps:]
+def prep_body(cot_in, state_in, gain_in, wq_in, wk_in, wv_in, wo_in, *refs):
+    cot_low, outs, cot_ref, sems = refs[0], refs[1:7], refs[7], refs[8]
+    sources = [state_in, gain_in, wq_in, wk_in, wv_in, wo_in]
+    copies = [pltpu.make_async_copy(cot_in, cot_ref, sems.at[0])]
+    for i, (src, dst) in enumerate(zip(sources, outs)):
+        copies.append(pltpu.make_async_copy(src, dst, sems.at[i + 1]))
+    for c in copies:
+        c.start()
+    copies[0].wait()
+    cot_low[...] = cot_ref[...].astype(BF16)
+    for c in copies[1:]:
+        c.wait()
+
+
+def kv_body(blocks, tps, *refs):
+    xs = refs[: blocks * tps]
+    gain_ref, wk_ref, wv_ref, kv_ref, normed_ref, inv_ref = refs[blocks * tps :]
     rows, cols = xs[0].shape
-    vals = [x[...].astype(F32) for x in xs]
-    total = jnp.zeros((rows, 1), F32)
-    for x in vals:
-        total = total + jnp.sum(x * x, axis=1, keepdims=True)
-    inverse = lax.rsqrt(total / (tps * cols) + EPSILON)
-    inv_ref[...] = jnp.broadcast_to(inverse, inv_ref.shape)
-    for x, at in zip(vals, feature_slices(tps, cols)):
-        normed_ref[:, at] = (x * inverse * gain_ref[:, at]).astype(BF16)
-
-
-def kv_body(blocks, *refs):
-    xs = refs[:blocks]
-    wk_ref, wv_ref, kv_ref = refs[blocks:]
-    rows = xs[0].shape[0]
     width = wk_ref.shape[1]
-    x = jnp.concatenate([r[...] for r in xs], axis=0)
+    at = feature_slices(tps, cols)
+    for b in range(blocks):
+        vals = [x[...].astype(F32) for x in xs[b * tps : (b + 1) * tps]]
+        total = jnp.zeros((rows, 1), F32)
+        for x in vals:
+            total = total + jnp.sum(x * x, axis=1, keepdims=True)
+        inverse = lax.rsqrt(total / (tps * cols) + EPSILON)
+        if b == 0:
+            inv_ref[...] = jnp.broadcast_to(inverse, inv_ref.shape)
+        for x, sl in zip(vals, at):
+            normed_ref[b * rows : (b + 1) * rows, sl] = (x * inverse * gain_ref[:, sl]).astype(
+                BF16
+            )
+    x = normed_ref[...]
     kv_ref[:, :width] = mm(x, wk_ref[...]).astype(BF16)
     kv_ref[:, width:] = mm(x, wv_ref[...]).astype(BF16)
 
 
-def q_body(blocks, tps, *refs):
-    xs = refs[:blocks]
-    cots = refs[blocks : blocks + tps]
-    wq_ref, wo_ref, q_ref, go_ref, cot_ref = refs[blocks + tps :]
-    x = jnp.concatenate([r[...] for r in xs], axis=0)
-    q_ref[...] = mm(x, wq_ref[...]).astype(BF16)
+def q_body(tps, *refs):
+    cots = refs[:tps]
+    normed_ref, wq_ref, wo_ref, q_ref, go_ref, cot_ref = refs[tps:]
+    q_ref[...] = mm(normed_ref[...], wq_ref[...]).astype(BF16)
     for c, at in zip(cots, feature_slices(tps, cots[0].shape[1])):
         cot_ref[:, at] = c[...]
     go_ref[...] = mm(cot_ref[...], wo_ref[...], NT).astype(BF16)
@@ -185,15 +194,25 @@
     pack_rows(packed_ref, rows, heads, corr + lse)
 
 
-def scores_t_body(half, qm_ref, qo_ref, kv_ref, st_ref):
-    rows = st_ref.shape[1]
+def split_slots(blocks):
+    early = list(range(blocks - 1)) + list(range(blocks, 2 * blocks - 1))
+    return early, [blocks - 1, 2 * blocks - 1]
+
+
+def scores_t_body(half, qm_ref, qo_ref, kv_ref, early_ref, late_ref):
+    rows = early_ref.shape[1]
     masks = masks_of(half, rows)
-    for h in range(st_ref.shape[0]):
+    cut = qm_ref.shape[0] - rows
+    groups = split_slots(len(masks) // 2)
+    for h in range(early_ref.shape[0]):
         k = kv_ref[:rows, col(h)]
-        s = jnp.concatenate(
-            [mm(k, qm_ref[:, col(h)], NT), mm(k, qo_ref[:, col(h)], NT)], axis=1
-        )
-        st_ref[h] = masked(s * SCALE, masks)
+        for ref, slots, part in zip(
+            (early_ref, late_ref), groups, (slice(0, cut), slice(cut, cut + rows))
+        ):
+            s = jnp.concatenate(
+                [mm(k, qm_ref[part, col(h)], NT), mm(k, qo_ref[part, col(h)], NT)], axis=1
+            )
+            ref[h] = masked(s * SCALE, [masks[i] for i in slots])
 
 
 def query_body(packed_ref, att_ref, p_ref, kvm_ref, kvo_ref, wq_ref, part_ref):
@@ -212,37 +231,65 @@
     part_ref[...] = mm(jnp.concatenate(grads, axis=1), wq_ref[...], NT)
 
 
-def key_body(slots, first, *refs):
+def key_terms(got, part, first, pt_in, pt_ref, kv_ref, qm_ref, qo_ref, gow_ref, h):
+    rows, width = got[0].shape[0] - PAD, got[0].shape[1]
+    near = part.stop - part.start
+    corr = unpack_row(got, rows, h, 0)
+    if first:
+        pt = jnp.exp(pt_in[h] - unpack_row(got, rows, h, 1))
+        pt_ref[h] = pt
+    else:
+        pt = pt_in[h]
+    go = gow_ref[:, col(h)]
+    gp = mm(kv_ref[:rows, col(width // HD + h)], go, NT)
+    gs = (SCALE * pt * (gp - corr)).astype(BF16)
+    gk = mm(gs[:, :near], qm_ref[part, col(h)]) + mm(gs[:, near:], qo_ref[part, col(h)])
+    return gk, mm(pt.astype(BF16), go)
+
+
+def key_early_body(slots, first, *refs):
     got = refs[:slots]
-    pt_in, kv_ref, qm_ref, qo_ref, wk_ref, wv_ref, partq_ref = refs[slots : slots + 7]
-    if first:
-        part_ref, send_ref, pt_ref, gow_ref = refs[slots + 7 :]
-    else:
-        part_ref, send_ref, gow_ref = refs[slots + 7 :]
-        pt_ref = pt_in
-    rows, width = got[0].shape[0] - PAD, got[0].shape[1]
-    heads = width // HD
-    near = qm_ref.shape[0]
+    pt_in, kv_ref, qm_ref, qo_ref = refs[slots : slots + 4]
+    gk_ref, gv_ref = refs[slots + 4 : slots + 6]
+    pt_ref = refs[slots + 6] if first else None
+    gow_ref = refs[-1]
+    rows = got[0].shape[0] - PAD
     for b in range(slots):
         gow_ref[b * rows : (b + 1) * rows, :] = got[b][:rows, :]
+    part = slice(0, slots // 2 * rows)
+    for h in range(pt_in.shape[0]):
+        gk, gv = key_terms(got, part, first, pt_in, pt_ref, kv_ref, qm_ref, qo_ref, gow_ref, h)
+        gk_ref[:, col(h)] = gk
+        gv_ref[:, col(h)] = gv
+
+
+def key_late_body(first, halved, *refs):
+    got = refs[:2]
+    pt_in, kv_ref, qm_ref, qo_ref, gk_ref, gv_ref, wk_ref, wv_ref, partq_ref = refs[2:11]
+    part_ref, send_ref = refs[11:13]
+    pt_ref = refs[13] if first else None
+    gow_ref, sum_ref = refs[-2:]
+    rows = got[0].shape[0] - PAD
+    for b in range(2):
+        gow_ref[b * rows : (b + 1) * rows, :] = got[b][:rows, :]
+    total = qm_ref.shape[0]
+    part = slice(total - rows, total)
     gks, gvs = [], []
-    for h in range(heads):
-        corr = unpack_row(got, rows, h, 0)
-        if first:
-            pt = jnp.exp(pt_in[h] - unpack_row(got, rows, h, 1))
-            pt_ref[h] = pt
-        else:
-            pt = pt_ref[h]
-        go = gow_ref[:, col(h)]
-        gp = mm(kv_ref[:rows, col(heads + h)], go, NT)
-        gs = (SCALE * pt * (gp - corr)).astype(BF16)
-        gk = mm(gs[:, :near], qm_ref[:, col(h)]) + mm(gs[:, near:], qo_ref[:, col(h)])
-        gks.append(gk.astype(BF16))
-        gvs.append(mm(pt.astype(BF16), go).astype(BF16))
-    part = partq_ref[...] + mm(jnp.concatenate(gks, axis=1), wk_ref[...], NT)
-    part = part + mm(jnp.concatenate(gvs, axis=1), wv_ref[...], NT)
-    part_ref[...] = part
-    send_ref[...] = part.astype(BF16)
+    for h in range(pt_in.shape[0]):
+        gk, gv = key_terms(got, part, first, pt_in, pt_ref, kv_ref, qm_ref, qo_ref, gow_ref, h)
+        gks.append((gk_ref[:, col(h)] + gk).astype(BF16))
+        gvs.append((gv_ref[:, col(h)] + gv).astype(BF16))
+    acc = partq_ref[...] + mm(jnp.concatenate(gks, axis=1), wk_ref[...], NT)
+    acc = acc + mm(jnp.concatenate(gvs, axis=1), wv_ref[...], NT)
+    if halved:
+        cols = part_ref.shape[1]
+        sum_ref[...] = acc
+        mine, other = feature_slices(2, cols)
+        part_ref[...] = sum_ref[:, mine]
+        send_ref[...] = sum_ref[:, other].astype(BF16)
+    else:
+        part_ref[...] = acc
+        send_ref[...] = acc.astype(BF16)
 
 
 def combine_body(part_ref, recv_ref, inv_ref, gain_ref, wo_ref, att_ref, *refs):
@@ -268,9 +315,12 @@
     last_ref, sums_ref, vec_ref = refs[SSTEP:]
     rows, cols = last_ref.shape
     inverse = inv_ref[:, :1]
-    vec_ref[...] = inverse * (gain_ref[...] * (part_ref[...] + recv_ref[...].astype(F32)))
-    off = pl.multiple_of(lax.axis_index("tp") * cols, HD)
-    last_ref[...] = vec_ref[:, pl.ds(off, cols)]
+    own = pl.ds(pl.multiple_of(lax.axis_index("tp") * cols, HD), cols)
+    vec = part_ref[...] + recv_ref[...].astype(F32)
+    if part_ref.shape[1] != cols:
+        vec_ref[...] = vec
+        vec = vec_ref[:, own]
+    last_ref[...] = inverse * (gain_ref[:, own] * vec)
     all_k = list(kry) + [last_ref]
     count = SSTEP * (SSTEP + 1) // 2 + SSTEP
     acc = [jnp.zeros((8, HD), F32) for _ in range(count)]
@@ -355,17 +405,18 @@
     chips = seq // 2
     hops = hops_of(half, rows)
     blocks = 1 + len(hops)
-    slots = 2 * blocks
-    nwin = slots * rows
-    gain = norm_gain[None, :]
+    early, late = split_slots(blocks)
+    ranks = seq * tps
+    full = tps * cols
 
     def swap_core(x):
         return lax.ppermute(x, "seq", [(i, i ^ 1) for i in range(seq)])
 
     def tp_blocks(x):
-        return [x] + [
-            lax.ppermute(x, "tp", [((i + k) % tps, i) for i in range(tps)]) for k in range(1, tps)
-        ]
+        out = [x]
+        for k in range(1, tps):
+            out.append(lax.ppermute(x, "tp", [((i + k) % tps, i) for i in range(tps)]))
+        return out
 
     def fetch(x):
         got = [x]
@@ -375,67 +426,87 @@
                 q = swap_partner(c, d, odd)
                 if 0 <= q < chips:
                     pairs += [(2 * c, 2 * q), (2 * c + 1, 2 * q + 1)]
+                else:
+                    pairs += [(2 * c, 2 * c + 1), (2 * c + 1, 2 * c)]
             got.append(lax.ppermute(x, "seq", pairs))
         return got
 
-    states = tp_blocks(state)
-    (cot_low,) = kernel_call(round_body, [sds(rows, cols, dtype=BF16)], [cotangent])
+    raw = fetch(state)
+    cot_low, state_v, gain, w_query, w_key, w_value, w_out = kernel_call(
+        prep_body,
+        [sds(rows, cols, dtype=BF16), state, sds(1, full)]
+        + [w_query, w_key, w_value, w_out],
+        [cotangent, state, norm_gain[None, :], w_query, w_key, w_value, w_out],
+        scratch=[pltpu.VMEM((rows, cols), F32), pltpu.SemaphoreType.DMA((7,))],
+        hbm=7,
+        limit=49 << 20,
+    )
+    pieces = []
+    for x in raw:
+        pieces += tp_blocks(x)
+    pieces[0] = state_v
     cots = tp_blocks(cot_low)
-    normed, inv = kernel_call(
-        functools.partial(norm_body, tps),
-        [sds(rows, tps * cols, dtype=BF16), sds(rows, HD)],
-        states + [gain],
-    )
-    near = fetch(normed)
-    (kv_mine,) = kernel_call(
-        functools.partial(kv_body, blocks),
-        [sds(blocks * rows, 2 * width, dtype=BF16)],
-        near + [w_key, w_value],
+    kv_mine, normed, inv = kernel_call(
+        functools.partial(kv_body, blocks, tps),
+        [
+            sds(blocks * rows, 2 * width, dtype=BF16),
+            sds(blocks * rows, full, dtype=BF16),
+            sds(rows, HD),
+        ],
+        pieces + [gain, w_key, w_value],
     )
     kv_other = swap_core(kv_mine)
     q_mine, go0 = kernel_call(
-        functools.partial(q_body, blocks, tps),
+        functools.partial(q_body, tps),
         [sds(blocks * rows, width, dtype=BF16), sds(rows, width, dtype=BF16)],
-        near + cots + [w_query, w_out],
-        scratch=[pltpu.VMEM((rows, tps * cols), BF16)],
+        cots + [normed, w_query, w_out],
+        scratch=[pltpu.VMEM((rows, full), BF16)],
     )
     q_other = swap_core(q_mine)
     probs, att, packed = kernel_call(
         functools.partial(stats_body, half),
-        [
-            sds(heads, rows, nwin),
-            sds(rows, width),
-            sds(rows + PAD, width, dtype=BF16),
-        ],
+        [sds(heads, rows, 2 * blocks * rows), sds(rows, width), sds(rows + PAD, width, dtype=BF16)],
         [kv_mine, kv_other, q_mine, go0],
     )
-    (probs_t,) = kernel_call(
-        functools.partial(scores_t_body, half),
-        [sds(heads, rows, nwin)],
-        [q_mine, q_other, kv_mine],
-    )
     krylov = [cotangent]
-    ranks = seq * tps
     for n in range(SSTEP):
+        first, last = n == 0, n == SSTEP - 1
+        if first:
+            pt_early, pt_late = kernel_call(
+                functools.partial(scores_t_body, half),
+                [sds(heads, rows, len(early) * rows), sds(heads, rows, 2 * rows)],
+                [q_mine, q_other, kv_mine],
+            )
         got = fetch(packed)
         got = got + [swap_core(x) for x in got]
         (part_q,) = kernel_call(
             query_body,
-            [sds(rows, tps * cols)],
+            [sds(rows, full)],
             [packed, att, probs, kv_mine, kv_other, w_query],
         )
-        outs = [sds(rows, tps * cols), sds(rows, tps * cols, dtype=BF16)]
-        if n == 0:
-            outs.append(sds(heads, rows, nwin))
         res = kernel_call(
-            functools.partial(key_body, slots, n == 0),
-            outs,
-            got + [probs_t, kv_mine, q_mine, q_other, w_key, w_value, part_q],
-            scratch=[pltpu.VMEM((nwin, width), BF16)],
+            functools.partial(key_early_body, len(early), first),
+            [sds(rows, width), sds(rows, width)]
+            + ([sds(heads, rows, len(early) * rows)] if first else []),
+            [got[i] for i in early] + [pt_early, kv_mine, q_mine, q_other],
+            scratch=[pltpu.VMEM((len(early) * rows, width), BF16)],
+        )
+        gk, gv = res[:2]
+        if first:
+            pt_early = res[2]
+        halved = last and tps == 2
+        span = cols if halved else full
+        res = kernel_call(
+            functools.partial(key_late_body, first, halved),
+            [sds(rows, span), sds(rows, span, dtype=BF16)]
+            + ([sds(heads, rows, 2 * rows)] if first else []),
+            [got[i] for i in late]
+            + [pt_late, kv_mine, q_mine, q_other, gk, gv, w_key, w_value, part_q],
+            scratch=[pltpu.VMEM((2 * rows, width), BF16), pltpu.VMEM((rows, full), F32)],
         )
         part, send = res[:2]
-        if n == 0:
-            probs_t = res[2]
+        if first:
+            pt_late = res[2]
         k = 1
         while True:
             recv = lax.ppermute(send, "tp", [(i, i ^ k) for i in range(tps)])
@@ -444,22 +515,21 @@
                 break
             part = part + recv.astype(F32)
             send = part.astype(BF16)
-        if n < SSTEP - 1:
+        if not last:
             kry, packed = kernel_call(
                 combine_body,
                 [sds(rows, cols), sds(rows + PAD, width, dtype=BF16)],
                 [part, recv, inv, gain, w_out, att],
-                scratch=[pltpu.VMEM((rows, tps * cols), F32)],
+                scratch=[pltpu.VMEM((rows, full), F32)],
             )
-            krylov.append(kry)
         else:
-            last, sums = kernel_call(
+            kry, sums = kernel_call(
                 gram_body,
                 [sds(rows, cols), sds(ranks, PAD, HD)],
                 [part, recv, inv, gain] + krylov,
-                scratch=[pltpu.VMEM((rows, tps * cols), F32)],
+                scratch=[pltpu.VMEM((rows, full), F32)],
             )
-            krylov.append(last)
+        krylov.append(kry)
     sums = lax.all_to_all(sums, ("seq", "tp"), 0, 0)
     adjoint, residual = kernel_call(
         finish_body,

time: 160 us -> 148 us (0.925)
  starting transfers between devices: 59.4 us -> 36.9 us
  waiting for transfers between devices: 50.1 us -> 62.5 us
  Pallas kernels: 25.7 us -> 29.6 us
  blocking collectives: 19 us -> 15.2 us
    ppermute x20, starting transfers between devices: 44 us -> 21 us  [fetch(): got.append(lax.ppermute(x, 'seq', pairs))]
    ppermute x20, waiting for transfers between devices: 15.1 us -> 28.4 us  [fetch(): got.append(lax.ppermute(x, 'seq', pairs))]
    pallas_call x19 -> x22, Pallas kernels: 25.7 us -> 29.6 us  [kernel_call(): pl.pallas_call(body, out_shape=[jax.ShapeDtypeStruct(o.shape, o.dtype) fo...]
    all_to_all x1, blocking collectives: 19 us -> 15.2 us  [on_device(): sums = lax.all_to_all(sums, ('seq', 'tp'), 0, 0)]
    ppermute x2 -> x6, starting transfers between devices: 4.59 us -> 7.1 us  [tp_blocks(): out.append(lax.ppermute(x, 'tp', [((i + k) % tps, i) for i in range(tps)]))]
    ppermute x22, starting transfers between devices: 4.51 us -> 2.49 us  [swap_core(): return lax.ppermute(x, 'seq', [(i, i ^ 1) for i in range(seq)])]
    unnamed x20 -> x6, local copies, waits for them, and re-layouts: 4.07 us -> 2.54 us
    ppermute x2 -> x6, waiting for transfers between devices: 8.1 us -> 8.06 us  [tp_blocks(): out.append(lax.ppermute(x, 'tp', [((i + k) % tps, i) for i in range(tps)]))]
  transfers between devices with their start and end apart: 48 -> 52, of which waited for: 16 -> 17; matrix products, arithmetic and copies ran while one was open for 0% -> 0% of each run, Pallas kernels for 7% -> 13%
where the time goes in v3:
time: 148 us
  waiting for transfers between devices  62.5 us (42%)
  starting transfers between devices  36.9 us (25%)
  Pallas kernels  29.6 us (20%)
  blocking collectives  15.2 us (10%)
  local copies, waits for them, and re-layouts  2.54 us (2%)
    pallas_call x22, Pallas kernels, kernel_call(): pl.pallas_call(body, out_shape=[jax.ShapeDtypeStruct(o.shape, o.dtype) fo...  29.6 us
    ppermute x20, waiting for transfers between devices, fetch(): got.append(lax.ppermute(x, 'seq', pairs))  28.4 us
    ppermute x4, waiting for transfers between devices, on_device(): recv = lax.ppermute(send, 'tp', [(i, i ^ k) for i in range(tps)])  26 us
    ppermute x20, starting transfers between devices, fetch(): got.append(lax.ppermute(x, 'seq', pairs))  21 us
    all_to_all x1, blocking collectives, on_device(): sums = lax.all_to_all(sums, ('seq', 'tp'), 0, 0)  15.2 us
    ppermute x6, waiting for transfers between devices, tp_blocks(): out.append(lax.ppermute(x, 'tp', [((i + k) % tps, i) for i in range(tps)]))  8.06 us
    ppermute x6, starting transfers between devices, tp_blocks(): out.append(lax.ppermute(x, 'tp', [((i + k) % tps, i) for i in range(tps)]))  7.1 us
    ppermute x4, starting transfers between devices, on_device(): recv = lax.ppermute(send, 'tp', [(i, i ^ k) for i in range(tps)])  6.27 us
  transfers between devices with their start and end apart: 52, of which 17 were waited for; matrix products, arithmetic and copies ran while one was open for 0% of the time, Pallas kernels for 13%

profile of v3, /device:TPU:0, one launch (start us, length us, event | category | flops | bytes accessed | tf_op | source)
XLA Modules:
  0.0 147.8 jit_solution(16044869625377082549)
XLA Ops:
  1.3 4.1 %collective-permute-start.7 = (bf16[128,512]{1,0:T(8,128)(2,1)}, bf16[128,512]{1,0:T(8,128)(2,1)S(1)}, u32[]{:S(2)}, u32[]{:S(2)}) collective-permute-start(bf16[128,512]{1,0:T(8,128)(2,1)} %state_in.1), channel_id=1, source_target_pairs={{0,8},{2,10},{4,12},{6,14},{8,0},{10,2},{12,4},{14,6},{16,24},{18,... | collective-permute-start | bytes 393224 | tf_op jit(solution)/shard_map/ppermute | solution.py:431
  5.3 1.9 %collective-permute-start.5 = (bf16[128,512]{1,0:T(8,128)(2,1)}, bf16[128,512]{1,0:T(8,128)(2,1)S(1)}, u32[]{:S(2)}, u32[]{:S(2)}) collective-permute-start(bf16[128,512]{1,0:T(8,128)(2,1)} %state_in.1), channel_id=1, source_target_pairs={{0,4},{2,6},{4,0},{6,2},{8,12},{10,14},{12,8},{14,10},{16,20},{18,... | collective-permute-start | bytes 393224 | tf_op jit(solution)/shard_map/ppermute | solution.py:431
  16.6 2.4 %shard_map.86 = (bf16[128,512]{1,0:T(8,128)(2,1)S(1)}, bf16[128,512]{1,0:T(8,128)(2,1)S(1)}, f32[1,1024]{1,0:T(1,128)S(1)}, bf16[1024,512]{1,0:T(8,128)(2,1)S(1)...) custom-call(f32[128,512]{1,0:T(8,128)S(1)} %copy-done, ...), custom_call_target="tpu_custom_call" | custom-call | flops 100000000 | bytes 9052160 | tf_op jit(solution)/shard_map/pallas_call | solution.py:37
  19.4 2.0 %collective-permute-done.8.refs_9_ = bf16[128,512]{1,0:T(8,128)(2,1)S(1)} collective-permute-done((bf16[128,512]{1,0:T(8,128)(2,1)S(1)}, bf16[128,512]{1,0:T(8,128)(2,1)S(1)}, u32[]{:S(2)}, u32[]{:S(2)}) %collective-permute-start.8) | collective-permute-done | bytes 131104 | tf_op jit(solution)/shard_map/ppermute | solution.py:418
  22.8 1.9 %shard_map.87 = (bf16[640,1024]{1,0:T(8,128)(2,1)S(1)}, bf16[640,1024]{1,0:T(8,128)(2,1)S(1)}, f32[128,128]{1,0:T(8,128)S(1)}) custom-call(bf16[128,512]{1,0:T(8,128)(2,1)S(1)} %get-tuple-element.45.refs_0_, bf16[128,512]{1,0:T(8,128)(2,1)S(1)} %collective-permute-done.refs_1_, bf16[128,512]{1,0:T(8,128)(2,1)S(1)} %collective-permute-done.1.refs_2_, ...), custom_call_target="tpu_custom_call" | custom-call | flops 100000000 | bytes 6098944 | tf_op jit(solution)/shard_map/pallas_call | solution.py:37
  26.4 4.3 %collective-permute-done.10.refs_1_ = bf16[128,512]{1,0:T(8,128)(2,1)S(1)} collective-permute-done((bf16[128,512]{1,0:T(8,128)(2,1)S(1)}, bf16[128,512]{1,0:T(8,128)(2,1)S(1)}, u32[]{:S(2)}, u32[]{:S(2)}) %collective-permute-start.10) | collective-permute-done | bytes 131104 | tf_op jit(solution)/shard_map/ppermute | solution.py:418
  31.9 2.6 %shard_map.89 = (f32[4,128,1280]{2,1,0:T(8,128)S(1)}, f32[128,512]{1,0:T(8,128)S(1)}, bf16[144,512]{1,0:T(8,128)(2,1)S(1)}) custom-call(bf16[640,1024]{1,0:T(8,128)(2,1)S(1)} %get-tuple-element.49.kvm_ref.kv_ref.refs_9_.refs_3_, bf16[640,1024]{1,0:T(8,128)(2,1)S(1)} %collective-permute-done.9.kvo_ref, ...), custom_call_target="tpu_custom_call" | custom-call | flops 100000000 | bytes 6438912 | tf_op jit(solution)/shard_map/pallas_call | solution.py:37
  36.0 2.3 %collective-permute-start.11 = (bf16[144,512]{1,0:T(8,128)(2,1)S(1)}, bf16[144,512]{1,0:T(8,128)(2,1)S(1)}, u32[]{:S(2)}, u32[]{:S(2)}) collective-permute-start(bf16[144,512]{1,0:T(8,128)(2,1)S(1)} %get-tuple-element.56.refs_0_.packed_ref), channel_id=1, source_target_pairs={{0,8},{2,10},{4,12},{6,14},{8,0},{10,2},{12,4},{14,6},{16,24},{18,... | collective-permute-start | bytes 442376 | tf_op jit(solution)/shard_map/ppermute | solution.py:431
  38.4 4.1 %collective-permute-done.16.refs_3_ = bf16[144,512]{1,0:T(8,128)(2,1)S(1)} collective-permute-done((bf16[144,512]{1,0:T(8,128)(2,1)S(1)}, bf16[144,512]{1,0:T(8,128)(2,1)S(1)}, u32[]{:S(2)}, u32[]{:S(2)}) %collective-permute-start.16) | collective-permute-done | bytes 147488 | tf_op jit(solution)/shard_map/ppermute | solution.py:431
  43.1 2.5 %collective-permute-done.11.refs_0_ = bf16[144,512]{1,0:T(8,128)(2,1)S(1)} collective-permute-done((bf16[144,512]{1,0:T(8,128)(2,1)S(1)}, bf16[144,512]{1,0:T(8,128)(2,1)S(1)}, u32[]{:S(2)}, u32[]{:S(2)}) %collective-permute-start.11) | collective-permute-done | bytes 147488 | tf_op jit(solution)/shard_map/ppermute | solution.py:431
  52.1 7.2 %collective-permute-done.21.recv_ref = bf16[128,1024]{1,0:T(8,128)(2,1)S(1)} collective-permute-done((bf16[128,1024]{1,0:T(8,128)(2,1)S(1)}, bf16[128,1024]{1,0:T(8,128)(2,1)S(1)}, u32[]{:S(2)}, u32[]{:S(2)}) %collective-permute-start.21) | collective-permute-done | bytes 262176 | tf_op jit(solution)/shard_map/ppermute | solution.py:512
  61.3 2.4 %collective-permute-start.22 = (bf16[144,512]{1,0:T(8,128)(2,1)S(1)}, bf16[144,512]{1,0:T(8,128)(2,1)S(1)}, u32[]{:S(2)}, u32[]{:S(2)}) collective-permute-start(bf16[144,512]{1,0:T(8,128)(2,1)S(1)} %get-tuple-element.66.refs_0_.packed_ref), channel_id=1, source_target_pairs={{0,8},{2,10},{4,12},{6,14},{8,0},{10,2},{12,4},{14,6},{16,24},{18,... | collective-permute-start | bytes 442376 | tf_op jit(solution)/shard_map/ppermute | solution.py:431
  63.7 1.9 %collective-permute-done.26.refs_3_ = bf16[144,512]{1,0:T(8,128)(2,1)S(1)} collective-permute-done((bf16[144,512]{1,0:T(8,128)(2,1)S(1)}, bf16[144,512]{1,0:T(8,128)(2,1)S(1)}, u32[]{:S(2)}, u32[]{:S(2)}) %collective-permute-start.26) | collective-permute-done | bytes 147488 | tf_op jit(solution)/shard_map/ppermute | solution.py:431
  66.1 4.9 %collective-permute-done.22.refs_0_ = bf16[144,512]{1,0:T(8,128)(2,1)S(1)} collective-permute-done((bf16[144,512]{1,0:T(8,128)(2,1)S(1)}, bf16[144,512]{1,0:T(8,128)(2,1)S(1)}, u32[]{:S(2)}, u32[]{:S(2)}) %collective-permute-start.22) | collective-permute-done | bytes 147488 | tf_op jit(solution)/shard_map/ppermute | solution.py:431
  77.0 7.2 %collective-permute-done.31.recv_ref = bf16[128,1024]{1,0:T(8,128)(2,1)S(1)} collective-permute-done((bf16[128,1024]{1,0:T(8,128)(2,1)S(1)}, bf16[128,1024]{1,0:T(8,128)(2,1)S(1)}, u32[]{:S(2)}, u32[]{:S(2)}) %collective-permute-start.31) | collective-permute-done | bytes 262176 | tf_op jit(solution)/shard_map/ppermute | solution.py:512
  85.6 2.9 %collective-permute-start.32 = (bf16[144,512]{1,0:T(8,128)(2,1)S(1)}, bf16[144,512]{1,0:T(8,128)(2,1)S(1)}, u32[]{:S(2)}, u32[]{:S(2)}) collective-permute-start(bf16[144,512]{1,0:T(8,128)(2,1)S(1)} %get-tuple-element.73.refs_0_.packed_ref), channel_id=1, source_target_pairs={{0,8},{2,10},{4,12},{6,14},{8,0},{10,2},{12,4},{14,6},{16,24},{18,... | collective-permute-start | bytes 442376 | tf_op jit(solution)/shard_map/ppermute | solution.py:431
  88.5 1.9 %collective-permute-done.36.refs_3_ = bf16[144,512]{1,0:T(8,128)(2,1)S(1)} collective-permute-done((bf16[144,512]{1,0:T(8,128)(2,1)S(1)}, bf16[144,512]{1,0:T(8,128)(2,1)S(1)}, u32[]{:S(2)}, u32[]{:S(2)}) %collective-permute-start.36) | collective-permute-done | bytes 147488 | tf_op jit(solution)/shard_map/ppermute | solution.py:431
  91.0 4.9 %collective-permute-done.32.refs_0_ = bf16[144,512]{1,0:T(8,128)(2,1)S(1)} collective-permute-done((bf16[144,512]{1,0:T(8,128)(2,1)S(1)}, bf16[144,512]{1,0:T(8,128)(2,1)S(1)}, u32[]{:S(2)}, u32[]{:S(2)}) %collective-permute-start.32) | collective-permute-done | bytes 147488 | tf_op jit(solution)/shard_map/ppermute | solution.py:431
  101.7 7.2 %collective-permute-done.41.recv_ref = bf16[128,1024]{1,0:T(8,128)(2,1)S(1)} collective-permute-done((bf16[128,1024]{1,0:T(8,128)(2,1)S(1)}, bf16[128,1024]{1,0:T(8,128)(2,1)S(1)}, u32[]{:S(2)}, u32[]{:S(2)}) %collective-permute-start.41) | collective-permute-done | bytes 262176 | tf_op jit(solution)/shard_map/ppermute | solution.py:512
  110.3 2.9 %collective-permute-start.42 = (bf16[144,512]{1,0:T(8,128)(2,1)S(1)}, bf16[144,512]{1,0:T(8,128)(2,1)S(1)}, u32[]{:S(2)}, u32[]{:S(2)}) collective-permute-start(bf16[144,512]{1,0:T(8,128)(2,1)S(1)} %get-tuple-element.78.refs_0_.packed_ref), channel_id=1, source_target_pairs={{0,8},{2,10},{4,12},{6,14},{8,0},{10,2},{12,4},{14,6},{16,24},{18,... | collective-permute-start | bytes 442376 | tf_op jit(solution)/shard_map/ppermute | solution.py:431
  113.2 1.9 %collective-permute-done.46.refs_3_ = bf16[144,512]{1,0:T(8,128)(2,1)S(1)} collective-permute-done((bf16[144,512]{1,0:T(8,128)(2,1)S(1)}, bf16[144,512]{1,0:T(8,128)(2,1)S(1)}, u32[]{:S(2)}, u32[]{:S(2)}) %collective-permute-start.46) | collective-permute-done | bytes 147488 | tf_op jit(solution)/shard_map/ppermute | solution.py:431
  115.7 4.9 %collective-permute-done.42.refs_0_ = bf16[144,512]{1,0:T(8,128)(2,1)S(1)} collective-permute-done((bf16[144,512]{1,0:T(8,128)(2,1)S(1)}, bf16[144,512]{1,0:T(8,128)(2,1)S(1)}, u32[]{:S(2)}, u32[]{:S(2)}) %collective-permute-start.42) | collective-permute-done | bytes 147488 | tf_op jit(solution)/shard_map/ppermute | solution.py:431
  126.5 4.4 %collective-permute-done.51.recv_ref = bf16[128,512]{1,0:T(8,128)(2,1)S(1)} collective-permute-done((bf16[128,512]{1,0:T(8,128)(2,1)S(1)}, bf16[128,512]{1,0:T(8,128)(2,1)S(1)}, u32[]{:S(2)}, u32[]{:S(2)}) %collective-permute-start.51) | collective-permute-done | bytes 131104 | tf_op jit(solution)/shard_map/ppermute | solution.py:512
  131.3 15.2 %all_to_all.5.sums_ref = f32[32,16,128]{2,1,0:T(8,128)S(1)} all-to-all(f32[32,16,128]{2,1,0:T(8,128)S(1)} %get-tuple-element.86), channel_id=1, replica_groups=mesh['seq'=16,'tp'=2] {'seq','tp'}, dimensions={0} | all-to-all | bytes 524288 | tf_op jit(solution)/shard_map/all_to_all | solution.py:533
  (109 shorter events, 48.7 us)
Async XLA Ops:
  0.6 8.1 %collective-permute-start.3 = (bf16[128,512]{1,0:T(8,128)(2,1)}, bf16[128,512]{1,0:T(8,128)(2,1)S(1)}, u32[]{:S(2)}, u32[]{:S(2)}) collective-permute-start(bf16[128,512]{1,0:T(8,128)(2,1)} %state_in.1), channel_id=1, source_target_pairs={{0,2},{2,0},{4,6},{6,4},{8,16},{10,18},{12,20},{14,22},{16,8},{18,... | collective-permute-start | bytes 393224 | tf_op jit(solution)/shard_map/ppermute | solution.py:431
  1.2 8.1 %collective-permute-start.1 = (bf16[128,512]{1,0:T(8,128)(2,1)}, bf16[128,512]{1,0:T(8,128)(2,1)S(1)}, u32[]{:S(2)}, u32[]{:S(2)}) collective-permute-start(bf16[128,512]{1,0:T(8,128)(2,1)} %state_in.1), channel_id=1, source_target_pairs={{0,2},{2,0},{4,8},{6,10},{8,4},{10,6},{12,16},{14,18},{16,12},{18,... | collective-permute-start | bytes 393224 | tf_op jit(solution)/shard_map/ppermute | solution.py:431
  1.3 10.8 %collective-permute-start.7 = (bf16[128,512]{1,0:T(8,128)(2,1)}, bf16[128,512]{1,0:T(8,128)(2,1)S(1)}, u32[]{:S(2)}, u32[]{:S(2)}) collective-permute-start(bf16[128,512]{1,0:T(8,128)(2,1)} %state_in.1), channel_id=1, source_target_pairs={{0,8},{2,10},{4,12},{6,14},{8,0},{10,2},{12,4},{14,6},{16,24},{18,... | collective-permute-start | bytes 393224 | tf_op jit(solution)/shard_map/ppermute | solution.py:431
  5.3 8.2 %collective-permute-start.5 = (bf16[128,512]{1,0:T(8,128)(2,1)}, bf16[128,512]{1,0:T(8,128)(2,1)S(1)}, u32[]{:S(2)}, u32[]{:S(2)}) collective-permute-start(bf16[128,512]{1,0:T(8,128)(2,1)} %state_in.1), channel_id=1, source_target_pairs={{0,4},{2,6},{4,0},{6,2},{8,12},{10,14},{12,8},{14,10},{16,20},{18,... | collective-permute-start | bytes 393224 | tf_op jit(solution)/shard_map/ppermute | solution.py:431
  7.2 11.8 %collective-permute-start = (bf16[128,512]{1,0:T(8,128)(2,1)}, bf16[128,512]{1,0:T(8,128)(2,1)S(1)}, u32[]{:S(2)}, u32[]{:S(2)}) collective-permute-start(bf16[128,512]{1,0:T(8,128)(2,1)} %state_in.1), channel_id=1, source_target_pairs={{1,0},{0,1},{3,2},{2,3},{5,4},{4,5},{7,6},{6,7},{9,8},{8,9},{11,10... | collective-permute-start | bytes 393224 | tf_op jit(solution)/shard_map/ppermute | solution.py:418
  8.7 10.3 %collective-permute-start.4 = (bf16[128,512]{1,0:T(8,128)(2,1)S(1)}, bf16[128,512]{1,0:T(8,128)(2,1)S(1)}, u32[]{:S(2)}, u32[]{:S(2)}) collective-permute-start(bf16[128,512]{1,0:T(8,128)(2,1)S(1)} %collective-permute-done.3.refs_4_), channel_id=1, source_target_pairs={{1,0},{0,1},{3,2},{2,3},{5,4},{4,5},{7,6},{6,7},{9,8},{8,9},{11,10... | collective-permute-start | bytes 393224 | tf_op jit(solution)/shard_map/ppermute | solution.py:418
  9.3 10.2 %collective-permute-start.2 = (bf16[128,512]{1,0:T(8,128)(2,1)S(1)}, bf16[128,512]{1,0:T(8,128)(2,1)S(1)}, u32[]{:S(2)}, u32[]{:S(2)}) collective-permute-start(bf16[128,512]{1,0:T(8,128)(2,1)S(1)} %collective-permute-done.1.refs_2_), channel_id=1, source_target_pairs={{1,0},{0,1},{3,2},{2,3},{5,4},{4,5},{7,6},{6,7},{9,8},{8,9},{11,10... | collective-permute-start | bytes 393224 | tf_op jit(solution)/shard_map/ppermute | solution.py:418
  12.1 9.3 %collective-permute-start.8 = (bf16[128,512]{1,0:T(8,128)(2,1)S(1)}, bf16[128,512]{1,0:T(8,128)(2,1)S(1)}, u32[]{:S(2)}, u32[]{:S(2)}) collective-permute-start(bf16[128,512]{1,0:T(8,128)(2,1)S(1)} %collective-permute-done.7.refs_8_), channel_id=1, source_target_pairs={{1,0},{0,1},{3,2},{2,3},{5,4},{4,5},{7,6},{6,7},{9,8},{8,9},{11,10... | collective-permute-start | bytes 393224 | tf_op jit(solution)/shard_map/ppermute | solution.py:418
  13.6 9.2 %collective-permute-start.6 = (bf16[128,512]{1,0:T(8,128)(2,1)S(1)}, bf16[128,512]{1,0:T(8,128)(2,1)S(1)}, u32[]{:S(2)}, u32[]{:S(2)}) collective-permute-start(bf16[128,512]{1,0:T(8,128)(2,1)S(1)} %collective-permute-done.5.refs_6_), channel_id=1, source_target_pairs={{1,0},{0,1},{3,2},{2,3},{5,4},{4,5},{7,6},{6,7},{9,8},{8,9},{11,10... | collective-permute-start | bytes 393224 | tf_op jit(solution)/shard_map/ppermute | solution.py:418
  34.6 7.9 %collective-permute-start.16 = (bf16[144,512]{1,0:T(8,128)(2,1)S(1)}, bf16[144,512]{1,0:T(8,128)(2,1)S(1)}, u32[]{:S(2)}, u32[]{:S(2)}) collective-permute-start(bf16[144,512]{1,0:T(8,128)(2,1)S(1)} %get-tuple-element.56.refs_0_.packed_ref), channel_id=1, source_target_pairs={{0,4},{2,6},{4,0},{6,2},{8,12},{10,14},{12,8},{14,10},{16,20},{18,... | collective-permute-start | bytes 442376 | tf_op jit(solution)/shard_map/ppermute | solution.py:431
  35.7 7.3 %collective-permute-start.14 = (bf16[144,512]{1,0:T(8,128)(2,1)S(1)}, bf16[144,512]{1,0:T(8,128)(2,1)S(1)}, u32[]{:S(2)}, u32[]{:S(2)}) collective-permute-start(bf16[144,512]{1,0:T(8,128)(2,1)S(1)} %get-tuple-element.56.refs_0_.packed_ref), channel_id=1, source_target_pairs={{0,2},{2,0},{4,8},{6,10},{8,4},{10,6},{12,16},{14,18},{16,12},{18,... | collective-permute-start | bytes 442376 | tf_op jit(solution)/shard_map/ppermute | solution.py:431
  36.0 9.5 %collective-permute-start.11 = (bf16[144,512]{1,0:T(8,128)(2,1)S(1)}, bf16[144,512]{1,0:T(8,128)(2,1)S(1)}, u32[]{:S(2)}, u32[]{:S(2)}) collective-permute-start(bf16[144,512]{1,0:T(8,128)(2,1)S(1)} %get-tuple-element.56.refs_0_.packed_ref), channel_id=1, source_target_pairs={{0,8},{2,10},{4,12},{6,14},{8,0},{10,2},{12,4},{14,6},{16,24},{18,... | collective-permute-start | bytes 442376 | tf_op jit(solution)/shard_map/ppermute | solution.py:431
  38.4 9.6 %collective-permute-start.17 = (bf16[144,512]{1,0:T(8,128)(2,1)S(1)}, bf16[144,512]{1,0:T(8,128)(2,1)S(1)}, u32[]{:S(2)}, u32[]{:S(2)}) collective-permute-start(bf16[144,512]{1,0:T(8,128)(2,1)S(1)} %get-tuple-element.56.refs_0_.packed_ref), channel_id=1, source_target_pairs={{0,2},{2,0},{4,6},{6,4},{8,10},{10,8},{12,14},{14,12},{16,18},{18,... | collective-permute-start | bytes 442376 | tf_op jit(solution)/shard_map/ppermute | solution.py:413
  50.6 8.8 %collective-permute-start.21 = (bf16[128,1024]{1,0:T(8,128)(2,1)S(1)}, bf16[128,1024]{1,0:T(8,128)(2,1)S(1)}, u32[]{:S(2)}, u32[]{:S(2)}) collective-permute-start(bf16[128,1024]{1,0:T(8,128)(2,1)S(1)} %get-tuple-element.64), channel_id=1, source_target_pairs={{0,1},{1,0},{2,3},{3,2},{4,5},{5,4},{6,7},{7,6},{8,9},{9,8},{10,11... | collective-permute-start | bytes 786440 | tf_op jit(solution)/shard_map/ppermute | solution.py:512
  61.3 9.8 %collective-permute-start.22 = (bf16[144,512]{1,0:T(8,128)(2,1)S(1)}, bf16[144,512]{1,0:T(8,128)(2,1)S(1)}, u32[]{:S(2)}, u32[]{:S(2)}) collective-permute-start(bf16[144,512]{1,0:T(8,128)(2,1)S(1)} %get-tuple-element.66.refs_0_.packed_ref), channel_id=1, source_target_pairs={{0,8},{2,10},{4,12},{6,14},{8,0},{10,2},{12,4},{14,6},{16,24},{18,... | collective-permute-start | bytes 442376 | tf_op jit(solution)/shard_map/ppermute | solution.py:431
  63.7 9.1 %collective-permute-start.27 = (bf16[144,512]{1,0:T(8,128)(2,1)S(1)}, bf16[144,512]{1,0:T(8,128)(2,1)S(1)}, u32[]{:S(2)}, u32[]{:S(2)}) collective-permute-start(bf16[144,512]{1,0:T(8,128)(2,1)S(1)} %get-tuple-element.66.refs_0_.packed_ref), channel_id=1, source_target_pairs={{0,2},{2,0},{4,6},{6,4},{8,10},{10,8},{12,14},{14,12},{16,18},{18,... | collective-permute-start | bytes 442376 | tf_op jit(solution)/shard_map/ppermute | solution.py:413
  65.6 7.3 %collective-permute-start.30 = (bf16[144,512]{1,0:T(8,128)(2,1)S(1)}, bf16[144,512]{1,0:T(8,128)(2,1)S(1)}, u32[]{:S(2)}, u32[]{:S(2)}) collective-permute-start(bf16[144,512]{1,0:T(8,128)(2,1)S(1)} %collective-permute-done.26.refs_3_), channel_id=1, source_target_pairs={{0,2},{2,0},{4,6},{6,4},{8,10},{10,8},{12,14},{14,12},{16,18},{18,... | collective-permute-start | bytes 442376 | tf_op jit(solution)/shard_map/ppermute | solution.py:413
  65.6 7.3 %collective-permute-start.29 = (bf16[144,512]{1,0:T(8,128)(2,1)S(1)}, bf16[144,512]{1,0:T(8,128)(2,1)S(1)}, u32[]{:S(2)}, u32[]{:S(2)}) collective-permute-start(bf16[144,512]{1,0:T(8,128)(2,1)S(1)} %collective-permute-done.25.refs_2_), channel_id=1, source_target_pairs={{0,2},{2,0},{4,6},{6,4},{8,10},{10,8},{12,14},{14,12},{16,18},{18,... | collective-permute-start | bytes 442376 | tf_op jit(solution)/shard_map/ppermute | solution.py:413
  75.4 8.8 %collective-permute-start.31 = (bf16[128,1024]{1,0:T(8,128)(2,1)S(1)}, bf16[128,1024]{1,0:T(8,128)(2,1)S(1)}, u32[]{:S(2)}, u32[]{:S(2)}) collective-permute-start(bf16[128,1024]{1,0:T(8,128)(2,1)S(1)} %get-tuple-element.72), channel_id=1, source_target_pairs={{0,1},{1,0},{2,3},{3,2},{4,5},{5,4},{6,7},{7,6},{8,9},{9,8},{10,11... | collective-permute-start | bytes 786440 | tf_op jit(solution)/shard_map/ppermute | solution.py:512
  85.6 10.3 %collective-permute-start.32 = (bf16[144,512]{1,0:T(8,128)(2,1)S(1)}, bf16[144,512]{1,0:T(8,128)(2,1)S(1)}, u32[]{:S(2)}, u32[]{:S(2)}) collective-permute-start(bf16[144,512]{1,0:T(8,128)(2,1)S(1)} %get-tuple-element.73.refs_0_.packed_ref), channel_id=1, source_target_pairs={{0,8},{2,10},{4,12},{6,14},{8,0},{10,2},{12,4},{14,6},{16,24},{18,... | collective-permute-start | bytes 442376 | tf_op jit(solution)/shard_map/ppermute | solution.py:431
  88.5 9.0 %collective-permute-start.37 = (bf16[144,512]{1,0:T(8,128)(2,1)S(1)}, bf16[144,512]{1,0:T(8,128)(2,1)S(1)}, u32[]{:S(2)}, u32[]{:S(2)}) collective-permute-start(bf16[144,512]{1,0:T(8,128)(2,1)S(1)} %get-tuple-element.73.refs_0_.packed_ref), channel_id=1, source_target_pairs={{0,2},{2,0},{4,6},{6,4},{8,10},{10,8},{12,14},{14,12},{16,18},{18,... | collective-permute-start | bytes 442376 | tf_op jit(solution)/shard_map/ppermute | solution.py:413
  100.1 8.8 %collective-permute-start.41 = (bf16[128,1024]{1,0:T(8,128)(2,1)S(1)}, bf16[128,1024]{1,0:T(8,128)(2,1)S(1)}, u32[]{:S(2)}, u32[]{:S(2)}) collective-permute-start(bf16[128,1024]{1,0:T(8,128)(2,1)S(1)} %get-tuple-element.77), channel_id=1, source_target_pairs={{0,1},{1,0},{2,3},{3,2},{4,5},{5,4},{6,7},{7,6},{8,9},{9,8},{10,11... | collective-permute-start | bytes 786440 | tf_op jit(solution)/shard_map/ppermute | solution.py:512
  110.3 10.3 %collective-permute-start.42 = (bf16[144,512]{1,0:T(8,128)(2,1)S(1)}, bf16[144,512]{1,0:T(8,128)(2,1)S(1)}, u32[]{:S(2)}, u32[]{:S(2)}) collective-permute-start(bf16[144,512]{1,0:T(8,128)(2,1)S(1)} %get-tuple-element.78.refs_0_.packed_ref), channel_id=1, source_target_pairs={{0,8},{2,10},{4,12},{6,14},{8,0},{10,2},{12,4},{14,6},{16,24},{18,... | collective-permute-start | bytes 442376 | tf_op jit(solution)/shard_map/ppermute | solution.py:431
  113.2 9.0 %collective-permute-start.47 = (bf16[144,512]{1,0:T(8,128)(2,1)S(1)}, bf16[144,512]{1,0:T(8,128)(2,1)S(1)}, u32[]{:S(2)}, u32[]{:S(2)}) collective-permute-start(bf16[144,512]{1,0:T(8,128)(2,1)S(1)} %get-tuple-element.78.refs_0_.packed_ref), channel_id=1, source_target_pairs={{0,2},{2,0},{4,6},{6,4},{8,10},{10,8},{12,14},{14,12},{16,18},{18,... | collective-permute-start | bytes 442376 | tf_op jit(solution)/shard_map/ppermute | solution.py:413
  (31 other events, 162.2 us)

commit v4 on v3

--- a/solution.py
+++ b/solution.py
@@ -121,38 +121,56 @@
     return [pl.ds(pl.multiple_of(((me + k) % tps) * cols, HD), cols) for k in range(tps)]
 
 
-def prep_body(cot_in, state_in, gain_in, wq_in, wk_in, wv_in, wo_in, *refs):
-    cot_low, outs, cot_ref, sems = refs[0], refs[1:7], refs[7], refs[8]
-    sources = [state_in, gain_in, wq_in, wk_in, wv_in, wo_in]
-    copies = [pltpu.make_async_copy(cot_in, cot_ref, sems.at[0])]
-    for i, (src, dst) in enumerate(zip(sources, outs)):
-        copies.append(pltpu.make_async_copy(src, dst, sems.at[i + 1]))
+def round_body(x_ref, o_ref):
+    o_ref[...] = x_ref[...].astype(o_ref.dtype)
+
+
+def prep_body(*refs):
+    count = len(refs) // 2
+    sources, outs, sems = refs[:count], refs[count : 2 * count], refs[-1]
+    copies = [
+        pltpu.make_async_copy(src, dst, sems.at[i])
+        for i, (src, dst) in enumerate(zip(sources, outs))
+    ]
     for c in copies:
         c.start()
-    copies[0].wait()
-    cot_low[...] = cot_ref[...].astype(BF16)
-    for c in copies[1:]:
+    for c in copies:
         c.wait()
 
 
-def kv_body(blocks, tps, *refs):
-    xs = refs[: blocks * tps]
-    gain_ref, wk_ref, wv_ref, kv_ref, normed_ref, inv_ref = refs[blocks * tps :]
-    rows, cols = xs[0].shape
+def norm_block(xs, gain_ref, at):
+    total = jnp.zeros((xs[0].shape[0], 1), F32)
+    vals = [x[...].astype(F32) for x in xs]
+    for x in vals:
+        total = total + jnp.sum(x * x, axis=1, keepdims=True)
+    inverse = lax.rsqrt(total / (len(xs) * xs[0].shape[1]) + EPSILON)
+    return inverse, [(x * inverse * gain_ref[:, sl]).astype(BF16) for x, sl in zip(vals, at)]
+
+
+def norm_body(tps, *refs):
+    xs = refs[:tps]
+    gain_ref, normed_ref, inv_ref = refs[tps:]
+    at = feature_slices(tps, xs[0].shape[1])
+    inverse, pieces = norm_block(xs, gain_ref, at)
+    inv_ref[...] = jnp.broadcast_to(inverse, inv_ref.shape)
+    for sl, piece in zip(at, pieces):
+        normed_ref[:, sl] = piece
+
+
+def kv_body(raw, done, tps, *refs):
+    xs = refs[: raw * tps]
+    full = refs[raw * tps : raw * tps + done]
+    gain_ref, wk_ref, wv_ref, kv_ref, normed_ref = refs[raw * tps + done :]
+    rows = full[0].shape[0]
     width = wk_ref.shape[1]
-    at = feature_slices(tps, cols)
-    for b in range(blocks):
-        vals = [x[...].astype(F32) for x in xs[b * tps : (b + 1) * tps]]
-        total = jnp.zeros((rows, 1), F32)
-        for x in vals:
-            total = total + jnp.sum(x * x, axis=1, keepdims=True)
-        inverse = lax.rsqrt(total / (tps * cols) + EPSILON)
-        if b == 0:
-            inv_ref[...] = jnp.broadcast_to(inverse, inv_ref.shape)
-        for x, sl in zip(vals, at):
-            normed_ref[b * rows : (b + 1) * rows, sl] = (x * inverse * gain_ref[:, sl]).astype(
-                BF16
-            )
+    at = feature_slices(tps, full[0].shape[1] // tps)
+    for b in range(raw):
+        _, pieces = norm_block(xs[b * tps : (b + 1) * tps], gain_ref, at)
+        for sl, piece in zip(at, pieces):
+            normed_ref[(b + 1) * rows : (b + 2) * rows, sl] = piece
+    for i, x in enumerate(full):
+        b = i if i == 0 else i + raw
+        normed_ref[b * rows : (b + 1) * rows, :] = x[...]
     x = normed_ref[...]
     kv_ref[:, :width] = mm(x, wk_ref[...]).astype(BF16)
     kv_ref[:, width:] = mm(x, wv_ref[...]).astype(BF16)
@@ -336,10 +354,11 @@
             for a in range(SSTEP):
                 acc[i] = acc[i] + ds[a] * ks[0]
                 i += 1
-    sub = lax.broadcasted_iota(jnp.int32, (PAD, HD), 0)
-    out = jnp.zeros((PAD, HD), F32)
+    lane = lax.broadcasted_iota(jnp.int32, (1, HD), 1)
+    out = jnp.zeros((1, HD), F32)
     for i in range(count):
-        out = jnp.where(sub == i, jnp.sum(acc[i], axis=0, keepdims=True), out)
+        line = jnp.sum(acc[i], axis=0, keepdims=True)
+        out = jnp.where(lane == i, jnp.sum(line, axis=1, keepdims=True), out)
     for r in range(sums_ref.shape[0]):
         sums_ref[r] = out
 
@@ -372,14 +391,18 @@
     kry = refs[: SSTEP + 1]
     adj_ref, res_ref = refs[SSTEP + 1 :]
     total = jnp.sum(sums_ref[...], axis=0)
-    vals = jnp.sum(total, axis=1, keepdims=True)
+    lane = lax.broadcasted_iota(jnp.int32, total.shape, 1)
+    count = SSTEP * (SSTEP + 1) // 2 + SSTEP
+    vals = [
+        jnp.sum(jnp.where(lane == i, total, 0.0), axis=1, keepdims=True) for i in range(count)
+    ]
     idx = 0
     gram = [[None] * SSTEP for _ in range(SSTEP)]
     for a in range(SSTEP):
         for b in range(a + 1):
-            gram[a][b] = vals[idx : idx + 1, :]
+            gram[a][b] = vals[idx]
             idx += 1
-    right = [vals[idx + a : idx + a + 1, :] for a in range(SSTEP)]
+    right = [vals[idx + a] for a in range(SSTEP)]
     coef = solve(gram, right)
     ks = [k[...] for k in kry]
     adj = coef[0] * ks[0]
@@ -418,42 +441,50 @@
             out.append(lax.ppermute(x, "tp", [((i + k) % tps, i) for i in range(tps)]))
         return out
 
+    def hop(x, i):
+        d, odd = hops[i]
+        pairs = []
+        for c in range(chips):
+            q = swap_partner(c, d, odd)
+            if 0 <= q < chips:
+                pairs += [(2 * c, 2 * q), (2 * c + 1, 2 * q + 1)]
+            else:
+                pairs += [(2 * c, 2 * c + 1), (2 * c + 1, 2 * c)]
+        return lax.ppermute(x, "seq", pairs)
+
     def fetch(x):
-        got = [x]
-        for d, odd in hops:
-            pairs = []
-            for c in range(chips):
-                q = swap_partner(c, d, odd)
-                if 0 <= q < chips:
-                    pairs += [(2 * c, 2 * q), (2 * c + 1, 2 * q + 1)]
-                else:
-                    pairs += [(2 * c, 2 * c + 1), (2 * c + 1, 2 * c)]
-            got.append(lax.ppermute(x, "seq", pairs))
-        return got
-
-    raw = fetch(state)
-    cot_low, state_v, gain, w_query, w_key, w_value, w_out = kernel_call(
+        return [x] + [hop(x, i) for i in range(len(hops))]
+
+    raw = len(hops) // 2
+    states = tp_blocks(state)
+    pieces = []
+    for i in range(raw):
+        pieces += tp_blocks(hop(state, i))
+    gain = norm_gain[None, :]
+    normed, inv = kernel_call(
+        functools.partial(norm_body, tps),
+        [sds(rows, full, dtype=BF16), sds(rows, HD)],
+        states + [gain],
+    )
+    done = [normed] + [hop(normed, i) for i in range(raw, len(hops))]
+    (cot_low,) = kernel_call(round_body, [sds(rows, cols, dtype=BF16)], [cotangent])
+    held = [w_query, w_key, w_value, w_out]
+    w_query, w_key, w_value, w_out = kernel_call(
         prep_body,
-        [sds(rows, cols, dtype=BF16), state, sds(1, full)]
-        + [w_query, w_key, w_value, w_out],
-        [cotangent, state, norm_gain[None, :], w_query, w_key, w_value, w_out],
-        scratch=[pltpu.VMEM((rows, cols), F32), pltpu.SemaphoreType.DMA((7,))],
-        hbm=7,
+        held,
+        held,
+        scratch=[pltpu.SemaphoreType.DMA((len(held),))],
+        hbm=len(held),
         limit=49 << 20,
     )
-    pieces = []
-    for x in raw:
-        pieces += tp_blocks(x)
-    pieces[0] = state_v
     cots = tp_blocks(cot_low)
-    kv_mine, normed, inv = kernel_call(
-        functools.partial(kv_body, blocks, tps),
+    kv_mine, normed = kernel_call(
+        functools.partial(kv_body, raw, len(done), tps),
         [
             sds(blocks * rows, 2 * width, dtype=BF16),
             sds(blocks * rows, full, dtype=BF16),
-            sds(rows, HD),
         ],
-        pieces + [gain, w_key, w_value],
+        pieces + done + [gain, w_key, w_value],
     )
     kv_other = swap_core(kv_mine)
     q_mine, go0 = kernel_call(
@@ -525,7 +556,7 @@
         else:
             kry, sums = kernel_call(
                 gram_body,
-                [sds(rows, cols), sds(ranks, PAD, HD)],
+                [sds(rows, cols), sds(ranks, 1, HD)],
                 [part, recv, inv, gain] + krylov,
                 scratch=[pltpu.VMEM((rows, full), F32)],
             )

time: 148 us -> 140 us (0.946)
  blocking collectives: 15.2 us -> 10.8 us
  starting transfers between devices: 36.9 us -> 33.7 us
    all_to_all x1, blocking collectives: 15.2 us -> 10.8 us  [on_device(): sums = lax.all_to_all(sums, ('seq', 'tp'), 0, 0)]
    ppermute x20, starting transfers between devices: 21 us -> 18.3 us  [hop(): return lax.ppermute(x, 'seq', pairs)]
    ppermute x6 -> x4, waiting for transfers between devices: 8.06 us -> 9.97 us  [tp_blocks(): out.append(lax.ppermute(x, 'tp', [((i + k) % tps, i) for i in range(tps)]))]
    ppermute x6 -> x4, starting transfers between devices: 7.1 us -> 6.61 us  [tp_blocks(): out.append(lax.ppermute(x, 'tp', [((i + k) % tps, i) for i in range(tps)]))]
    pallas_call x22 -> x24, Pallas kernels: 29.6 us -> 29.3 us  [kernel_call(): pl.pallas_call(body, out_shape=[jax.ShapeDtypeStruct(o.shape, o.dtype) fo...]
  transfers between devices with their start and end apart: 52 -> 50, of which waited for: 17 -> 16; matrix products, arithmetic and copies ran while one was open for 0% -> 0% of each run, Pallas kernels for 13% -> 14%
where the time goes in v4:
time: 140 us
  waiting for transfers between devices  63.1 us (45%)
  starting transfers between devices  33.7 us (24%)
  Pallas kernels  29.3 us (21%)
  blocking collectives  10.8 us (8%)
  local copies, waits for them, and re-layouts  1.6 us (1%)
    pallas_call x24, Pallas kernels, kernel_call(): pl.pallas_call(body, out_shape=[jax.ShapeDtypeStruct(o.shape, o.dtype) fo...  29.3 us
    ppermute x20, waiting for transfers between devices, hop(): return lax.ppermute(x, 'seq', pairs)  27.1 us
    ppermute x4, waiting for transfers between devices, on_device(): recv = lax.ppermute(send, 'tp', [(i, i ^ k) for i in range(tps)])  26.1 us
    ppermute x20, starting transfers between devices, hop(): return lax.ppermute(x, 'seq', pairs)  18.3 us
    all_to_all x1, blocking collectives, on_device(): sums = lax.all_to_all(sums, ('seq', 'tp'), 0, 0)  10.8 us
    ppermute x4, waiting for transfers between devices, tp_blocks(): out.append(lax.ppermute(x, 'tp', [((i + k) % tps, i) for i in range(tps)]))  9.97 us
    ppermute x4, starting transfers between devices, tp_blocks(): out.append(lax.ppermute(x, 'tp', [((i + k) % tps, i) for i in range(tps)]))  6.61 us
    ppermute x4, starting transfers between devices, on_device(): recv = lax.ppermute(send, 'tp', [(i, i ^ k) for i in range(tps)])  6.31 us
  transfers between devices with their start and end apart: 50, of which 16 were waited for; matrix products, arithmetic and copies ran while one was open for 0% of the time, Pallas kernels for 14%

profile of v4, /device:TPU:0, one launch (start us, length us, event | category | flops | bytes accessed | tf_op | source)
XLA Modules:
  0.0 139.6 jit_solution(7641594847431913108)
XLA Ops:
  0.6 3.0 %collective-permute-start.4 = (bf16[128,512]{1,0:T(8,128)(2,1)}, bf16[128,512]{1,0:T(8,128)(2,1)S(1)}, u32[]{:S(2)}, u32[]{:S(2)}) collective-permute-start(bf16[128,512]{1,0:T(8,128)(2,1)} %refs_0_.4), channel_id=1, source_target_pairs={{1,0},{0,1},{3,2},{2,3},{5,4},{4,5},{7,6},{6,7},{9,8},{8,9},{11,10... | collective-permute-start | bytes 393224 | tf_op jit(solution)/shard_map/ppermute | solution.py:441
  4.2 3.2 %collective-permute-done.4.refs_1_ = bf16[128,512]{1,0:T(8,128)(2,1)S(1)} collective-permute-done((bf16[128,512]{1,0:T(8,128)(2,1)}, bf16[128,512]{1,0:T(8,128)(2,1)S(1)}, u32[]{:S(2)}, u32[]{:S(2)}) %collective-permute-start.4) | collective-permute-done | bytes 131104 | tf_op jit(solution)/shard_map/ppermute | solution.py:441
  9.1 1.9 %collective-permute-start.6 = (bf16[128,1024]{1,0:T(8,128)(2,1)S(1)}, bf16[128,1024]{1,0:T(8,128)(2,1)S(1)}, u32[]{:S(2)}, u32[]{:S(2)}) collective-permute-start(bf16[128,1024]{1,0:T(8,128)(2,1)S(1)} %get-tuple-element.43.refs_4_), channel_id=1, source_target_pairs={{0,8},{2,10},{4,12},{6,14},{8,0},{10,2},{12,4},{14,6},{16,24},{18,... | collective-permute-start | bytes 786440 | tf_op jit(solution)/shard_map/ppermute | solution.py:453
  14.6 2.2 %shard_map.87 = (bf16[1024,512]{1,0:T(8,128)(2,1)S(1)}, bf16[1024,512]{1,0:T(8,128)(2,1)S(1)}, bf16[1024,512]{1,0:T(8,128)(2,1)S(1)}, bf16[512,1024]{1,0:T(8,128)(2,1)S(1)}) custom-call(bf16[1024,512]{1,0:T(8,128)(2,1)} %refs_0_.5, bf16[1024,512]{1,0:T(8,128)(2,1)} %refs_1_.1, bf16[1024,512]{1,0:T(8,128)(2,1)} %refs_2_.1, bf16[512,1024]{1,0:T(8,128)(2,1)} %refs_3_.1), custom_call_target="tpu_custom_call" | custom-call | flops 100000000 | bytes 8388608 | tf_op jit(solution)/shard_map/pallas_call | solution.py:37
  22.5 4.4 %collective-permute-done.8.refs_1_ = bf16[128,512]{1,0:T(8,128)(2,1)S(1)} collective-permute-done((bf16[128,512]{1,0:T(8,128)(2,1)S(1)}, bf16[128,512]{1,0:T(8,128)(2,1)S(1)}, u32[]{:S(2)}, u32[]{:S(2)}) %collective-permute-start.8) | collective-permute-done | bytes 131104 | tf_op jit(solution)/shard_map/ppermute | solution.py:441
  28.1 2.6 %shard_map.91 = (f32[4,128,1280]{2,1,0:T(8,128)S(1)}, f32[128,512]{1,0:T(8,128)S(1)}, bf16[144,512]{1,0:T(8,128)(2,1)S(1)}) custom-call(bf16[640,1024]{1,0:T(8,128)(2,1)S(1)} %get-tuple-element.46.kvm_ref.kv_ref.refs_9_.refs_3_, bf16[640,1024]{1,0:T(8,128)(2,1)S(1)} %collective-permute-done.7.kvo_ref, ...), custom_call_target="tpu_custom_call" | custom-call | flops 100000000 | bytes 6438912 | tf_op jit(solution)/shard_map/pallas_call | solution.py:37
  31.8 2.7 %collective-permute-start.9 = (bf16[144,512]{1,0:T(8,128)(2,1)S(1)}, bf16[144,512]{1,0:T(8,128)(2,1)S(1)}, u32[]{:S(2)}, u32[]{:S(2)}) collective-permute-start(bf16[144,512]{1,0:T(8,128)(2,1)S(1)} %get-tuple-element.52.refs_0_.packed_ref), channel_id=1, source_target_pairs={{0,8},{2,10},{4,12},{6,14},{8,0},{10,2},{12,4},{14,6},{16,24},{18,... | collective-permute-start | bytes 442376 | tf_op jit(solution)/shard_map/ppermute | solution.py:453
  34.5 3.6 %collective-permute-done.14.refs_3_ = bf16[144,512]{1,0:T(8,128)(2,1)S(1)} collective-permute-done((bf16[144,512]{1,0:T(8,128)(2,1)S(1)}, bf16[144,512]{1,0:T(8,128)(2,1)S(1)}, u32[]{:S(2)}, u32[]{:S(2)}) %collective-permute-start.14) | collective-permute-done | bytes 147488 | tf_op jit(solution)/shard_map/ppermute | solution.py:453
  38.7 3.1 %collective-permute-done.9.refs_0_ = bf16[144,512]{1,0:T(8,128)(2,1)S(1)} collective-permute-done((bf16[144,512]{1,0:T(8,128)(2,1)S(1)}, bf16[144,512]{1,0:T(8,128)(2,1)S(1)}, u32[]{:S(2)}, u32[]{:S(2)}) %collective-permute-start.9) | collective-permute-done | bytes 147488 | tf_op jit(solution)/shard_map/ppermute | solution.py:453
  48.3 7.2 %collective-permute-done.19.recv_ref = bf16[128,1024]{1,0:T(8,128)(2,1)S(1)} collective-permute-done((bf16[128,1024]{1,0:T(8,128)(2,1)S(1)}, bf16[128,1024]{1,0:T(8,128)(2,1)S(1)}, u32[]{:S(2)}, u32[]{:S(2)}) %collective-permute-start.19) | collective-permute-done | bytes 262176 | tf_op jit(solution)/shard_map/ppermute | solution.py:543
  57.4 2.4 %collective-permute-start.20 = (bf16[144,512]{1,0:T(8,128)(2,1)S(1)}, bf16[144,512]{1,0:T(8,128)(2,1)S(1)}, u32[]{:S(2)}, u32[]{:S(2)}) collective-permute-start(bf16[144,512]{1,0:T(8,128)(2,1)S(1)} %get-tuple-element.62.refs_0_.packed_ref), channel_id=1, source_target_pairs={{0,8},{2,10},{4,12},{6,14},{8,0},{10,2},{12,4},{14,6},{16,24},{18,... | collective-permute-start | bytes 442376 | tf_op jit(solution)/shard_map/ppermute | solution.py:453
  59.8 1.9 %collective-permute-done.24.refs_3_ = bf16[144,512]{1,0:T(8,128)(2,1)S(1)} collective-permute-done((bf16[144,512]{1,0:T(8,128)(2,1)S(1)}, bf16[144,512]{1,0:T(8,128)(2,1)S(1)}, u32[]{:S(2)}, u32[]{:S(2)}) %collective-permute-start.24) | collective-permute-done | bytes 147488 | tf_op jit(solution)/shard_map/ppermute | solution.py:453
  62.3 4.9 %collective-permute-done.20.refs_0_ = bf16[144,512]{1,0:T(8,128)(2,1)S(1)} collective-permute-done((bf16[144,512]{1,0:T(8,128)(2,1)S(1)}, bf16[144,512]{1,0:T(8,128)(2,1)S(1)}, u32[]{:S(2)}, u32[]{:S(2)}) %collective-permute-start.20) | collective-permute-done | bytes 147488 | tf_op jit(solution)/shard_map/ppermute | solution.py:453
  67.2 1.8 %shard_map.98.refs_10_ = f32[128,1024]{1,0:T(8,128)S(1)} custom-call(bf16[144,512]{1,0:T(8,128)(2,1)S(1)} %get-tuple-element.62.refs_0_.packed_ref, f32[128,512]{1,0:T(8,128)S(1)} %get-tuple-element.57.att_ref, f32[4,128,1280]{2,1,0:T(8,128)S(1)} %get-tuple-element.58.p_ref, bf16[640,1024]{1,0:T(8,128)(2,1)S(1)} %get-tuple-element.46.kvm_ref.kv_ref.refs_9_.refs_3_, ...), custom_call_target="tpu_custom_call" | custom-call | flops 100000000 | bytes 7225344 | tf_op jit(solution)/shard_map/pallas_call | solution.py:37
  73.2 7.2 %collective-permute-done.29.recv_ref = bf16[128,1024]{1,0:T(8,128)(2,1)S(1)} collective-permute-done((bf16[128,1024]{1,0:T(8,128)(2,1)S(1)}, bf16[128,1024]{1,0:T(8,128)(2,1)S(1)}, u32[]{:S(2)}, u32[]{:S(2)}) %collective-permute-start.29) | collective-permute-done | bytes 262176 | tf_op jit(solution)/shard_map/ppermute | solution.py:543
  81.9 2.9 %collective-permute-start.30 = (bf16[144,512]{1,0:T(8,128)(2,1)S(1)}, bf16[144,512]{1,0:T(8,128)(2,1)S(1)}, u32[]{:S(2)}, u32[]{:S(2)}) collective-permute-start(bf16[144,512]{1,0:T(8,128)(2,1)S(1)} %get-tuple-element.69.refs_0_.packed_ref), channel_id=1, source_target_pairs={{0,8},{2,10},{4,12},{6,14},{8,0},{10,2},{12,4},{14,6},{16,24},{18,... | collective-permute-start | bytes 442376 | tf_op jit(solution)/shard_map/ppermute | solution.py:453
  84.8 1.9 %collective-permute-done.34.refs_3_ = bf16[144,512]{1,0:T(8,128)(2,1)S(1)} collective-permute-done((bf16[144,512]{1,0:T(8,128)(2,1)S(1)}, bf16[144,512]{1,0:T(8,128)(2,1)S(1)}, u32[]{:S(2)}, u32[]{:S(2)}) %collective-permute-start.34) | collective-permute-done | bytes 147488 | tf_op jit(solution)/shard_map/ppermute | solution.py:453
  87.3 4.9 %collective-permute-done.30.refs_0_ = bf16[144,512]{1,0:T(8,128)(2,1)S(1)} collective-permute-done((bf16[144,512]{1,0:T(8,128)(2,1)S(1)}, bf16[144,512]{1,0:T(8,128)(2,1)S(1)}, u32[]{:S(2)}, u32[]{:S(2)}) %collective-permute-start.30) | collective-permute-done | bytes 147488 | tf_op jit(solution)/shard_map/ppermute | solution.py:453
  98.0 7.2 %collective-permute-done.39.recv_ref = bf16[128,1024]{1,0:T(8,128)(2,1)S(1)} collective-permute-done((bf16[128,1024]{1,0:T(8,128)(2,1)S(1)}, bf16[128,1024]{1,0:T(8,128)(2,1)S(1)}, u32[]{:S(2)}, u32[]{:S(2)}) %collective-permute-start.39) | collective-permute-done | bytes 262176 | tf_op jit(solution)/shard_map/ppermute | solution.py:543
  106.6 2.9 %collective-permute-start.40 = (bf16[144,512]{1,0:T(8,128)(2,1)S(1)}, bf16[144,512]{1,0:T(8,128)(2,1)S(1)}, u32[]{:S(2)}, u32[]{:S(2)}) collective-permute-start(bf16[144,512]{1,0:T(8,128)(2,1)S(1)} %get-tuple-element.74.refs_0_.packed_ref), channel_id=1, source_target_pairs={{0,8},{2,10},{4,12},{6,14},{8,0},{10,2},{12,4},{14,6},{16,24},{18,... | collective-permute-start | bytes 442376 | tf_op jit(solution)/shard_map/ppermute | solution.py:453
  109.5 1.9 %collective-permute-done.44.refs_3_ = bf16[144,512]{1,0:T(8,128)(2,1)S(1)} collective-permute-done((bf16[144,512]{1,0:T(8,128)(2,1)S(1)}, bf16[144,512]{1,0:T(8,128)(2,1)S(1)}, u32[]{:S(2)}, u32[]{:S(2)}) %collective-permute-start.44) | collective-permute-done | bytes 147488 | tf_op jit(solution)/shard_map/ppermute | solution.py:453
  112.0 4.9 %collective-permute-done.40.refs_0_ = bf16[144,512]{1,0:T(8,128)(2,1)S(1)} collective-permute-done((bf16[144,512]{1,0:T(8,128)(2,1)S(1)}, bf16[144,512]{1,0:T(8,128)(2,1)S(1)}, u32[]{:S(2)}, u32[]{:S(2)}) %collective-permute-start.40) | collective-permute-done | bytes 147488 | tf_op jit(solution)/shard_map/ppermute | solution.py:453
  122.8 4.4 %collective-permute-done.49.recv_ref = bf16[128,512]{1,0:T(8,128)(2,1)S(1)} collective-permute-done((bf16[128,512]{1,0:T(8,128)(2,1)S(1)}, bf16[128,512]{1,0:T(8,128)(2,1)S(1)}, u32[]{:S(2)}, u32[]{:S(2)}) %collective-permute-start.49) | collective-permute-done | bytes 131104 | tf_op jit(solution)/shard_map/ppermute | solution.py:543
  127.6 10.8 %all_to_all.5.sums_ref = f32[32,1,128]{2,1,0:T(1,128)S(1)} all-to-all(f32[32,1,128]{2,1,0:T(1,128)S(1)} %get-tuple-element.82), channel_id=1, replica_groups=mesh['seq'=16,'tp'=2] {'seq','tp'}, dimensions={0} | all-to-all | bytes 32768 | tf_op jit(solution)/shard_map/all_to_all | solution.py:564
  (109 shorter events, 44.7 us)
Async XLA Ops:
  3.7 8.9 %collective-permute-start.2 = (bf16[128,512]{1,0:T(8,128)(2,1)}, bf16[128,512]{1,0:T(8,128)(2,1)S(1)}, u32[]{:S(2)}, u32[]{:S(2)}) collective-permute-start(bf16[128,512]{1,0:T(8,128)(2,1)} %refs_0_.4), channel_id=1, source_target_pairs={{0,2},{2,0},{4,6},{6,4},{8,16},{10,18},{12,20},{14,22},{16,8},{18,... | collective-permute-start | bytes 393224 | tf_op jit(solution)/shard_map/ppermute | solution.py:453
  3.7 10.4 %collective-permute-start = (bf16[128,512]{1,0:T(8,128)(2,1)}, bf16[128,512]{1,0:T(8,128)(2,1)S(1)}, u32[]{:S(2)}, u32[]{:S(2)}) collective-permute-start(bf16[128,512]{1,0:T(8,128)(2,1)} %refs_0_.4), channel_id=1, source_target_pairs={{0,2},{2,0},{4,8},{6,10},{8,4},{10,6},{12,16},{14,18},{16,12},{18,... | collective-permute-start | bytes 393224 | tf_op jit(solution)/shard_map/ppermute | solution.py:453
  9.1 10.0 %collective-permute-start.6 = (bf16[128,1024]{1,0:T(8,128)(2,1)S(1)}, bf16[128,1024]{1,0:T(8,128)(2,1)S(1)}, u32[]{:S(2)}, u32[]{:S(2)}) collective-permute-start(bf16[128,1024]{1,0:T(8,128)(2,1)S(1)} %get-tuple-element.43.refs_4_), channel_id=1, source_target_pairs={{0,8},{2,10},{4,12},{6,14},{8,0},{10,2},{12,4},{14,6},{16,24},{18,... | collective-permute-start | bytes 786440 | tf_op jit(solution)/shard_map/ppermute | solution.py:453
  11.0 8.2 %collective-permute-start.5 = (bf16[128,1024]{1,0:T(8,128)(2,1)S(1)}, bf16[128,1024]{1,0:T(8,128)(2,1)S(1)}, u32[]{:S(2)}, u32[]{:S(2)}) collective-permute-start(bf16[128,1024]{1,0:T(8,128)(2,1)S(1)} %get-tuple-element.43.refs_4_), channel_id=1, source_target_pairs={{0,4},{2,6},{4,0},{6,2},{8,12},{10,14},{12,8},{14,10},{16,20},{18,... | collective-permute-start | bytes 786440 | tf_op jit(solution)/shard_map/ppermute | solution.py:453
  20.8 7.3 %collective-permute-start.7 = (bf16[640,1024]{1,0:T(8,128)(2,1)S(1)}, bf16[640,1024]{1,0:T(8,128)(2,1)S(1)}, u32[]{:S(2)}, u32[]{:S(2)}) collective-permute-start(bf16[640,1024]{1,0:T(8,128)(2,1)S(1)} %get-tuple-element.46.kvm_ref.kv_ref.refs_9_.refs_3_), channel_id=1, source_target_pairs={{0,2},{2,0},{4,6},{6,4},{8,10},{10,8},{12,14},{14,12},{16,18},{18,... | collective-permute-start | bytes 3932168 | tf_op jit(solution)/shard_map/ppermute | solution.py:436
  30.7 7.4 %collective-permute-start.14 = (bf16[144,512]{1,0:T(8,128)(2,1)S(1)}, bf16[144,512]{1,0:T(8,128)(2,1)S(1)}, u32[]{:S(2)}, u32[]{:S(2)}) collective-permute-start(bf16[144,512]{1,0:T(8,128)(2,1)S(1)} %get-tuple-element.52.refs_0_.packed_ref), channel_id=1, source_target_pairs={{0,4},{2,6},{4,0},{6,2},{8,12},{10,14},{12,8},{14,10},{16,20},{18,... | collective-permute-start | bytes 442376 | tf_op jit(solution)/shard_map/ppermute | solution.py:453
  31.5 7.1 %collective-permute-start.12 = (bf16[144,512]{1,0:T(8,128)(2,1)S(1)}, bf16[144,512]{1,0:T(8,128)(2,1)S(1)}, u32[]{:S(2)}, u32[]{:S(2)}) collective-permute-start(bf16[144,512]{1,0:T(8,128)(2,1)S(1)} %get-tuple-element.52.refs_0_.packed_ref), channel_id=1, source_target_pairs={{0,2},{2,0},{4,8},{6,10},{8,4},{10,6},{12,16},{14,18},{16,12},{18,... | collective-permute-start | bytes 442376 | tf_op jit(solution)/shard_map/ppermute | solution.py:453
  31.8 9.9 %collective-permute-start.9 = (bf16[144,512]{1,0:T(8,128)(2,1)S(1)}, bf16[144,512]{1,0:T(8,128)(2,1)S(1)}, u32[]{:S(2)}, u32[]{:S(2)}) collective-permute-start(bf16[144,512]{1,0:T(8,128)(2,1)S(1)} %get-tuple-element.52.refs_0_.packed_ref), channel_id=1, source_target_pairs={{0,8},{2,10},{4,12},{6,14},{8,0},{10,2},{12,4},{14,6},{16,24},{18,... | collective-permute-start | bytes 442376 | tf_op jit(solution)/shard_map/ppermute | solution.py:453
  34.5 9.6 %collective-permute-start.15 = (bf16[144,512]{1,0:T(8,128)(2,1)S(1)}, bf16[144,512]{1,0:T(8,128)(2,1)S(1)}, u32[]{:S(2)}, u32[]{:S(2)}) collective-permute-start(bf16[144,512]{1,0:T(8,128)(2,1)S(1)} %get-tuple-element.52.refs_0_.packed_ref), channel_id=1, source_target_pairs={{0,2},{2,0},{4,6},{6,4},{8,10},{10,8},{12,14},{14,12},{16,18},{18,... | collective-permute-start | bytes 442376 | tf_op jit(solution)/shard_map/ppermute | solution.py:436
  46.7 8.8 %collective-permute-start.19 = (bf16[128,1024]{1,0:T(8,128)(2,1)S(1)}, bf16[128,1024]{1,0:T(8,128)(2,1)S(1)}, u32[]{:S(2)}, u32[]{:S(2)}) collective-permute-start(bf16[128,1024]{1,0:T(8,128)(2,1)S(1)} %get-tuple-element.60), channel_id=1, source_target_pairs={{0,1},{1,0},{2,3},{3,2},{4,5},{5,4},{6,7},{7,6},{8,9},{9,8},{10,11... | collective-permute-start | bytes 786440 | tf_op jit(solution)/shard_map/ppermute | solution.py:543
  57.4 9.8 %collective-permute-start.20 = (bf16[144,512]{1,0:T(8,128)(2,1)S(1)}, bf16[144,512]{1,0:T(8,128)(2,1)S(1)}, u32[]{:S(2)}, u32[]{:S(2)}) collective-permute-start(bf16[144,512]{1,0:T(8,128)(2,1)S(1)} %get-tuple-element.62.refs_0_.packed_ref), channel_id=1, source_target_pairs={{0,8},{2,10},{4,12},{6,14},{8,0},{10,2},{12,4},{14,6},{16,24},{18,... | collective-permute-start | bytes 442376 | tf_op jit(solution)/shard_map/ppermute | solution.py:453
  59.8 9.2 %collective-permute-start.25 = (bf16[144,512]{1,0:T(8,128)(2,1)S(1)}, bf16[144,512]{1,0:T(8,128)(2,1)S(1)}, u32[]{:S(2)}, u32[]{:S(2)}) collective-permute-start(bf16[144,512]{1,0:T(8,128)(2,1)S(1)} %get-tuple-element.62.refs_0_.packed_ref), channel_id=1, source_target_pairs={{0,2},{2,0},{4,6},{6,4},{8,10},{10,8},{12,14},{14,12},{16,18},{18,... | collective-permute-start | bytes 442376 | tf_op jit(solution)/shard_map/ppermute | solution.py:436
  61.8 7.3 %collective-permute-start.28 = (bf16[144,512]{1,0:T(8,128)(2,1)S(1)}, bf16[144,512]{1,0:T(8,128)(2,1)S(1)}, u32[]{:S(2)}, u32[]{:S(2)}) collective-permute-start(bf16[144,512]{1,0:T(8,128)(2,1)S(1)} %collective-permute-done.24.refs_3_), channel_id=1, source_target_pairs={{0,2},{2,0},{4,6},{6,4},{8,10},{10,8},{12,14},{14,12},{16,18},{18,... | collective-permute-start | bytes 442376 | tf_op jit(solution)/shard_map/ppermute | solution.py:436
  61.8 7.3 %collective-permute-start.27 = (bf16[144,512]{1,0:T(8,128)(2,1)S(1)}, bf16[144,512]{1,0:T(8,128)(2,1)S(1)}, u32[]{:S(2)}, u32[]{:S(2)}) collective-permute-start(bf16[144,512]{1,0:T(8,128)(2,1)S(1)} %collective-permute-done.23.refs_2_), channel_id=1, source_target_pairs={{0,2},{2,0},{4,6},{6,4},{8,10},{10,8},{12,14},{14,12},{16,18},{18,... | collective-permute-start | bytes 442376 | tf_op jit(solution)/shard_map/ppermute | solution.py:436
  71.7 8.8 %collective-permute-start.29 = (bf16[128,1024]{1,0:T(8,128)(2,1)S(1)}, bf16[128,1024]{1,0:T(8,128)(2,1)S(1)}, u32[]{:S(2)}, u32[]{:S(2)}) collective-permute-start(bf16[128,1024]{1,0:T(8,128)(2,1)S(1)} %get-tuple-element.68), channel_id=1, source_target_pairs={{0,1},{1,0},{2,3},{3,2},{4,5},{5,4},{6,7},{7,6},{8,9},{9,8},{10,11... | collective-permute-start | bytes 786440 | tf_op jit(solution)/shard_map/ppermute | solution.py:543
  81.9 10.3 %collective-permute-start.30 = (bf16[144,512]{1,0:T(8,128)(2,1)S(1)}, bf16[144,512]{1,0:T(8,128)(2,1)S(1)}, u32[]{:S(2)}, u32[]{:S(2)}) collective-permute-start(bf16[144,512]{1,0:T(8,128)(2,1)S(1)} %get-tuple-element.69.refs_0_.packed_ref), channel_id=1, source_target_pairs={{0,8},{2,10},{4,12},{6,14},{8,0},{10,2},{12,4},{14,6},{16,24},{18,... | collective-permute-start | bytes 442376 | tf_op jit(solution)/shard_map/ppermute | solution.py:453
  84.8 9.0 %collective-permute-start.35 = (bf16[144,512]{1,0:T(8,128)(2,1)S(1)}, bf16[144,512]{1,0:T(8,128)(2,1)S(1)}, u32[]{:S(2)}, u32[]{:S(2)}) collective-permute-start(bf16[144,512]{1,0:T(8,128)(2,1)S(1)} %get-tuple-element.69.refs_0_.packed_ref), channel_id=1, source_target_pairs={{0,2},{2,0},{4,6},{6,4},{8,10},{10,8},{12,14},{14,12},{16,18},{18,... | collective-permute-start | bytes 442376 | tf_op jit(solution)/shard_map/ppermute | solution.py:436
  86.7 7.1 %collective-permute-start.38 = (bf16[144,512]{1,0:T(8,128)(2,1)S(1)}, bf16[144,512]{1,0:T(8,128)(2,1)S(1)}, u32[]{:S(2)}, u32[]{:S(2)}) collective-permute-start(bf16[144,512]{1,0:T(8,128)(2,1)S(1)} %collective-permute-done.34.refs_3_), channel_id=1, source_target_pairs={{0,2},{2,0},{4,6},{6,4},{8,10},{10,8},{12,14},{14,12},{16,18},{18,... | collective-permute-start | bytes 442376 | tf_op jit(solution)/shard_map/ppermute | solution.py:436
  86.7 7.1 %collective-permute-start.37 = (bf16[144,512]{1,0:T(8,128)(2,1)S(1)}, bf16[144,512]{1,0:T(8,128)(2,1)S(1)}, u32[]{:S(2)}, u32[]{:S(2)}) collective-permute-start(bf16[144,512]{1,0:T(8,128)(2,1)S(1)} %collective-permute-done.33.refs_2_), channel_id=1, source_target_pairs={{0,2},{2,0},{4,6},{6,4},{8,10},{10,8},{12,14},{14,12},{16,18},{18,... | collective-permute-start | bytes 442376 | tf_op jit(solution)/shard_map/ppermute | solution.py:436
  96.4 8.8 %collective-permute-start.39 = (bf16[128,1024]{1,0:T(8,128)(2,1)S(1)}, bf16[128,1024]{1,0:T(8,128)(2,1)S(1)}, u32[]{:S(2)}, u32[]{:S(2)}) collective-permute-start(bf16[128,1024]{1,0:T(8,128)(2,1)S(1)} %get-tuple-element.73), channel_id=1, source_target_pairs={{0,1},{1,0},{2,3},{3,2},{4,5},{5,4},{6,7},{7,6},{8,9},{9,8},{10,11... | collective-permute-start | bytes 786440 | tf_op jit(solution)/shard_map/ppermute | solution.py:543
  106.6 10.3 %collective-permute-start.40 = (bf16[144,512]{1,0:T(8,128)(2,1)S(1)}, bf16[144,512]{1,0:T(8,128)(2,1)S(1)}, u32[]{:S(2)}, u32[]{:S(2)}) collective-permute-start(bf16[144,512]{1,0:T(8,128)(2,1)S(1)} %get-tuple-element.74.refs_0_.packed_ref), channel_id=1, source_target_pairs={{0,8},{2,10},{4,12},{6,14},{8,0},{10,2},{12,4},{14,6},{16,24},{18,... | collective-permute-start | bytes 442376 | tf_op jit(solution)/shard_map/ppermute | solution.py:453
  109.5 9.0 %collective-permute-start.45 = (bf16[144,512]{1,0:T(8,128)(2,1)S(1)}, bf16[144,512]{1,0:T(8,128)(2,1)S(1)}, u32[]{:S(2)}, u32[]{:S(2)}) collective-permute-start(bf16[144,512]{1,0:T(8,128)(2,1)S(1)} %get-tuple-element.74.refs_0_.packed_ref), channel_id=1, source_target_pairs={{0,2},{2,0},{4,6},{6,4},{8,10},{10,8},{12,14},{14,12},{16,18},{18,... | collective-permute-start | bytes 442376 | tf_op jit(solution)/shard_map/ppermute | solution.py:436
  111.4 7.1 %collective-permute-start.48 = (bf16[144,512]{1,0:T(8,128)(2,1)S(1)}, bf16[144,512]{1,0:T(8,128)(2,1)S(1)}, u32[]{:S(2)}, u32[]{:S(2)}) collective-permute-start(bf16[144,512]{1,0:T(8,128)(2,1)S(1)} %collective-permute-done.44.refs_3_), channel_id=1, source_target_pairs={{0,2},{2,0},{4,6},{6,4},{8,10},{10,8},{12,14},{14,12},{16,18},{18,... | collective-permute-start | bytes 442376 | tf_op jit(solution)/shard_map/ppermute | solution.py:436
  111.4 7.2 %collective-permute-start.47 = (bf16[144,512]{1,0:T(8,128)(2,1)S(1)}, bf16[144,512]{1,0:T(8,128)(2,1)S(1)}, u32[]{:S(2)}, u32[]{:S(2)}) collective-permute-start(bf16[144,512]{1,0:T(8,128)(2,1)S(1)} %collective-permute-done.43.refs_2_), channel_id=1, source_target_pairs={{0,2},{2,0},{4,6},{6,4},{8,10},{10,8},{12,14},{14,12},{16,18},{18,... | collective-permute-start | bytes 442376 | tf_op jit(solution)/shard_map/ppermute | solution.py:436
  (30 other events, 158.6 us)

commit v5 on v4

--- a/solution.py
+++ b/solution.py
@@ -121,8 +121,10 @@
     return [pl.ds(pl.multiple_of(((me + k) % tps) * cols, HD), cols) for k in range(tps)]
 
 
-def round_body(x_ref, o_ref):
-    o_ref[...] = x_ref[...].astype(o_ref.dtype)
+def early_body(cot_ref, state_ref, gain_ref, cot_out, state_out, gain_out):
+    cot_out[...] = cot_ref[...].astype(BF16)
+    state_out[...] = state_ref[...]
+    gain_out[...] = gain_ref[...]
 
 
 def prep_body(*refs):
@@ -176,61 +178,59 @@
     kv_ref[:, width:] = mm(x, wv_ref[...]).astype(BF16)
 
 
-def q_body(tps, *refs):
+def q_body(rows, normed_ref, wq_ref, kv_ref, q_ref, s_ref):
+    q_ref[...] = mm(normed_ref[...], wq_ref[...]).astype(BF16)
+    for h in range(s_ref.shape[0]):
+        s_ref[h] = mm(q_ref[:rows, col(h)], kv_ref[:, col(h)], NT) * SCALE
+
+
+def stats_body(half, tps, *refs):
     cots = refs[:tps]
-    normed_ref, wq_ref, wo_ref, q_ref, go_ref, cot_ref = refs[tps:]
-    q_ref[...] = mm(normed_ref[...], wq_ref[...]).astype(BF16)
-    for c, at in zip(cots, feature_slices(tps, cots[0].shape[1])):
-        cot_ref[:, at] = c[...]
-    go_ref[...] = mm(cot_ref[...], wo_ref[...], NT).astype(BF16)
-
-
-def stats_body(half, kvm_ref, kvo_ref, q_ref, go_ref, p_ref, att_ref, packed_ref):
-    rows, width = go_ref.shape
+    kvm_ref, kvo_ref, q_ref, s_ref, wo_ref, p_ref, att_ref, packed_ref, cot_ref = refs[tps:]
+    rows, width = att_ref.shape
     heads = width // HD
     near = kvm_ref.shape[0]
     masks = masks_of(half, rows)
-    packed_ref[:rows, :] = go_ref[...]
+    for c, at in zip(cots, feature_slices(tps, cots[0].shape[1])):
+        cot_ref[:, at] = c[...]
+    go = mm(cot_ref[...], wo_ref[...], NT).astype(BF16)
+    packed_ref[:rows, :] = go
     lse, corr = [], []
     for h in range(heads):
         q = q_ref[:rows, col(h)]
-        s = jnp.concatenate(
-            [mm(q, kvm_ref[:, col(h)], NT), mm(q, kvo_ref[:, col(h)], NT)], axis=1
-        )
-        s = masked(s * SCALE, masks)
+        s = jnp.concatenate([s_ref[h], mm(q, kvo_ref[:, col(h)], NT) * SCALE], axis=1)
+        s = masked(s, masks)
         peak = jnp.max(s, axis=1, keepdims=True)
         raw = jnp.exp(s - peak)
         total = jnp.sum(raw, axis=1, keepdims=True)
-        probs = raw / total
+        probs = raw * (1.0 / total)
         p_ref[h] = probs
         low = probs.astype(BF16)
         att = mm(low[:, :near], kvm_ref[:, col(heads + h)])
         att = att + mm(low[:, near:], kvo_ref[:, col(heads + h)])
         att_ref[:, col(h)] = att
         lse.append(peak + jnp.log(total))
-        corr.append(jnp.sum(go_ref[:, col(h)].astype(F32) * att, axis=1, keepdims=True))
+        corr.append(jnp.sum(go[:, col(h)].astype(F32) * att, axis=1, keepdims=True))
     pack_rows(packed_ref, rows, heads, corr + lse)
 
 
-def split_slots(blocks):
-    early = list(range(blocks - 1)) + list(range(blocks, 2 * blocks - 1))
-    return early, [blocks - 1, 2 * blocks - 1]
-
-
-def scores_t_body(half, qm_ref, qo_ref, kv_ref, early_ref, late_ref):
-    rows = early_ref.shape[1]
+def groups_of(blocks):
+    cut = 1 + (blocks - 1) // 2
+    return [(0, 1), (1, cut), (cut, blocks)]
+
+
+def scores_t_body(half, qm_ref, qo_ref, kv_ref, *outs):
+    rows = outs[0].shape[1]
     masks = masks_of(half, rows)
-    cut = qm_ref.shape[0] - rows
-    groups = split_slots(len(masks) // 2)
-    for h in range(early_ref.shape[0]):
+    blocks = len(masks) // 2
+    for h in range(outs[0].shape[0]):
         k = kv_ref[:rows, col(h)]
-        for ref, slots, part in zip(
-            (early_ref, late_ref), groups, (slice(0, cut), slice(cut, cut + rows))
-        ):
+        for ref, (lo, hi) in zip(outs, groups_of(blocks)):
+            part = slice(lo * rows, hi * rows)
             s = jnp.concatenate(
                 [mm(k, qm_ref[part, col(h)], NT), mm(k, qo_ref[part, col(h)], NT)], axis=1
             )
-            ref[h] = masked(s * SCALE, [masks[i] for i in slots])
+            ref[h] = masked(s * SCALE, masks[lo:hi] + masks[blocks + lo : blocks + hi])
 
 
 def query_body(packed_ref, att_ref, p_ref, kvm_ref, kvo_ref, wq_ref, part_ref):
@@ -265,33 +265,43 @@
     return gk, mm(pt.astype(BF16), go)
 
 
-def key_early_body(slots, first, *refs):
+def key_part_body(span, first, *refs):
+    lo, hi = span
+    slots = 2 * (hi - lo)
     got = refs[:slots]
     pt_in, kv_ref, qm_ref, qo_ref = refs[slots : slots + 4]
-    gk_ref, gv_ref = refs[slots + 4 : slots + 6]
-    pt_ref = refs[slots + 6] if first else None
-    gow_ref = refs[-1]
+    rest = list(refs[slots + 4 :])
+    gow_ref = rest.pop()
+    pt_ref = rest.pop() if first else None
+    gk_ref, gv_ref = rest[-2:]
+    before = rest[:-2]
     rows = got[0].shape[0] - PAD
     for b in range(slots):
         gow_ref[b * rows : (b + 1) * rows, :] = got[b][:rows, :]
-    part = slice(0, slots // 2 * rows)
+    part = slice(lo * rows, hi * rows)
     for h in range(pt_in.shape[0]):
         gk, gv = key_terms(got, part, first, pt_in, pt_ref, kv_ref, qm_ref, qo_ref, gow_ref, h)
+        if before:
+            gk = gk + before[0][:, col(h)]
+            gv = gv + before[1][:, col(h)]
         gk_ref[:, col(h)] = gk
         gv_ref[:, col(h)] = gv
 
 
-def key_late_body(first, halved, *refs):
-    got = refs[:2]
-    pt_in, kv_ref, qm_ref, qo_ref, gk_ref, gv_ref, wk_ref, wv_ref, partq_ref = refs[2:11]
-    part_ref, send_ref = refs[11:13]
-    pt_ref = refs[13] if first else None
+def key_last_body(span, first, halved, *refs):
+    lo, hi = span
+    slots = 2 * (hi - lo)
+    got = refs[:slots]
+    pt_in, kv_ref, qm_ref, qo_ref, gk_ref, gv_ref, wk_ref, wv_ref, partq_ref = refs[
+        slots : slots + 9
+    ]
+    part_ref, send_ref = refs[slots + 9 : slots + 11]
+    pt_ref = refs[slots + 11] if first else None
     gow_ref, sum_ref = refs[-2:]
     rows = got[0].shape[0] - PAD
-    for b in range(2):
+    for b in range(slots):
         gow_ref[b * rows : (b + 1) * rows, :] = got[b][:rows, :]
-    total = qm_ref.shape[0]
-    part = slice(total - rows, total)
+    part = slice(lo * rows, hi * rows)
     gks, gvs = [], []
     for h in range(pt_in.shape[0]):
         gk, gv = key_terms(got, part, first, pt_in, pt_ref, kv_ref, qm_ref, qo_ref, gow_ref, h)
@@ -428,7 +438,8 @@
     chips = seq // 2
     hops = hops_of(half, rows)
     blocks = 1 + len(hops)
-    early, late = split_slots(blocks)
+    groups = groups_of(blocks)
+    wide = [2 * (hi - lo) * rows for lo, hi in groups]
     ranks = seq * tps
     full = tps * cols
 
@@ -460,14 +471,17 @@
     pieces = []
     for i in range(raw):
         pieces += tp_blocks(hop(state, i))
-    gain = norm_gain[None, :]
+    cot_low, states[0], gain = kernel_call(
+        early_body,
+        [sds(rows, cols, dtype=BF16), state, sds(1, full)],
+        [cotangent, state, norm_gain[None, :]],
+    )
     normed, inv = kernel_call(
         functools.partial(norm_body, tps),
         [sds(rows, full, dtype=BF16), sds(rows, HD)],
         states + [gain],
     )
     done = [normed] + [hop(normed, i) for i in range(raw, len(hops))]
-    (cot_low,) = kernel_call(round_body, [sds(rows, cols, dtype=BF16)], [cotangent])
     held = [w_query, w_key, w_value, w_out]
     w_query, w_key, w_value, w_out = kernel_call(
         prep_body,
@@ -487,25 +501,25 @@
         pieces + done + [gain, w_key, w_value],
     )
     kv_other = swap_core(kv_mine)
-    q_mine, go0 = kernel_call(
-        functools.partial(q_body, tps),
-        [sds(blocks * rows, width, dtype=BF16), sds(rows, width, dtype=BF16)],
-        cots + [normed, w_query, w_out],
-        scratch=[pltpu.VMEM((rows, full), BF16)],
+    q_mine, s_mine = kernel_call(
+        functools.partial(q_body, rows),
+        [sds(blocks * rows, width, dtype=BF16), sds(heads, rows, blocks * rows)],
+        [normed, w_query, kv_mine],
     )
     q_other = swap_core(q_mine)
     probs, att, packed = kernel_call(
-        functools.partial(stats_body, half),
+        functools.partial(stats_body, half, tps),
         [sds(heads, rows, 2 * blocks * rows), sds(rows, width), sds(rows + PAD, width, dtype=BF16)],
-        [kv_mine, kv_other, q_mine, go0],
+        cots + [kv_mine, kv_other, q_mine, s_mine, w_out],
+        scratch=[pltpu.VMEM((rows, full), BF16)],
     )
     krylov = [cotangent]
     for n in range(SSTEP):
         first, last = n == 0, n == SSTEP - 1
         if first:
-            pt_early, pt_late = kernel_call(
+            pts = kernel_call(
                 functools.partial(scores_t_body, half),
-                [sds(heads, rows, len(early) * rows), sds(heads, rows, 2 * rows)],
+                [sds(heads, rows, w) for w in wide],
                 [q_mine, q_other, kv_mine],
             )
         got = fetch(packed)
@@ -515,29 +529,38 @@
             [sds(rows, full)],
             [packed, att, probs, kv_mine, kv_other, w_query],
         )
-        res = kernel_call(
-            functools.partial(key_early_body, len(early), first),
-            [sds(rows, width), sds(rows, width)]
-            + ([sds(heads, rows, len(early) * rows)] if first else []),
-            [got[i] for i in early] + [pt_early, kv_mine, q_mine, q_other],
-            scratch=[pltpu.VMEM((len(early) * rows, width), BF16)],
-        )
-        gk, gv = res[:2]
-        if first:
-            pt_early = res[2]
+        static = [kv_mine, q_mine, q_other]
+        grads = []
+        new_pts = []
+        for g in range(2):
+            lo, hi = groups[g]
+            res = kernel_call(
+                functools.partial(key_part_body, groups[g], first),
+                [sds(rows, width), sds(rows, width)]
+                + ([sds(heads, rows, wide[g])] if first else []),
+                got[lo:hi] + got[blocks + lo : blocks + hi] + [pts[g]] + static + grads,
+                scratch=[pltpu.VMEM((wide[g], width), BF16)],
+            )
+            grads = list(res[:2])
+            new_pts += list(res[2:])
         halved = last and tps == 2
         span = cols if halved else full
+        lo, hi = groups[2]
         res = kernel_call(
-            functools.partial(key_late_body, first, halved),
+            functools.partial(key_last_body, groups[2], first, halved),
             [sds(rows, span), sds(rows, span, dtype=BF16)]
-            + ([sds(heads, rows, 2 * rows)] if first else []),
-            [got[i] for i in late]
-            + [pt_late, kv_mine, q_mine, q_other, gk, gv, w_key, w_value, part_q],
-            scratch=[pltpu.VMEM((2 * rows, width), BF16), pltpu.VMEM((rows, full), F32)],
+            + ([sds(heads, rows, wide[2])] if first else []),
+            got[lo:hi]
+            + got[blocks + lo : blocks + hi]
+            + [pts[2]]
+            + static
+            + grads
+            + [w_key, w_value, part_q],
+            scratch=[pltpu.VMEM((wide[2], width), BF16), pltpu.VMEM((rows, full), F32)],
         )
         part, send = res[:2]
         if first:
-            pt_late = res[2]
+            pts = new_pts + list(res[2:])
         k = 1
         while True:
             recv = lax.ppermute(send, "tp", [(i, i ^ k) for i in range(tps)])

time: 140 us -> 135 us (0.964)
  waiting for transfers between devices: 63.1 us -> 51.2 us
  starting transfers between devices: 33.7 us -> 36.7 us
  Pallas kernels: 29.3 us -> 32.2 us
    ppermute x20, waiting for transfers between devices: 27.1 us -> 13.7 us  [hop(): return lax.ppermute(x, 'seq', pairs)]
    ppermute x20, starting transfers between devices: 18.3 us -> 25.2 us  [hop(): return lax.ppermute(x, 'seq', pairs)]
    ppermute x4, starting transfers between devices: 6.31 us -> 2.83 us  [on_device(): recv = lax.ppermute(send, 'tp', [(i, i ^ k) for i in range(tps)])]
    ppermute x4, waiting for transfers between devices: 26.1 us -> 29.5 us  [on_device(): recv = lax.ppermute(send, 'tp', [(i, i ^ k) for i in range(tps)])]
    pallas_call x24 -> x28, Pallas kernels: 29.3 us -> 32.2 us  [kernel_call(): pl.pallas_call(body, out_shape=[jax.ShapeDtypeStruct(o.shape, o.dtype) fo...]
    ppermute x4, waiting for transfers between devices: 9.97 us -> 7.98 us  [tp_blocks(): out.append(lax.ppermute(x, 'tp', [((i + k) % tps, i) for i in range(tps)]))]
  transfers between devices with their start and end apart: 50 -> 50, of which waited for: 16 -> 16; matrix products, arithmetic and copies ran while one was open for 0% -> 0% of each run, Pallas kernels for 14% -> 15%
where the time goes in v5:
time: 135 us; the launch traced here: 134 us
  waiting for transfers between devices  51.2 us (38%)
  starting transfers between devices  36.7 us (27%)
  Pallas kernels  32.2 us (24%)
  blocking collectives  10.7 us (8%)
  local copies, waits for them, and re-layouts  2.55 us (2%)
    pallas_call x28, Pallas kernels, kernel_call(): pl.pallas_call(body, out_shape=[jax.ShapeDtypeStruct(o.shape, o.dtype) fo...  32.2 us
    ppermute x4, waiting for transfers between devices, on_device(): recv = lax.ppermute(send, 'tp', [(i, i ^ k) for i in range(tps)])  29.5 us
    ppermute x20, starting transfers between devices, hop(): return lax.ppermute(x, 'seq', pairs)  25.2 us
    ppermute x20, waiting for transfers between devices, hop(): return lax.ppermute(x, 'seq', pairs)  13.7 us
    all_to_all x1, blocking collectives, on_device(): sums = lax.all_to_all(sums, ('seq', 'tp'), 0, 0)  10.7 us
    ppermute x4, waiting for transfers between devices, tp_blocks(): out.append(lax.ppermute(x, 'tp', [((i + k) % tps, i) for i in range(tps)]))  7.98 us
    ppermute x4, starting transfers between devices, tp_blocks(): out.append(lax.ppermute(x, 'tp', [((i + k) % tps, i) for i in range(tps)]))  5.59 us
    ppermute x22, starting transfers between devices, swap_core(): return lax.ppermute(x, 'seq', [(i, i ^ 1) for i in range(seq)])  3.07 us
  transfers between devices with their start and end apart: 50, of which 16 were waited for; matrix products, arithmetic and copies ran while one was open for 0% of the time, Pallas kernels for 15%

profile of v5, /device:TPU:0, one launch (start us, length us, event | category | flops | bytes accessed | tf_op | source)
XLA Modules:
  0.0 134.4 jit_solution(13200970343842971219)
XLA Ops:
  0.6 3.0 %collective-permute-start.5 = (bf16[128,512]{1,0:T(8,128)(2,1)}, bf16[128,512]{1,0:T(8,128)(2,1)S(1)}, u32[]{:S(2)}, u32[]{:S(2)}) collective-permute-start(bf16[128,512]{1,0:T(8,128)(2,1)} %state_ref.1), channel_id=1, source_target_pairs={{1,0},{0,1},{3,2},{2,3},{5,4},{4,5},{7,6},{6,7},{9,8},{8,9},{11,10... | collective-permute-start | bytes 393224 | tf_op jit(solution)/shard_map/ppermute | solution.py:452
  7.5 2.0 %collective-permute-start.6 = (bf16[128,1024]{1,0:T(8,128)(2,1)S(1)}, bf16[128,1024]{1,0:T(8,128)(2,1)S(1)}, u32[]{:S(2)}, u32[]{:S(2)}) collective-permute-start(bf16[128,1024]{1,0:T(8,128)(2,1)S(1)} %get-tuple-element.59.refs_4_), channel_id=1, source_target_pairs={{0,4},{2,6},{4,0},{6,2},{8,12},{10,14},{12,8},{14,10},{16,20},{18,... | collective-permute-start | bytes 786440 | tf_op jit(solution)/shard_map/ppermute | solution.py:464
  9.5 3.1 %collective-permute-start.7 = (bf16[128,1024]{1,0:T(8,128)(2,1)S(1)}, bf16[128,1024]{1,0:T(8,128)(2,1)S(1)}, u32[]{:S(2)}, u32[]{:S(2)}) collective-permute-start(bf16[128,1024]{1,0:T(8,128)(2,1)S(1)} %get-tuple-element.59.refs_4_), channel_id=1, source_target_pairs={{0,8},{2,10},{4,12},{6,14},{8,0},{10,2},{12,4},{14,6},{16,24},{18,... | collective-permute-start | bytes 786440 | tf_op jit(solution)/shard_map/ppermute | solution.py:464
  14.7 2.2 %shard_map.88 = (bf16[1024,512]{1,0:T(8,128)(2,1)S(1)}, bf16[1024,512]{1,0:T(8,128)(2,1)S(1)}, bf16[1024,512]{1,0:T(8,128)(2,1)S(1)}, bf16[512,1024]{1,0:T(8,128)(2,1)S(1)}) custom-call(bf16[1024,512]{1,0:T(8,128)(2,1)} %refs_0_.3, bf16[1024,512]{1,0:T(8,128)(2,1)} %refs_1_.1, bf16[1024,512]{1,0:T(8,128)(2,1)} %refs_2_.1, bf16[512,1024]{1,0:T(8,128)(2,1)} %refs_3_.1), custom_call_target="tpu_custom_call" | custom-call | flops 100000000 | bytes 8388608 | tf_op jit(solution)/shard_map/pallas_call | solution.py:37
  23.2 4.9 %collective-permute-done.refs_1_ = bf16[128,512]{1,0:T(8,128)(2,1)S(1)} collective-permute-done((bf16[128,512]{1,0:T(8,128)(2,1)S(1)}, bf16[128,512]{1,0:T(8,128)(2,1)S(1)}, u32[]{:S(2)}, u32[]{:S(2)}) %collective-permute-start) | collective-permute-done | bytes 131104 | tf_op jit(solution)/shard_map/ppermute | solution.py:452
  28.2 2.8 %shard_map.91 = (f32[4,128,1280]{2,1,0:T(8,128)S(1)}, f32[128,512]{1,0:T(8,128)S(1)}, bf16[144,512]{1,0:T(8,128)(2,1)S(1)}) custom-call(bf16[128,512]{1,0:T(8,128)(2,1)S(1)} %get-tuple-element.56.refs_0_, bf16[128,512]{1,0:T(8,128)(2,1)S(1)} %collective-permute-done.refs_1_, bf16[640,1024]{1,0:T(8,128)(2,1)S(1)} %get-tuple-element.62.kv_ref.refs_2_.refs_3_.refs_5_.kvm_ref, ...), custom_call_target="tpu_custom_call" | custom-call | flops 100000000 | bytes 8929280 | tf_op jit(solution)/shard_map/pallas_call | solution.py:37
  32.8 2.1 %collective-permute-start.10 = (bf16[144,512]{1,0:T(8,128)(2,1)S(1)}, bf16[144,512]{1,0:T(8,128)(2,1)S(1)}, u32[]{:S(2)}, u32[]{:S(2)}) collective-permute-start(bf16[144,512]{1,0:T(8,128)(2,1)S(1)} %get-tuple-element.68.refs_0_.packed_ref), channel_id=1, source_target_pairs={{0,8},{2,10},{4,12},{6,14},{8,0},{10,2},{12,4},{14,6},{16,24},{18,... | collective-permute-start | bytes 442376 | tf_op jit(solution)/shard_map/ppermute | solution.py:464
  35.5 2.6 %collective-permute-done.9.refs_0_ = bf16[144,512]{1,0:T(8,128)(2,1)S(1)} collective-permute-done((bf16[144,512]{1,0:T(8,128)(2,1)S(1)}, bf16[144,512]{1,0:T(8,128)(2,1)S(1)}, u32[]{:S(2)}, u32[]{:S(2)}) %collective-permute-start.9) | collective-permute-done | bytes 147488 | tf_op jit(solution)/shard_map/ppermute | solution.py:464
  45.4 8.2 %collective-permute-done.19.recv_ref = bf16[128,1024]{1,0:T(8,128)(2,1)S(1)} collective-permute-done((bf16[128,1024]{1,0:T(8,128)(2,1)S(1)}, bf16[128,1024]{1,0:T(8,128)(2,1)S(1)}, u32[]{:S(2)}, u32[]{:S(2)}) %collective-permute-start.19) | collective-permute-done | bytes 262176 | tf_op jit(solution)/shard_map/ppermute | solution.py:566
  54.9 2.2 %collective-permute-start.20 = (bf16[144,512]{1,0:T(8,128)(2,1)S(1)}, bf16[144,512]{1,0:T(8,128)(2,1)S(1)}, u32[]{:S(2)}, u32[]{:S(2)}) collective-permute-start(bf16[144,512]{1,0:T(8,128)(2,1)S(1)} %get-tuple-element.81.refs_0_.packed_ref), channel_id=1, source_target_pairs={{0,4},{2,6},{4,0},{6,2},{8,12},{10,14},{12,8},{14,10},{16,20},{18,... | collective-permute-start | bytes 442376 | tf_op jit(solution)/shard_map/ppermute | solution.py:464
  57.2 2.3 %collective-permute-start.21 = (bf16[144,512]{1,0:T(8,128)(2,1)S(1)}, bf16[144,512]{1,0:T(8,128)(2,1)S(1)}, u32[]{:S(2)}, u32[]{:S(2)}) collective-permute-start(bf16[144,512]{1,0:T(8,128)(2,1)S(1)} %get-tuple-element.81.refs_0_.packed_ref), channel_id=1, source_target_pairs={{0,8},{2,10},{4,12},{6,14},{8,0},{10,2},{12,4},{14,6},{16,24},{18,... | collective-permute-start | bytes 442376 | tf_op jit(solution)/shard_map/ppermute | solution.py:464
  60.1 2.4 %collective-permute-done.20.refs_0_ = bf16[144,512]{1,0:T(8,128)(2,1)S(1)} collective-permute-done((bf16[144,512]{1,0:T(8,128)(2,1)S(1)}, bf16[144,512]{1,0:T(8,128)(2,1)S(1)}, u32[]{:S(2)}, u32[]{:S(2)}) %collective-permute-start.20) | collective-permute-done | bytes 147488 | tf_op jit(solution)/shard_map/ppermute | solution.py:464
  63.7 1.8 %shard_map.100.refs_12_ = f32[128,1024]{1,0:T(8,128)S(1)} custom-call(bf16[144,512]{1,0:T(8,128)(2,1)S(1)} %get-tuple-element.81.refs_0_.packed_ref, f32[128,512]{1,0:T(8,128)S(1)} %get-tuple-element.76.att_ref, f32[4,128,1280]{2,1,0:T(8,128)S(1)} %get-tuple-element.77.p_ref, bf16[640,1024]{1,0:T(8,128)(2,1)S(1)} %get-tuple-element.62.kv_ref.refs_2_.refs_3_.refs_5_.kvm_ref, ...), custom_call_target="tpu_custom_call" | custom-call | flops 100000000 | bytes 7225344 | tf_op jit(solution)/shard_map/pallas_call | solution.py:37
  69.5 8.2 %collective-permute-done.29.recv_ref = bf16[128,1024]{1,0:T(8,128)(2,1)S(1)} collective-permute-done((bf16[128,1024]{1,0:T(8,128)(2,1)S(1)}, bf16[128,1024]{1,0:T(8,128)(2,1)S(1)}, u32[]{:S(2)}, u32[]{:S(2)}) %collective-permute-start.29) | collective-permute-done | bytes 262176 | tf_op jit(solution)/shard_map/ppermute | solution.py:566
  79.0 1.9 %collective-permute-start.30 = (bf16[144,512]{1,0:T(8,128)(2,1)S(1)}, bf16[144,512]{1,0:T(8,128)(2,1)S(1)}, u32[]{:S(2)}, u32[]{:S(2)}) collective-permute-start(bf16[144,512]{1,0:T(8,128)(2,1)S(1)} %get-tuple-element.91.refs_0_.packed_ref), channel_id=1, source_target_pairs={{0,4},{2,6},{4,0},{6,2},{8,12},{10,14},{12,8},{14,10},{16,20},{18,... | collective-permute-start | bytes 442376 | tf_op jit(solution)/shard_map/ppermute | solution.py:464
  80.9 2.6 %collective-permute-start.31 = (bf16[144,512]{1,0:T(8,128)(2,1)S(1)}, bf16[144,512]{1,0:T(8,128)(2,1)S(1)}, u32[]{:S(2)}, u32[]{:S(2)}) collective-permute-start(bf16[144,512]{1,0:T(8,128)(2,1)S(1)} %get-tuple-element.91.refs_0_.packed_ref), channel_id=1, source_target_pairs={{0,8},{2,10},{4,12},{6,14},{8,0},{10,2},{12,4},{14,6},{16,24},{18,... | collective-permute-start | bytes 442376 | tf_op jit(solution)/shard_map/ppermute | solution.py:464
  84.1 2.2 %collective-permute-done.30.refs_0_ = bf16[144,512]{1,0:T(8,128)(2,1)S(1)} collective-permute-done((bf16[144,512]{1,0:T(8,128)(2,1)S(1)}, bf16[144,512]{1,0:T(8,128)(2,1)S(1)}, u32[]{:S(2)}, u32[]{:S(2)}) %collective-permute-start.30) | collective-permute-done | bytes 147488 | tf_op jit(solution)/shard_map/ppermute | solution.py:464
  93.1 8.1 %collective-permute-done.39.recv_ref = bf16[128,1024]{1,0:T(8,128)(2,1)S(1)} collective-permute-done((bf16[128,1024]{1,0:T(8,128)(2,1)S(1)}, bf16[128,1024]{1,0:T(8,128)(2,1)S(1)}, u32[]{:S(2)}, u32[]{:S(2)}) %collective-permute-start.39) | collective-permute-done | bytes 262176 | tf_op jit(solution)/shard_map/ppermute | solution.py:566
  102.5 2.1 %collective-permute-start.40 = (bf16[144,512]{1,0:T(8,128)(2,1)S(1)}, bf16[144,512]{1,0:T(8,128)(2,1)S(1)}, u32[]{:S(2)}, u32[]{:S(2)}) collective-permute-start(bf16[144,512]{1,0:T(8,128)(2,1)S(1)} %get-tuple-element.98.refs_0_.packed_ref), channel_id=1, source_target_pairs={{0,4},{2,6},{4,0},{6,2},{8,12},{10,14},{12,8},{14,10},{16,20},{18,... | collective-permute-start | bytes 442376 | tf_op jit(solution)/shard_map/ppermute | solution.py:464
  104.6 2.7 %collective-permute-start.41 = (bf16[144,512]{1,0:T(8,128)(2,1)S(1)}, bf16[144,512]{1,0:T(8,128)(2,1)S(1)}, u32[]{:S(2)}, u32[]{:S(2)}) collective-permute-start(bf16[144,512]{1,0:T(8,128)(2,1)S(1)} %get-tuple-element.98.refs_0_.packed_ref), channel_id=1, source_target_pairs={{0,8},{2,10},{4,12},{6,14},{8,0},{10,2},{12,4},{14,6},{16,24},{18,... | collective-permute-start | bytes 442376 | tf_op jit(solution)/shard_map/ppermute | solution.py:464
  107.9 2.1 %collective-permute-done.40.refs_0_ = bf16[144,512]{1,0:T(8,128)(2,1)S(1)} collective-permute-done((bf16[144,512]{1,0:T(8,128)(2,1)S(1)}, bf16[144,512]{1,0:T(8,128)(2,1)S(1)}, u32[]{:S(2)}, u32[]{:S(2)}) %collective-permute-start.40) | collective-permute-done | bytes 147488 | tf_op jit(solution)/shard_map/ppermute | solution.py:464
  114.2 1.8 %shard_map.111 = (f32[128,512]{1,0:T(8,128)S(1)}, bf16[128,512]{1,0:T(8,128)(2,1)S(1)}) custom-call(bf16[144,512]{1,0:T(8,128)(2,1)S(1)} %collective-permute-done.40.refs_0_, bf16[144,512]{1,0:T(8,128)(2,1)S(1)} %collective-permute-done.41.refs_1_, bf16[144,512]{1,0:T(8,128)(2,1)S(1)} %collective-permute-done.42.refs_2_, ...), custom_call_target="tpu_custom_call" | custom-call | flops 100000000 | bytes 7798784 | tf_op jit(solution)/shard_map/pallas_call | solution.py:37
  117.0 5.0 %collective-permute-done.49.recv_ref = bf16[128,512]{1,0:T(8,128)(2,1)S(1)} collective-permute-done((bf16[128,512]{1,0:T(8,128)(2,1)S(1)}, bf16[128,512]{1,0:T(8,128)(2,1)S(1)}, u32[]{:S(2)}, u32[]{:S(2)}) %collective-permute-start.49) | collective-permute-done | bytes 131104 | tf_op jit(solution)/shard_map/ppermute | solution.py:566
  122.5 10.7 %all_to_all.5.sums_ref = f32[32,1,128]{2,1,0:T(1,128)S(1)} all-to-all(f32[32,1,128]{2,1,0:T(1,128)S(1)} %get-tuple-element.108), channel_id=1, replica_groups=mesh['seq'=16,'tp'=2] {'seq','tp'}, dimensions={0} | all-to-all | bytes 32768 | tf_op jit(solution)/shard_map/all_to_all | solution.py:587
  (113 shorter events, 46.2 us)
Async XLA Ops:
  0.6 6.7 %collective-permute-start.5 = (bf16[128,512]{1,0:T(8,128)(2,1)}, bf16[128,512]{1,0:T(8,128)(2,1)S(1)}, u32[]{:S(2)}, u32[]{:S(2)}) collective-permute-start(bf16[128,512]{1,0:T(8,128)(2,1)} %state_ref.1), channel_id=1, source_target_pairs={{1,0},{0,1},{3,2},{2,3},{5,4},{4,5},{7,6},{6,7},{9,8},{8,9},{11,10... | collective-permute-start | bytes 393224 | tf_op jit(solution)/shard_map/ppermute | solution.py:452
  3.7 9.0 %collective-permute-start.1 = (bf16[128,512]{1,0:T(8,128)(2,1)}, bf16[128,512]{1,0:T(8,128)(2,1)S(1)}, u32[]{:S(2)}, u32[]{:S(2)}) collective-permute-start(bf16[128,512]{1,0:T(8,128)(2,1)} %state_ref.1), channel_id=1, source_target_pairs={{0,2},{2,0},{4,8},{6,10},{8,4},{10,6},{12,16},{14,18},{16,12},{18,... | collective-permute-start | bytes 393224 | tf_op jit(solution)/shard_map/ppermute | solution.py:464
  3.7 9.5 %collective-permute-start.3 = (bf16[128,512]{1,0:T(8,128)(2,1)}, bf16[128,512]{1,0:T(8,128)(2,1)S(1)}, u32[]{:S(2)}, u32[]{:S(2)}) collective-permute-start(bf16[128,512]{1,0:T(8,128)(2,1)} %state_ref.1), channel_id=1, source_target_pairs={{0,2},{2,0},{4,6},{6,4},{8,16},{10,18},{12,20},{14,22},{16,8},{18,... | collective-permute-start | bytes 393224 | tf_op jit(solution)/shard_map/ppermute | solution.py:464
  7.5 11.8 %collective-permute-start.6 = (bf16[128,1024]{1,0:T(8,128)(2,1)S(1)}, bf16[128,1024]{1,0:T(8,128)(2,1)S(1)}, u32[]{:S(2)}, u32[]{:S(2)}) collective-permute-start(bf16[128,1024]{1,0:T(8,128)(2,1)S(1)} %get-tuple-element.59.refs_4_), channel_id=1, source_target_pairs={{0,4},{2,6},{4,0},{6,2},{8,12},{10,14},{12,8},{14,10},{16,20},{18,... | collective-permute-start | bytes 786440 | tf_op jit(solution)/shard_map/ppermute | solution.py:464
  9.5 9.8 %collective-permute-start.7 = (bf16[128,1024]{1,0:T(8,128)(2,1)S(1)}, bf16[128,1024]{1,0:T(8,128)(2,1)S(1)}, u32[]{:S(2)}, u32[]{:S(2)}) collective-permute-start(bf16[128,1024]{1,0:T(8,128)(2,1)S(1)} %get-tuple-element.59.refs_4_), channel_id=1, source_target_pairs={{0,8},{2,10},{4,12},{6,14},{8,0},{10,2},{12,4},{14,6},{16,24},{18,... | collective-permute-start | bytes 786440 | tf_op jit(solution)/shard_map/ppermute | solution.py:464
  13.2 6.1 %collective-permute-start.4 = (bf16[128,512]{1,0:T(8,128)(2,1)S(1)}, bf16[128,512]{1,0:T(8,128)(2,1)S(1)}, u32[]{:S(2)}, u32[]{:S(2)}) collective-permute-start(bf16[128,512]{1,0:T(8,128)(2,1)S(1)} %collective-permute-done.3.refs_2_), channel_id=1, source_target_pairs={{1,0},{0,1},{3,2},{2,3},{5,4},{4,5},{7,6},{6,7},{9,8},{8,9},{11,10... | collective-permute-start | bytes 393224 | tf_op jit(solution)/shard_map/ppermute | solution.py:452
  21.0 7.2 %collective-permute-start.8 = (bf16[640,1024]{1,0:T(8,128)(2,1)S(1)}, bf16[640,1024]{1,0:T(8,128)(2,1)S(1)}, u32[]{:S(2)}, u32[]{:S(2)}) collective-permute-start(bf16[640,1024]{1,0:T(8,128)(2,1)S(1)} %get-tuple-element.62.kv_ref.refs_2_.refs_3_.refs_5_.kvm_ref), channel_id=1, source_target_pairs={{0,2},{2,0},{4,6},{6,4},{8,10},{10,8},{12,14},{14,12},{16,18},{18,... | collective-permute-start | bytes 3932168 | tf_op jit(solution)/shard_map/ppermute | solution.py:447
  22.1 12.8 %collective-permute-start.13 = (bf16[640,512]{1,0:T(8,128)(2,1)S(1)}, bf16[640,512]{1,0:T(8,128)(2,1)S(1)}, u32[]{:S(2)}, u32[]{:S(2)}) collective-permute-start(bf16[640,512]{1,0:T(8,128)(2,1)S(1)} %get-tuple-element.65.refs_4_.qm_ref.refs_6_), channel_id=1, source_target_pairs={{0,2},{2,0},{4,6},{6,4},{8,10},{10,8},{12,14},{14,12},{16,18},{18,... | collective-permute-start | bytes 1966088 | tf_op jit(solution)/shard_map/ppermute | solution.py:447
  31.5 6.6 %collective-permute-start.9 = (bf16[144,512]{1,0:T(8,128)(2,1)S(1)}, bf16[144,512]{1,0:T(8,128)(2,1)S(1)}, u32[]{:S(2)}, u32[]{:S(2)}) collective-permute-start(bf16[144,512]{1,0:T(8,128)(2,1)S(1)} %get-tuple-element.68.refs_0_.packed_ref), channel_id=1, source_target_pairs={{0,4},{2,6},{4,0},{6,2},{8,12},{10,14},{12,8},{14,10},{16,20},{18,... | collective-permute-start | bytes 442376 | tf_op jit(solution)/shard_map/ppermute | solution.py:464
  32.8 6.3 %collective-permute-start.10 = (bf16[144,512]{1,0:T(8,128)(2,1)S(1)}, bf16[144,512]{1,0:T(8,128)(2,1)S(1)}, u32[]{:S(2)}, u32[]{:S(2)}) collective-permute-start(bf16[144,512]{1,0:T(8,128)(2,1)S(1)} %get-tuple-element.68.refs_0_.packed_ref), channel_id=1, source_target_pairs={{0,8},{2,10},{4,12},{6,14},{8,0},{10,2},{12,4},{14,6},{16,24},{18,... | collective-permute-start | bytes 442376 | tf_op jit(solution)/shard_map/ppermute | solution.py:464
  34.9 6.6 %collective-permute-start.18 = (bf16[144,512]{1,0:T(8,128)(2,1)S(1)}, bf16[144,512]{1,0:T(8,128)(2,1)S(1)}, u32[]{:S(2)}, u32[]{:S(2)}) collective-permute-start(bf16[144,512]{1,0:T(8,128)(2,1)S(1)} %get-tuple-element.68.refs_0_.packed_ref), channel_id=1, source_target_pairs={{0,2},{2,0},{4,6},{6,4},{8,10},{10,8},{12,14},{14,12},{16,18},{18,... | collective-permute-start | bytes 442376 | tf_op jit(solution)/shard_map/ppermute | solution.py:447
  34.9 7.1 %collective-permute-start.16 = (bf16[144,512]{1,0:T(8,128)(2,1)S(1)}, bf16[144,512]{1,0:T(8,128)(2,1)S(1)}, u32[]{:S(2)}, u32[]{:S(2)}) collective-permute-start(bf16[144,512]{1,0:T(8,128)(2,1)S(1)} %collective-permute-done.14.refs_0_), channel_id=1, source_target_pairs={{0,2},{2,0},{4,6},{6,4},{8,10},{10,8},{12,14},{14,12},{16,18},{18,... | collective-permute-start | bytes 442376 | tf_op jit(solution)/shard_map/ppermute | solution.py:447
  35.5 6.6 %collective-permute-start.17 = (bf16[144,512]{1,0:T(8,128)(2,1)S(1)}, bf16[144,512]{1,0:T(8,128)(2,1)S(1)}, u32[]{:S(2)}, u32[]{:S(2)}) collective-permute-start(bf16[144,512]{1,0:T(8,128)(2,1)S(1)} %collective-permute-done.15.refs_1_), channel_id=1, source_target_pairs={{0,2},{2,0},{4,6},{6,4},{8,10},{10,8},{12,14},{14,12},{16,18},{18,... | collective-permute-start | bytes 442376 | tf_op jit(solution)/shard_map/ppermute | solution.py:447
  44.8 8.8 %collective-permute-start.19 = (bf16[128,1024]{1,0:T(8,128)(2,1)S(1)}, bf16[128,1024]{1,0:T(8,128)(2,1)S(1)}, u32[]{:S(2)}, u32[]{:S(2)}) collective-permute-start(bf16[128,1024]{1,0:T(8,128)(2,1)S(1)} %get-tuple-element.79), channel_id=1, source_target_pairs={{0,1},{1,0},{2,3},{3,2},{4,5},{5,4},{6,7},{7,6},{8,9},{9,8},{10,11... | collective-permute-start | bytes 786440 | tf_op jit(solution)/shard_map/ppermute | solution.py:566
  54.9 7.6 %collective-permute-start.20 = (bf16[144,512]{1,0:T(8,128)(2,1)S(1)}, bf16[144,512]{1,0:T(8,128)(2,1)S(1)}, u32[]{:S(2)}, u32[]{:S(2)}) collective-permute-start(bf16[144,512]{1,0:T(8,128)(2,1)S(1)} %get-tuple-element.81.refs_0_.packed_ref), channel_id=1, source_target_pairs={{0,4},{2,6},{4,0},{6,2},{8,12},{10,14},{12,8},{14,10},{16,20},{18,... | collective-permute-start | bytes 442376 | tf_op jit(solution)/shard_map/ppermute | solution.py:464
  57.2 6.6 %collective-permute-start.21 = (bf16[144,512]{1,0:T(8,128)(2,1)S(1)}, bf16[144,512]{1,0:T(8,128)(2,1)S(1)}, u32[]{:S(2)}, u32[]{:S(2)}) collective-permute-start(bf16[144,512]{1,0:T(8,128)(2,1)S(1)} %get-tuple-element.81.refs_0_.packed_ref), channel_id=1, source_target_pairs={{0,8},{2,10},{4,12},{6,14},{8,0},{10,2},{12,4},{14,6},{16,24},{18,... | collective-permute-start | bytes 442376 | tf_op jit(solution)/shard_map/ppermute | solution.py:464
  59.5 6.6 %collective-permute-start.26 = (bf16[144,512]{1,0:T(8,128)(2,1)S(1)}, bf16[144,512]{1,0:T(8,128)(2,1)S(1)}, u32[]{:S(2)}, u32[]{:S(2)}) collective-permute-start(bf16[144,512]{1,0:T(8,128)(2,1)S(1)} %collective-permute-done.24.refs_0_), channel_id=1, source_target_pairs={{0,2},{2,0},{4,6},{6,4},{8,10},{10,8},{12,14},{14,12},{16,18},{18,... | collective-permute-start | bytes 442376 | tf_op jit(solution)/shard_map/ppermute | solution.py:447
  68.9 8.8 %collective-permute-start.29 = (bf16[128,1024]{1,0:T(8,128)(2,1)S(1)}, bf16[128,1024]{1,0:T(8,128)(2,1)S(1)}, u32[]{:S(2)}, u32[]{:S(2)}) collective-permute-start(bf16[128,1024]{1,0:T(8,128)(2,1)S(1)} %get-tuple-element.90), channel_id=1, source_target_pairs={{0,1},{1,0},{2,3},{3,2},{4,5},{5,4},{6,7},{7,6},{8,9},{9,8},{10,11... | collective-permute-start | bytes 786440 | tf_op jit(solution)/shard_map/ppermute | solution.py:566
  79.0 7.3 %collective-permute-start.30 = (bf16[144,512]{1,0:T(8,128)(2,1)S(1)}, bf16[144,512]{1,0:T(8,128)(2,1)S(1)}, u32[]{:S(2)}, u32[]{:S(2)}) collective-permute-start(bf16[144,512]{1,0:T(8,128)(2,1)S(1)} %get-tuple-element.91.refs_0_.packed_ref), channel_id=1, source_target_pairs={{0,4},{2,6},{4,0},{6,2},{8,12},{10,14},{12,8},{14,10},{16,20},{18,... | collective-permute-start | bytes 442376 | tf_op jit(solution)/shard_map/ppermute | solution.py:464
  80.9 6.6 %collective-permute-start.31 = (bf16[144,512]{1,0:T(8,128)(2,1)S(1)}, bf16[144,512]{1,0:T(8,128)(2,1)S(1)}, u32[]{:S(2)}, u32[]{:S(2)}) collective-permute-start(bf16[144,512]{1,0:T(8,128)(2,1)S(1)} %get-tuple-element.91.refs_0_.packed_ref), channel_id=1, source_target_pairs={{0,8},{2,10},{4,12},{6,14},{8,0},{10,2},{12,4},{14,6},{16,24},{18,... | collective-permute-start | bytes 442376 | tf_op jit(solution)/shard_map/ppermute | solution.py:464
  83.5 6.2 %collective-permute-start.36 = (bf16[144,512]{1,0:T(8,128)(2,1)S(1)}, bf16[144,512]{1,0:T(8,128)(2,1)S(1)}, u32[]{:S(2)}, u32[]{:S(2)}) collective-permute-start(bf16[144,512]{1,0:T(8,128)(2,1)S(1)} %collective-permute-done.34.refs_0_), channel_id=1, source_target_pairs={{0,2},{2,0},{4,6},{6,4},{8,10},{10,8},{12,14},{14,12},{16,18},{18,... | collective-permute-start | bytes 442376 | tf_op jit(solution)/shard_map/ppermute | solution.py:447
  92.4 8.8 %collective-permute-start.39 = (bf16[128,1024]{1,0:T(8,128)(2,1)S(1)}, bf16[128,1024]{1,0:T(8,128)(2,1)S(1)}, u32[]{:S(2)}, u32[]{:S(2)}) collective-permute-start(bf16[128,1024]{1,0:T(8,128)(2,1)S(1)} %get-tuple-element.97), channel_id=1, source_target_pairs={{0,1},{1,0},{2,3},{3,2},{4,5},{5,4},{6,7},{7,6},{8,9},{9,8},{10,11... | collective-permute-start | bytes 786440 | tf_op jit(solution)/shard_map/ppermute | solution.py:566
  102.5 7.5 %collective-permute-start.40 = (bf16[144,512]{1,0:T(8,128)(2,1)S(1)}, bf16[144,512]{1,0:T(8,128)(2,1)S(1)}, u32[]{:S(2)}, u32[]{:S(2)}) collective-permute-start(bf16[144,512]{1,0:T(8,128)(2,1)S(1)} %get-tuple-element.98.refs_0_.packed_ref), channel_id=1, source_target_pairs={{0,4},{2,6},{4,0},{6,2},{8,12},{10,14},{12,8},{14,10},{16,20},{18,... | collective-permute-start | bytes 442376 | tf_op jit(solution)/shard_map/ppermute | solution.py:464
  104.6 6.4 %collective-permute-start.41 = (bf16[144,512]{1,0:T(8,128)(2,1)S(1)}, bf16[144,512]{1,0:T(8,128)(2,1)S(1)}, u32[]{:S(2)}, u32[]{:S(2)}) collective-permute-start(bf16[144,512]{1,0:T(8,128)(2,1)S(1)} %get-tuple-element.98.refs_0_.packed_ref), channel_id=1, source_target_pairs={{0,8},{2,10},{4,12},{6,14},{8,0},{10,2},{12,4},{14,6},{16,24},{18,... | collective-permute-start | bytes 442376 | tf_op jit(solution)/shard_map/ppermute | solution.py:464
  (30 other events, 140.2 us)

commit v6 on v5

--- a/solution.py
+++ b/solution.py
@@ -13,7 +13,7 @@
 WIN = 1024
 SSTEP = 4
 EPSILON = 1e-05
-PAD = 16
+PAD = 8
 NEG = -1e30
 SCALE = 1.0 / math.sqrt(HD)
 NT = (((1,), (1,)), ((), ()))
@@ -233,11 +233,10 @@
             ref[h] = masked(s * SCALE, masks[lo:hi] + masks[blocks + lo : blocks + hi])
 
 
-def query_body(packed_ref, att_ref, p_ref, kvm_ref, kvo_ref, wq_ref, part_ref):
+def query_grads(packed_ref, att_ref, p_ref, kvm_ref, kvo_ref, gq_ref):
     rows, width = att_ref.shape
     heads = width // HD
     near = kvm_ref.shape[0]
-    grads = []
     for h in range(heads):
         go = packed_ref[:rows, col(h)]
         corr = jnp.sum(go.astype(F32) * att_ref[:, col(h)], axis=1, keepdims=True)
@@ -245,8 +244,12 @@
         gp = jnp.concatenate([mm(go, kvm_ref[:, v], NT), mm(go, kvo_ref[:, v], NT)], axis=1)
         gs = (SCALE * p_ref[h] * (gp - corr)).astype(BF16)
         gq = mm(gs[:, :near], kvm_ref[:, col(h)]) + mm(gs[:, near:], kvo_ref[:, col(h)])
-        grads.append(gq.astype(BF16))
-    part_ref[...] = mm(jnp.concatenate(grads, axis=1), wq_ref[...], NT)
+        gq_ref[:, col(h)] = gq.astype(BF16)
+
+
+def query_body(packed_ref, att_ref, p_ref, kvm_ref, kvo_ref, wq_ref, part_ref, gq_ref):
+    query_grads(packed_ref, att_ref, p_ref, kvm_ref, kvo_ref, gq_ref)
+    part_ref[...] = mm(gq_ref[...], wq_ref[...], NT)
 
 
 def key_terms(got, part, first, pt_in, pt_ref, kv_ref, qm_ref, qo_ref, gow_ref, h):
@@ -318,6 +321,77 @@
     else:
         part_ref[...] = acc
         send_ref[...] = acc.astype(BF16)
+
+
+def half_rows_body(w_ref, o_ref):
+    n = o_ref.shape[0]
+    core = lax.axis_index("seq") % 2
+    o_ref[...] = w_ref[pl.ds(pl.multiple_of(core * n, n), n), :]
+
+
+def fold_body(wo_ref, mine_ref, other_ref, gain_ref, wq_ref, wk_ref, wv_ref, ft_ref, full_ref):
+    n = mine_ref.shape[0]
+    core = lax.axis_index("seq") % 2
+    full_ref[pl.ds(pl.multiple_of(core * n, n), n), :] = mine_ref[...]
+    full_ref[pl.ds(pl.multiple_of((1 - core) * n, n), n), :] = other_ref[...]
+    for i, ref in enumerate((wo_ref, full_ref)):
+        scaled = (ref[...].astype(F32) * gain_ref[...]).astype(BF16)
+        for j, w in enumerate((wq_ref, wk_ref, wv_ref)):
+            ft_ref[i, j] = mm(scaled, w[...]).astype(BF16)
+
+
+def query_fold_body(packed_ref, att_ref, p_ref, kvm_ref, kvo_ref, ft_ref, gq_ref, own_ref, oth_ref):
+    query_grads(packed_ref, att_ref, p_ref, kvm_ref, kvo_ref, gq_ref)
+    gq = gq_ref[...]
+    own_ref[...] = mm(gq, ft_ref[0, 0], NT)
+    oth_ref[...] = mm(gq, ft_ref[1, 0], NT)
+
+
+def key_fold_body(span, *refs):
+    lo, hi = span
+    slots = 2 * (hi - lo)
+    got = refs[:slots]
+    pt_in, kv_ref, qm_ref, qo_ref, gk_in, gv_in, ft_ref, ownq_ref, othq_ref = refs[
+        slots : slots + 9
+    ]
+    own_ref, send_ref, gk_ref, gv_ref, gow_ref = refs[slots + 9 :]
+    rows = got[0].shape[0] - PAD
+    for b in range(slots):
+        gow_ref[b * rows : (b + 1) * rows, :] = got[b][:rows, :]
+    part = slice(lo * rows, hi * rows)
+    for h in range(pt_in.shape[0]):
+        gk, gv = key_terms(got, part, False, pt_in, None, kv_ref, qm_ref, qo_ref, gow_ref, h)
+        gk_ref[:, col(h)] = (gk_in[:, col(h)] + gk).astype(BF16)
+        gv_ref[:, col(h)] = (gv_in[:, col(h)] + gv).astype(BF16)
+    gk, gv = gk_ref[...], gv_ref[...]
+    own_ref[...] = ownq_ref[...] + mm(gk, ft_ref[0, 1], NT) + mm(gv, ft_ref[0, 2], NT)
+    oth = othq_ref[...] + mm(gk, ft_ref[1, 1], NT) + mm(gv, ft_ref[1, 2], NT)
+    send_ref[...] = oth.astype(BF16)
+
+
+def combine_fold_body(own_ref, recv_ref, inv_ref, att_ref, packed_ref):
+    rows, width = att_ref.shape
+    go = (inv_ref[:, :1] * (own_ref[...] + recv_ref[...].astype(F32))).astype(BF16)
+    packed_ref[:rows, :] = go
+    corr = [
+        jnp.sum(go[:, col(h)].astype(F32) * att_ref[:, col(h)], axis=1, keepdims=True)
+        for h in range(width // HD)
+    ]
+    pack_rows(packed_ref, rows, width // HD, corr)
+
+
+def side_body(gq_ref, gk_ref, gv_ref, wq_ref, wk_ref, wv_ref, part_ref, send_ref, sum_ref):
+    acc = mm(gq_ref[...], wq_ref[...], NT) + mm(gk_ref[...], wk_ref[...], NT)
+    sum_ref[...] = acc + mm(gv_ref[...], wv_ref[...], NT)
+    mine, other = feature_slices(2, part_ref.shape[1])
+    part_ref[...] = sum_ref[:, mine]
+    send_ref[...] = sum_ref[:, other].astype(BF16)
+
+
+def side_sum_body(part_ref, recv_ref, inv_ref, gain_ref, kry_ref):
+    mine = feature_slices(2, part_ref.shape[1])[0]
+    vec = part_ref[...] + recv_ref[...].astype(F32)
+    kry_ref[...] = inv_ref[:, :1] * (gain_ref[:, mine] * vec)
 
 
 def combine_body(part_ref, recv_ref, inv_ref, gain_ref, wo_ref, att_ref, *refs):
@@ -513,7 +587,12 @@
         cots + [kv_mine, kv_other, q_mine, s_mine, w_out],
         scratch=[pltpu.VMEM((rows, full), BF16)],
     )
+    fold = tps == 2
+    if fold:
+        (wo_half,) = kernel_call(half_rows_body, [sds(width // 2, full, dtype=BF16)], [w_out])
+        wo_mine = tp_blocks(wo_half)[1]
     krylov = [cotangent]
+    side = None
     for n in range(SSTEP):
         first, last = n == 0, n == SSTEP - 1
         if first:
@@ -524,11 +603,34 @@
             )
         got = fetch(packed)
         got = got + [swap_core(x) for x in got]
-        (part_q,) = kernel_call(
-            query_body,
-            [sds(rows, full)],
-            [packed, att, probs, kv_mine, kv_other, w_query],
-        )
+        folded = fold and 1 <= n < SSTEP - 1
+        if side is not None:
+            mine, other = kernel_call(
+                side_body,
+                [sds(rows, cols), sds(rows, cols, dtype=BF16)],
+                side + [w_query, w_key, w_value],
+                scratch=[pltpu.VMEM((rows, full), F32)],
+            )
+            other = tp_blocks(other)[1]
+            (kry,) = kernel_call(
+                side_sum_body, [sds(rows, cols)], [mine, other, inv, gain]
+            )
+            krylov.append(kry)
+            side = None
+        inputs = [packed, att, probs, kv_mine, kv_other]
+        if folded:
+            gq, *part_q = kernel_call(
+                query_fold_body,
+                [sds(rows, width, dtype=BF16), sds(rows, width), sds(rows, width)],
+                inputs + [folds],
+            )
+        else:
+            part_q = kernel_call(
+                query_body,
+                [sds(rows, full)],
+                inputs + [w_query],
+                scratch=[pltpu.VMEM((rows, width), BF16)],
+            )
         static = [kv_mine, q_mine, q_other]
         grads = []
         new_pts = []
@@ -546,6 +648,28 @@
         halved = last and tps == 2
         span = cols if halved else full
         lo, hi = groups[2]
+        if folded:
+            own, send, gk, gv = kernel_call(
+                functools.partial(key_fold_body, groups[2]),
+                [sds(rows, width), sds(rows, width, dtype=BF16)]
+                + [sds(rows, width, dtype=BF16)] * 2,
+                got[lo:hi]
+                + got[blocks + lo : blocks + hi]
+                + [pts[2]]
+                + static
+                + grads
+                + [folds]
+                + list(part_q),
+                scratch=[pltpu.VMEM((wide[2], width), BF16)],
+            )
+            recv = tp_blocks(send)[1]
+            (packed,) = kernel_call(
+                combine_fold_body,
+                [sds(rows + PAD, width, dtype=BF16)],
+                [own, recv, inv, att],
+            )
+            side = [gq, gk, gv]
+            continue
         res = kernel_call(
             functools.partial(key_last_body, groups[2], first, halved),
             [sds(rows, span), sds(rows, span, dtype=BF16)]
@@ -555,7 +679,8 @@
             + [pts[2]]
             + static
             + grads
-            + [w_key, w_value, part_q],
+            + [w_key, w_value]
+            + list(part_q),
             scratch=[pltpu.VMEM((wide[2], width), BF16), pltpu.VMEM((rows, full), F32)],
         )
         part, send = res[:2]
@@ -569,6 +694,15 @@
                 break
             part = part + recv.astype(F32)
             send = part.astype(BF16)
+        if fold and first:
+            wo_other = swap_core(wo_mine)
+            (folds,) = kernel_call(
+                fold_body,
+                [sds(2, 3, width, width, dtype=BF16)],
+                [w_out, wo_mine, wo_other, gain, w_query, w_key, w_value],
+                scratch=[pltpu.VMEM((width, full), BF16)],
+                limit=16 << 20,
+            )
         if not last:
             kry, packed = kernel_call(
                 combine_body,

time: 135 us -> 148 us (1.096)
  Pallas kernels: 32.2 us -> 38.1 us
  starting transfers between devices: 36.7 us -> 41.1 us
  waiting for transfers between devices: 51.2 us -> 54.1 us
    ppermute x4 -> x9, waiting for transfers between devices: 7.98 us -> 31.2 us  [tp_blocks(): out.append(lax.ppermute(x, 'tp', [((i + k) % tps, i) for i in range(tps)]))]
    ppermute x4 -> x2, waiting for transfers between devices: 29.5 us -> 9.94 us  [on_device(): recv = lax.ppermute(send, 'tp', [(i, i ^ k) for i in range(tps)])]
    pallas_call x28 -> x34, Pallas kernels: 32.2 us -> 38.1 us  [kernel_call(): pl.pallas_call(body, out_shape=[jax.ShapeDtypeStruct(o.shape, o.dtype) fo...]
    ppermute x4 -> x9, starting transfers between devices: 5.59 us -> 10.6 us  [tp_blocks(): out.append(lax.ppermute(x, 'tp', [((i + k) % tps, i) for i in range(tps)]))]
    ppermute x22 -> x23, starting transfers between devices: 3.07 us -> 3.61 us  [swap_core(): return lax.ppermute(x, 'seq', [(i, i ^ 1) for i in range(seq)])]
  transfers between devices with their start and end apart: 50 -> 54, of which waited for: 16 -> 18; matrix products, arithmetic and copies ran while one was open for 0% -> 0% of each run, Pallas kernels for 15% -> 21%
where the time goes in v6:
time: 148 us
  waiting for transfers between devices  54.1 us (37%)
  starting transfers between devices  41.1 us (28%)
  Pallas kernels  38.1 us (26%)
  blocking collectives  10.5 us (7%)
  local copies, waits for them, and re-layouts  2.55 us (2%)
    pallas_call x34, Pallas kernels, kernel_call(): pl.pallas_call(body, out_shape=[jax.ShapeDtypeStruct(o.shape, o.dtype) fo...  38.1 us
    ppermute x9, waiting for transfers between devices, tp_blocks(): out.append(lax.ppermute(x, 'tp', [((i + k) % tps, i) for i in range(tps)]))  31.2 us
    ppermute x20, starting transfers between devices, hop(): return lax.ppermute(x, 'seq', pairs)  25.5 us
    ppermute x20, waiting for transfers between devices, hop(): return lax.ppermute(x, 'seq', pairs)  13 us
    ppermute x9, starting transfers between devices, tp_blocks(): out.append(lax.ppermute(x, 'tp', [((i + k) % tps, i) for i in range(tps)]))  10.6 us
    all_to_all x1, blocking collectives, on_device(): sums = lax.all_to_all(sums, ('seq', 'tp'), 0, 0)  10.5 us
    ppermute x2, waiting for transfers between devices, on_device(): recv = lax.ppermute(send, 'tp', [(i, i ^ k) for i in range(tps)])  9.94 us
    ppermute x23, starting transfers between devices, swap_core(): return lax.ppermute(x, 'seq', [(i, i ^ 1) for i in range(seq)])  3.61 us
  transfers between devices with their start and end apart: 54, of which 18 were waited for; matrix products, arithmetic and copies ran while one was open for 0% of the time, Pallas kernels for 21%

profile of v6, /device:TPU:0, one launch (start us, length us, event | category | flops | bytes accessed | tf_op | source)
XLA Modules:
  0.0 147.5 jit_solution(11235724070101545348)
XLA Ops:
  0.6 3.0 %collective-permute-start.5 = (bf16[128,512]{1,0:T(8,128)(2,1)}, bf16[128,512]{1,0:T(8,128)(2,1)S(1)}, u32[]{:S(2)}, u32[]{:S(2)}) collective-permute-start(bf16[128,512]{1,0:T(8,128)(2,1)} %state_ref.1), channel_id=1, source_target_pairs={{1,0},{0,1},{3,2},{2,3},{5,4},{4,5},{7,6},{6,7},{9,8},{8,9},{11,10... | collective-permute-start | bytes 393224 | tf_op jit(solution)/shard_map/ppermute | solution.py:526
  7.5 2.0 %collective-permute-start.6 = (bf16[128,1024]{1,0:T(8,128)(2,1)S(1)}, bf16[128,1024]{1,0:T(8,128)(2,1)S(1)}, u32[]{:S(2)}, u32[]{:S(2)}) collective-permute-start(bf16[128,1024]{1,0:T(8,128)(2,1)S(1)} %get-tuple-element.69.refs_4_), channel_id=1, source_target_pairs={{0,4},{2,6},{4,0},{6,2},{8,12},{10,14},{12,8},{14,10},{16,20},{18,... | collective-permute-start | bytes 786440 | tf_op jit(solution)/shard_map/ppermute | solution.py:538
  9.5 3.1 %collective-permute-start.7 = (bf16[128,1024]{1,0:T(8,128)(2,1)S(1)}, bf16[128,1024]{1,0:T(8,128)(2,1)S(1)}, u32[]{:S(2)}, u32[]{:S(2)}) collective-permute-start(bf16[128,1024]{1,0:T(8,128)(2,1)S(1)} %get-tuple-element.69.refs_4_), channel_id=1, source_target_pairs={{0,8},{2,10},{4,12},{6,14},{8,0},{10,2},{12,4},{14,6},{16,24},{18,... | collective-permute-start | bytes 786440 | tf_op jit(solution)/shard_map/ppermute | solution.py:538
  14.7 2.2 %shard_map.88 = (bf16[1024,512]{1,0:T(8,128)(2,1)S(1)}, bf16[1024,512]{1,0:T(8,128)(2,1)S(1)}, bf16[1024,512]{1,0:T(8,128)(2,1)S(1)}, bf16[512,1024]{1,0:T(8,128)(2,1)S(1)}) custom-call(bf16[1024,512]{1,0:T(8,128)(2,1)} %refs_0_.3, bf16[1024,512]{1,0:T(8,128)(2,1)} %refs_1_.1, bf16[1024,512]{1,0:T(8,128)(2,1)} %refs_2_.1, bf16[512,1024]{1,0:T(8,128)(2,1)} %refs_3_.1), custom_call_target="tpu_custom_call" | custom-call | flops 100000000 | bytes 8388608 | tf_op jit(solution)/shard_map/pallas_call | solution.py:37
  24.8 14.6 %collective-permute-done.refs_1_ = bf16[128,512]{1,0:T(8,128)(2,1)S(1)} collective-permute-done((bf16[128,512]{1,0:T(8,128)(2,1)S(1)}, bf16[128,512]{1,0:T(8,128)(2,1)S(1)}, u32[]{:S(2)}, u32[]{:S(2)}) %collective-permute-start) | collective-permute-done | bytes 131104 | tf_op jit(solution)/shard_map/ppermute | solution.py:526
  39.5 2.8 %shard_map.91 = (f32[4,128,1280]{2,1,0:T(8,128)S(1)}, f32[128,512]{1,0:T(8,128)S(1)}, bf16[136,512]{1,0:T(8,128)(2,1)S(1)}) custom-call(bf16[128,512]{1,0:T(8,128)(2,1)S(1)} %get-tuple-element.66.refs_0_, bf16[128,512]{1,0:T(8,128)(2,1)S(1)} %collective-permute-done.refs_1_, bf16[640,1024]{1,0:T(8,128)(2,1)S(1)} %get-tuple-element.72.kv_ref.refs_2_.refs_3_.refs_5_.kvm_ref, ...), custom_call_target="tpu_custom_call" | custom-call | flops 100000000 | bytes 8921088 | tf_op jit(solution)/shard_map/pallas_call | solution.py:37
  44.2 2.1 %collective-permute-start.10 = (bf16[136,512]{1,0:T(8,128)(2,1)S(1)}, bf16[136,512]{1,0:T(8,128)(2,1)S(1)}, u32[]{:S(2)}, u32[]{:S(2)}) collective-permute-start(bf16[136,512]{1,0:T(8,128)(2,1)S(1)} %get-tuple-element.78.refs_0_.packed_ref), channel_id=1, source_target_pairs={{0,8},{2,10},{4,12},{6,14},{8,0},{10,2},{12,4},{14,6},{16,24},{18,... | collective-permute-start | bytes 417800 | tf_op jit(solution)/shard_map/ppermute | solution.py:538
  46.9 2.3 %collective-permute-done.9.refs_0_ = bf16[136,512]{1,0:T(8,128)(2,1)S(1)} collective-permute-done((bf16[136,512]{1,0:T(8,128)(2,1)S(1)}, bf16[136,512]{1,0:T(8,128)(2,1)S(1)}, u32[]{:S(2)}, u32[]{:S(2)}) %collective-permute-start.9) | collective-permute-done | bytes 139296 | tf_op jit(solution)/shard_map/ppermute | solution.py:538
  57.2 7.7 %collective-permute-done.19.recv_ref = bf16[128,1024]{1,0:T(8,128)(2,1)S(1)} collective-permute-done((bf16[128,1024]{1,0:T(8,128)(2,1)S(1)}, bf16[128,1024]{1,0:T(8,128)(2,1)S(1)}, u32[]{:S(2)}, u32[]{:S(2)}) %collective-permute-start.19) | collective-permute-done | bytes 262176 | tf_op jit(solution)/shard_map/ppermute | solution.py:691
  66.1 2.6 %collective-permute-start.20 = (bf16[136,512]{1,0:T(8,128)(2,1)S(1)}, bf16[136,512]{1,0:T(8,128)(2,1)S(1)}, u32[]{:S(2)}, u32[]{:S(2)}) collective-permute-start(bf16[136,512]{1,0:T(8,128)(2,1)S(1)} %get-tuple-element.91.refs_0_.packed_ref), channel_id=1, source_target_pairs={{0,4},{2,6},{4,0},{6,2},{8,12},{10,14},{12,8},{14,10},{16,20},{18,... | collective-permute-start | bytes 417800 | tf_op jit(solution)/shard_map/ppermute | solution.py:538
  68.8 2.4 %collective-permute-start.21 = (bf16[136,512]{1,0:T(8,128)(2,1)S(1)}, bf16[136,512]{1,0:T(8,128)(2,1)S(1)}, u32[]{:S(2)}, u32[]{:S(2)}) collective-permute-start(bf16[136,512]{1,0:T(8,128)(2,1)S(1)} %get-tuple-element.91.refs_0_.packed_ref), channel_id=1, source_target_pairs={{0,8},{2,10},{4,12},{6,14},{8,0},{10,2},{12,4},{14,6},{16,24},{18,... | collective-permute-start | bytes 417800 | tf_op jit(solution)/shard_map/ppermute | solution.py:538
  71.7 2.4 %collective-permute-done.20.refs_0_ = bf16[136,512]{1,0:T(8,128)(2,1)S(1)} collective-permute-done((bf16[136,512]{1,0:T(8,128)(2,1)S(1)}, bf16[136,512]{1,0:T(8,128)(2,1)S(1)}, u32[]{:S(2)}, u32[]{:S(2)}) %collective-permute-start.20) | collective-permute-done | bytes 139296 | tf_op jit(solution)/shard_map/ppermute | solution.py:538
  75.2 3.6 %shard_map.101.ft_ref.refs_10_ = bf16[2,3,512,512]{3,2,1,0:T(8,128)(2,1)S(1)} custom-call(bf16[512,1024]{1,0:T(8,128)(2,1)S(1)} %get-tuple-element.77.refs_6_.wo_ref.w_ref, bf16[256,1024]{1,0:T(8,128)(2,1)S(1)} %collective-permute-done.29.mine_ref, bf16[256,1024]{1,0:T(8,128)(2,1)S(1)} %collective-permute-done.30.other_ref, ...), custom_call_target="tpu_custom_call" | custom-call | flops 100000000 | bytes 8392704 | tf_op jit(solution)/shard_map/pallas_call | solution.py:37
  84.5 5.4 %collective-permute-done.31.recv_ref = bf16[128,512]{1,0:T(8,128)(2,1)S(1)} collective-permute-done((bf16[128,512]{1,0:T(8,128)(2,1)S(1)}, bf16[128,512]{1,0:T(8,128)(2,1)S(1)}, u32[]{:S(2)}, u32[]{:S(2)}) %collective-permute-start.31) | collective-permute-done | bytes 131104 | tf_op jit(solution)/shard_map/ppermute | solution.py:526
  90.7 2.1 %collective-permute-start.32 = (bf16[136,512]{1,0:T(8,128)(2,1)S(1)}, bf16[136,512]{1,0:T(8,128)(2,1)S(1)}, u32[]{:S(2)}, u32[]{:S(2)}) collective-permute-start(bf16[136,512]{1,0:T(8,128)(2,1)S(1)} %shard_map.104.refs_0_.packed_ref), channel_id=1, source_target_pairs={{0,4},{2,6},{4,0},{6,2},{8,12},{10,14},{12,8},{14,10},{16,20},{18,... | collective-permute-start | bytes 417800 | tf_op jit(solution)/shard_map/ppermute | solution.py:538
  92.9 2.5 %collective-permute-start.33 = (bf16[136,512]{1,0:T(8,128)(2,1)S(1)}, bf16[136,512]{1,0:T(8,128)(2,1)S(1)}, u32[]{:S(2)}, u32[]{:S(2)}) collective-permute-start(bf16[136,512]{1,0:T(8,128)(2,1)S(1)} %shard_map.104.refs_0_.packed_ref), channel_id=1, source_target_pairs={{0,8},{2,10},{4,12},{6,14},{8,0},{10,2},{12,4},{14,6},{16,24},{18,... | collective-permute-start | bytes 417800 | tf_op jit(solution)/shard_map/ppermute | solution.py:538
  95.9 2.1 %collective-permute-done.32.refs_0_ = bf16[136,512]{1,0:T(8,128)(2,1)S(1)} collective-permute-done((bf16[136,512]{1,0:T(8,128)(2,1)S(1)}, bf16[136,512]{1,0:T(8,128)(2,1)S(1)}, u32[]{:S(2)}, u32[]{:S(2)}) %collective-permute-start.32) | collective-permute-done | bytes 139296 | tf_op jit(solution)/shard_map/ppermute | solution.py:538
  105.0 5.3 %collective-permute-done.41.recv_ref = bf16[128,512]{1,0:T(8,128)(2,1)S(1)} collective-permute-done((bf16[128,512]{1,0:T(8,128)(2,1)S(1)}, bf16[128,512]{1,0:T(8,128)(2,1)S(1)}, u32[]{:S(2)}, u32[]{:S(2)}) %collective-permute-start.41) | collective-permute-done | bytes 131104 | tf_op jit(solution)/shard_map/ppermute | solution.py:526
  111.2 2.1 %collective-permute-start.42 = (bf16[136,512]{1,0:T(8,128)(2,1)S(1)}, bf16[136,512]{1,0:T(8,128)(2,1)S(1)}, u32[]{:S(2)}, u32[]{:S(2)}) collective-permute-start(bf16[136,512]{1,0:T(8,128)(2,1)S(1)} %shard_map.109.refs_0_.packed_ref), channel_id=1, source_target_pairs={{0,4},{2,6},{4,0},{6,2},{8,12},{10,14},{12,8},{14,10},{16,20},{18,... | collective-permute-start | bytes 417800 | tf_op jit(solution)/shard_map/ppermute | solution.py:538
  113.3 2.5 %collective-permute-start.43 = (bf16[136,512]{1,0:T(8,128)(2,1)S(1)}, bf16[136,512]{1,0:T(8,128)(2,1)S(1)}, u32[]{:S(2)}, u32[]{:S(2)}) collective-permute-start(bf16[136,512]{1,0:T(8,128)(2,1)S(1)} %shard_map.109.refs_0_.packed_ref), channel_id=1, source_target_pairs={{0,8},{2,10},{4,12},{6,14},{8,0},{10,2},{12,4},{14,6},{16,24},{18,... | collective-permute-start | bytes 417800 | tf_op jit(solution)/shard_map/ppermute | solution.py:538
  116.3 2.0 %collective-permute-done.42.refs_0_ = bf16[136,512]{1,0:T(8,128)(2,1)S(1)} collective-permute-done((bf16[136,512]{1,0:T(8,128)(2,1)S(1)}, bf16[136,512]{1,0:T(8,128)(2,1)S(1)}, u32[]{:S(2)}, u32[]{:S(2)}) %collective-permute-start.42) | collective-permute-done | bytes 139296 | tf_op jit(solution)/shard_map/ppermute | solution.py:538
  130.2 2.7 %collective-permute-done.53.recv_ref = bf16[128,512]{1,0:T(8,128)(2,1)S(1)} collective-permute-done((bf16[128,512]{1,0:T(8,128)(2,1)S(1)}, bf16[128,512]{1,0:T(8,128)(2,1)S(1)}, u32[]{:S(2)}, u32[]{:S(2)}) %collective-permute-start.53) | collective-permute-done | bytes 131104 | tf_op jit(solution)/shard_map/ppermute | solution.py:526
  133.0 2.3 %collective-permute-done.51.recv_ref = bf16[128,512]{1,0:T(8,128)(2,1)S(1)} collective-permute-done((bf16[128,512]{1,0:T(8,128)(2,1)S(1)}, bf16[128,512]{1,0:T(8,128)(2,1)S(1)}, u32[]{:S(2)}, u32[]{:S(2)}) %collective-permute-start.51) | collective-permute-done | bytes 131104 | tf_op jit(solution)/shard_map/ppermute | solution.py:691
  135.7 10.5 %all_to_all.5.sums_ref = f32[32,1,128]{2,1,0:T(1,128)S(1)} all-to-all(f32[32,1,128]{2,1,0:T(1,128)S(1)} %get-tuple-element.128), channel_id=1, replica_groups=mesh['seq'=16,'tp'=2] {'seq','tp'}, dimensions={0} | all-to-all | bytes 32768 | tf_op jit(solution)/shard_map/all_to_all | solution.py:721
  (127 shorter events, 56.0 us)
Async XLA Ops:
  3.7 9.0 %collective-permute-start.1 = (bf16[128,512]{1,0:T(8,128)(2,1)}, bf16[128,512]{1,0:T(8,128)(2,1)S(1)}, u32[]{:S(2)}, u32[]{:S(2)}) collective-permute-start(bf16[128,512]{1,0:T(8,128)(2,1)} %state_ref.1), channel_id=1, source_target_pairs={{0,2},{2,0},{4,8},{6,10},{8,4},{10,6},{12,16},{14,18},{16,12},{18,... | collective-permute-start | bytes 393224 | tf_op jit(solution)/shard_map/ppermute | solution.py:538
  3.7 9.5 %collective-permute-start.3 = (bf16[128,512]{1,0:T(8,128)(2,1)}, bf16[128,512]{1,0:T(8,128)(2,1)S(1)}, u32[]{:S(2)}, u32[]{:S(2)}) collective-permute-start(bf16[128,512]{1,0:T(8,128)(2,1)} %state_ref.1), channel_id=1, source_target_pairs={{0,2},{2,0},{4,6},{6,4},{8,16},{10,18},{12,20},{14,22},{16,8},{18,... | collective-permute-start | bytes 393224 | tf_op jit(solution)/shard_map/ppermute | solution.py:538
  7.5 11.8 %collective-permute-start.6 = (bf16[128,1024]{1,0:T(8,128)(2,1)S(1)}, bf16[128,1024]{1,0:T(8,128)(2,1)S(1)}, u32[]{:S(2)}, u32[]{:S(2)}) collective-permute-start(bf16[128,1024]{1,0:T(8,128)(2,1)S(1)} %get-tuple-element.69.refs_4_), channel_id=1, source_target_pairs={{0,4},{2,6},{4,0},{6,2},{8,12},{10,14},{12,8},{14,10},{16,20},{18,... | collective-permute-start | bytes 786440 | tf_op jit(solution)/shard_map/ppermute | solution.py:538
  9.5 9.8 %collective-permute-start.7 = (bf16[128,1024]{1,0:T(8,128)(2,1)S(1)}, bf16[128,1024]{1,0:T(8,128)(2,1)S(1)}, u32[]{:S(2)}, u32[]{:S(2)}) collective-permute-start(bf16[128,1024]{1,0:T(8,128)(2,1)S(1)} %get-tuple-element.69.refs_4_), channel_id=1, source_target_pairs={{0,8},{2,10},{4,12},{6,14},{8,0},{10,2},{12,4},{14,6},{16,24},{18,... | collective-permute-start | bytes 786440 | tf_op jit(solution)/shard_map/ppermute | solution.py:538
  21.0 18.5 %collective-permute-start.8 = (bf16[640,1024]{1,0:T(8,128)(2,1)S(1)}, bf16[640,1024]{1,0:T(8,128)(2,1)S(1)}, u32[]{:S(2)}, u32[]{:S(2)}) collective-permute-start(bf16[640,1024]{1,0:T(8,128)(2,1)S(1)} %get-tuple-element.72.kv_ref.refs_2_.refs_3_.refs_5_.kvm_ref), channel_id=1, source_target_pairs={{0,2},{2,0},{4,6},{6,4},{8,10},{10,8},{12,14},{14,12},{16,18},{18,... | collective-permute-start | bytes 3932168 | tf_op jit(solution)/shard_map/ppermute | solution.py:521
  22.1 24.1 %collective-permute-start.13 = (bf16[640,512]{1,0:T(8,128)(2,1)S(1)}, bf16[640,512]{1,0:T(8,128)(2,1)S(1)}, u32[]{:S(2)}, u32[]{:S(2)}) collective-permute-start(bf16[640,512]{1,0:T(8,128)(2,1)S(1)} %get-tuple-element.75.refs_4_.qm_ref.refs_6_), channel_id=1, source_target_pairs={{0,2},{2,0},{4,6},{6,4},{8,10},{10,8},{12,14},{14,12},{16,18},{18,... | collective-permute-start | bytes 1966088 | tf_op jit(solution)/shard_map/ppermute | solution.py:521
  22.7 21.5 %collective-permute-start.29 = (bf16[256,1024]{1,0:T(8,128)(2,1)S(1)}, bf16[256,1024]{1,0:T(8,128)(2,1)S(1)}, u32[]{:S(2)}, u32[]{:S(2)}) collective-permute-start(bf16[256,1024]{1,0:T(8,128)(2,1)S(1)} %shard_map.100), channel_id=1, source_target_pairs={{1,0},{0,1},{3,2},{2,3},{5,4},{4,5},{7,6},{6,7},{9,8},{8,9},{11,10... | collective-permute-start | bytes 1572872 | tf_op jit(solution)/shard_map/ppermute | solution.py:526
  23.3 16.1 %collective-permute-start = (bf16[128,512]{1,0:T(8,128)(2,1)S(1)}, bf16[128,512]{1,0:T(8,128)(2,1)S(1)}, u32[]{:S(2)}, u32[]{:S(2)}) collective-permute-start(bf16[128,512]{1,0:T(8,128)(2,1)S(1)} %get-tuple-element.66.refs_0_), channel_id=1, source_target_pairs={{1,0},{0,1},{3,2},{2,3},{5,4},{4,5},{7,6},{6,7},{9,8},{8,9},{11,10... | collective-permute-start | bytes 393224 | tf_op jit(solution)/shard_map/ppermute | solution.py:526
  46.3 7.4 %collective-permute-start.16 = (bf16[136,512]{1,0:T(8,128)(2,1)S(1)}, bf16[136,512]{1,0:T(8,128)(2,1)S(1)}, u32[]{:S(2)}, u32[]{:S(2)}) collective-permute-start(bf16[136,512]{1,0:T(8,128)(2,1)S(1)} %collective-permute-done.14.refs_0_), channel_id=1, source_target_pairs={{0,2},{2,0},{4,6},{6,4},{8,10},{10,8},{12,14},{14,12},{16,18},{18,... | collective-permute-start | bytes 417800 | tf_op jit(solution)/shard_map/ppermute | solution.py:521
  50.2 21.0 %collective-permute-start.30 = (bf16[256,1024]{1,0:T(8,128)(2,1)S(1)}, bf16[256,1024]{1,0:T(8,128)(2,1)S(1)}, u32[]{:S(2)}, u32[]{:S(2)}) collective-permute-start(bf16[256,1024]{1,0:T(8,128)(2,1)S(1)} %collective-permute-done.29.mine_ref), channel_id=1, source_target_pairs={{0,2},{2,0},{4,6},{6,4},{8,10},{10,8},{12,14},{14,12},{16,18},{18,... | collective-permute-start | bytes 1572872 | tf_op jit(solution)/shard_map/ppermute | solution.py:521
  56.6 8.3 %collective-permute-start.19 = (bf16[128,1024]{1,0:T(8,128)(2,1)S(1)}, bf16[128,1024]{1,0:T(8,128)(2,1)S(1)}, u32[]{:S(2)}, u32[]{:S(2)}) collective-permute-start(bf16[128,1024]{1,0:T(8,128)(2,1)S(1)} %get-tuple-element.89), channel_id=1, source_target_pairs={{0,1},{1,0},{2,3},{3,2},{4,5},{5,4},{6,7},{7,6},{8,9},{9,8},{10,11... | collective-permute-start | bytes 786440 | tf_op jit(solution)/shard_map/ppermute | solution.py:691
  66.1 8.1 %collective-permute-start.20 = (bf16[136,512]{1,0:T(8,128)(2,1)S(1)}, bf16[136,512]{1,0:T(8,128)(2,1)S(1)}, u32[]{:S(2)}, u32[]{:S(2)}) collective-permute-start(bf16[136,512]{1,0:T(8,128)(2,1)S(1)} %get-tuple-element.91.refs_0_.packed_ref), channel_id=1, source_target_pairs={{0,4},{2,6},{4,0},{6,2},{8,12},{10,14},{12,8},{14,10},{16,20},{18,... | collective-permute-start | bytes 417800 | tf_op jit(solution)/shard_map/ppermute | solution.py:538
  71.2 9.4 %collective-permute-start.28 = (bf16[136,512]{1,0:T(8,128)(2,1)S(1)}, bf16[136,512]{1,0:T(8,128)(2,1)S(1)}, u32[]{:S(2)}, u32[]{:S(2)}) collective-permute-start(bf16[136,512]{1,0:T(8,128)(2,1)S(1)} %get-tuple-element.91.refs_0_.packed_ref), channel_id=1, source_target_pairs={{0,2},{2,0},{4,6},{6,4},{8,10},{10,8},{12,14},{14,12},{16,18},{18,... | collective-permute-start | bytes 417800 | tf_op jit(solution)/shard_map/ppermute | solution.py:521
  71.2 9.9 %collective-permute-start.26 = (bf16[136,512]{1,0:T(8,128)(2,1)S(1)}, bf16[136,512]{1,0:T(8,128)(2,1)S(1)}, u32[]{:S(2)}, u32[]{:S(2)}) collective-permute-start(bf16[136,512]{1,0:T(8,128)(2,1)S(1)} %collective-permute-done.24.refs_0_), channel_id=1, source_target_pairs={{0,2},{2,0},{4,6},{6,4},{8,10},{10,8},{12,14},{14,12},{16,18},{18,... | collective-permute-start | bytes 417800 | tf_op jit(solution)/shard_map/ppermute | solution.py:521
  71.7 9.4 %collective-permute-start.27 = (bf16[136,512]{1,0:T(8,128)(2,1)S(1)}, bf16[136,512]{1,0:T(8,128)(2,1)S(1)}, u32[]{:S(2)}, u32[]{:S(2)}) collective-permute-start(bf16[136,512]{1,0:T(8,128)(2,1)S(1)} %collective-permute-done.25.refs_1_), channel_id=1, source_target_pairs={{0,2},{2,0},{4,6},{6,4},{8,10},{10,8},{12,14},{14,12},{16,18},{18,... | collective-permute-start | bytes 417800 | tf_op jit(solution)/shard_map/ppermute | solution.py:521
  74.2 8.0 %collective-permute-start.22 = (bf16[136,512]{1,0:T(8,128)(2,1)S(1)}, bf16[136,512]{1,0:T(8,128)(2,1)S(1)}, u32[]{:S(2)}, u32[]{:S(2)}) collective-permute-start(bf16[136,512]{1,0:T(8,128)(2,1)S(1)} %collective-permute-done.20.refs_0_), channel_id=1, source_target_pairs={{0,2},{2,0},{4,6},{6,4},{8,10},{10,8},{12,14},{14,12},{16,18},{18,... | collective-permute-start | bytes 417800 | tf_op jit(solution)/shard_map/ppermute | solution.py:521
  90.7 7.2 %collective-permute-start.32 = (bf16[136,512]{1,0:T(8,128)(2,1)S(1)}, bf16[136,512]{1,0:T(8,128)(2,1)S(1)}, u32[]{:S(2)}, u32[]{:S(2)}) collective-permute-start(bf16[136,512]{1,0:T(8,128)(2,1)S(1)} %shard_map.104.refs_0_.packed_ref), channel_id=1, source_target_pairs={{0,4},{2,6},{4,0},{6,2},{8,12},{10,14},{12,8},{14,10},{16,20},{18,... | collective-permute-start | bytes 417800 | tf_op jit(solution)/shard_map/ppermute | solution.py:538
  111.2 7.2 %collective-permute-start.42 = (bf16[136,512]{1,0:T(8,128)(2,1)S(1)}, bf16[136,512]{1,0:T(8,128)(2,1)S(1)}, u32[]{:S(2)}, u32[]{:S(2)}) collective-permute-start(bf16[136,512]{1,0:T(8,128)(2,1)S(1)} %shard_map.109.refs_0_.packed_ref), channel_id=1, source_target_pairs={{0,4},{2,6},{4,0},{6,2},{8,12},{10,14},{12,8},{14,10},{16,20},{18,... | collective-permute-start | bytes 417800 | tf_op jit(solution)/shard_map/ppermute | solution.py:538
  115.7 7.9 %collective-permute-start.50 = (bf16[136,512]{1,0:T(8,128)(2,1)S(1)}, bf16[136,512]{1,0:T(8,128)(2,1)S(1)}, u32[]{:S(2)}, u32[]{:S(2)}) collective-permute-start(bf16[136,512]{1,0:T(8,128)(2,1)S(1)} %shard_map.109.refs_0_.packed_ref), channel_id=1, source_target_pairs={{0,2},{2,0},{4,6},{6,4},{8,10},{10,8},{12,14},{14,12},{16,18},{18,... | collective-permute-start | bytes 417800 | tf_op jit(solution)/shard_map/ppermute | solution.py:521
  115.8 9.2 %collective-permute-start.48 = (bf16[136,512]{1,0:T(8,128)(2,1)S(1)}, bf16[136,512]{1,0:T(8,128)(2,1)S(1)}, u32[]{:S(2)}, u32[]{:S(2)}) collective-permute-start(bf16[136,512]{1,0:T(8,128)(2,1)S(1)} %collective-permute-done.46.refs_0_), channel_id=1, source_target_pairs={{0,2},{2,0},{4,6},{6,4},{8,10},{10,8},{12,14},{14,12},{16,18},{18,... | collective-permute-start | bytes 417800 | tf_op jit(solution)/shard_map/ppermute | solution.py:521
  116.3 10.1 %collective-permute-start.49 = (bf16[136,512]{1,0:T(8,128)(2,1)S(1)}, bf16[136,512]{1,0:T(8,128)(2,1)S(1)}, u32[]{:S(2)}, u32[]{:S(2)}) collective-permute-start(bf16[136,512]{1,0:T(8,128)(2,1)S(1)} %collective-permute-done.47.refs_1_), channel_id=1, source_target_pairs={{0,2},{2,0},{4,6},{6,4},{8,10},{10,8},{12,14},{14,12},{16,18},{18,... | collective-permute-start | bytes 417800 | tf_op jit(solution)/shard_map/ppermute | solution.py:521
  118.3 9.1 %collective-permute-start.44 = (bf16[136,512]{1,0:T(8,128)(2,1)S(1)}, bf16[136,512]{1,0:T(8,128)(2,1)S(1)}, u32[]{:S(2)}, u32[]{:S(2)}) collective-permute-start(bf16[136,512]{1,0:T(8,128)(2,1)S(1)} %collective-permute-done.42.refs_0_), channel_id=1, source_target_pairs={{0,2},{2,0},{4,6},{6,4},{8,10},{10,8},{12,14},{14,12},{16,18},{18,... | collective-permute-start | bytes 417800 | tf_op jit(solution)/shard_map/ppermute | solution.py:521
  119.3 8.1 %collective-permute-start.45 = (bf16[136,512]{1,0:T(8,128)(2,1)S(1)}, bf16[136,512]{1,0:T(8,128)(2,1)S(1)}, u32[]{:S(2)}, u32[]{:S(2)}) collective-permute-start(bf16[136,512]{1,0:T(8,128)(2,1)S(1)} %collective-permute-done.43.refs_1_), channel_id=1, source_target_pairs={{0,2},{2,0},{4,6},{6,4},{8,10},{10,8},{12,14},{14,12},{16,18},{18,... | collective-permute-start | bytes 417800 | tf_op jit(solution)/shard_map/ppermute | solution.py:521
  125.0 7.9 %collective-permute-start.53 = (bf16[128,512]{1,0:T(8,128)(2,1)S(1)}, bf16[128,512]{1,0:T(8,128)(2,1)S(1)}, u32[]{:S(2)}, u32[]{:S(2)}) collective-permute-start(bf16[128,512]{1,0:T(8,128)(2,1)S(1)} %get-tuple-element.127), channel_id=1, source_target_pairs={{1,0},{0,1},{3,2},{2,3},{5,4},{4,5},{7,6},{6,7},{9,8},{8,9},{11,10... | collective-permute-start | bytes 393224 | tf_op jit(solution)/shard_map/ppermute | solution.py:526
  (34 other events, 177.4 us)

commit v7 on v6

--- a/solution.py
+++ b/solution.py
@@ -605,12 +605,7 @@
         got = got + [swap_core(x) for x in got]
         folded = fold and 1 <= n < SSTEP - 1
         if side is not None:
-            mine, other = kernel_call(
-                side_body,
-                [sds(rows, cols), sds(rows, cols, dtype=BF16)],
-                side + [w_query, w_key, w_value],
-                scratch=[pltpu.VMEM((rows, full), F32)],
-            )
+            mine, other = side
             other = tp_blocks(other)[1]
             (kry,) = kernel_call(
                 side_sum_body, [sds(rows, cols)], [mine, other, inv, gain]
@@ -668,7 +663,12 @@
                 [sds(rows + PAD, width, dtype=BF16)],
                 [own, recv, inv, att],
             )
-            side = [gq, gk, gv]
+            side = kernel_call(
+                side_body,
+                [sds(rows, cols), sds(rows, cols, dtype=BF16)],
+                [gq, gk, gv, w_query, w_key, w_value],
+                scratch=[pltpu.VMEM((rows, full), F32)],
+            )
             continue
         res = kernel_call(
             functools.partial(key_last_body, groups[2], first, halved),

time: 148 us -> 148 us (level)
  no operation moved by 1% of the time
where the time goes in v7:
time: 148 us
  waiting for transfers between devices  54.1 us (37%)
  starting transfers between devices  41.1 us (28%)
  Pallas kernels  38.1 us (26%)
  blocking collectives  10.5 us (7%)
  local copies, waits for them, and re-layouts  2.55 us (2%)
    pallas_call x34, Pallas kernels, kernel_call(): pl.pallas_call(body, out_shape=[jax.ShapeDtypeStruct(o.shape, o.dtype) fo...  38.1 us
    ppermute x9, waiting for transfers between devices, tp_blocks(): out.append(lax.ppermute(x, 'tp', [((i + k) % tps, i) for i in range(tps)]))  31.2 us
    ppermute x20, starting transfers between devices, hop(): return lax.ppermute(x, 'seq', pairs)  25.5 us
    ppermute x20, waiting for transfers between devices, hop(): return lax.ppermute(x, 'seq', pairs)  13 us
    ppermute x9, starting transfers between devices, tp_blocks(): out.append(lax.ppermute(x, 'tp', [((i + k) % tps, i) for i in range(tps)]))  10.6 us
    all_to_all x1, blocking collectives, on_device(): sums = lax.all_to_all(sums, ('seq', 'tp'), 0, 0)  10.5 us
    ppermute x2, waiting for transfers between devices, on_device(): recv = lax.ppermute(send, 'tp', [(i, i ^ k) for i in range(tps)])  9.94 us
    ppermute x23, starting transfers between devices, swap_core(): return lax.ppermute(x, 'seq', [(i, i ^ 1) for i in range(seq)])  3.61 us
  transfers between devices with their start and end apart: 54, of which 18 were waited for; matrix products, arithmetic and copies ran while one was open for 0% of the time, Pallas kernels for 21%

profile of v7, /device:TPU:0, one launch (start us, length us, event | category | flops | bytes accessed | tf_op | source)
XLA Modules:
  0.0 147.5 jit_solution(11235724070101545348)
XLA Ops:
  0.6 3.0 %collective-permute-start.5 = (bf16[128,512]{1,0:T(8,128)(2,1)}, bf16[128,512]{1,0:T(8,128)(2,1)S(1)}, u32[]{:S(2)}, u32[]{:S(2)}) collective-permute-start(bf16[128,512]{1,0:T(8,128)(2,1)} %state_ref.1), channel_id=1, source_target_pairs={{1,0},{0,1},{3,2},{2,3},{5,4},{4,5},{7,6},{6,7},{9,8},{8,9},{11,10... | collective-permute-start | bytes 393224 | tf_op jit(solution)/shard_map/ppermute | solution.py:526
  7.5 2.0 %collective-permute-start.6 = (bf16[128,1024]{1,0:T(8,128)(2,1)S(1)}, bf16[128,1024]{1,0:T(8,128)(2,1)S(1)}, u32[]{:S(2)}, u32[]{:S(2)}) collective-permute-start(bf16[128,1024]{1,0:T(8,128)(2,1)S(1)} %get-tuple-element.69.refs_4_), channel_id=1, source_target_pairs={{0,4},{2,6},{4,0},{6,2},{8,12},{10,14},{12,8},{14,10},{16,20},{18,... | collective-permute-start | bytes 786440 | tf_op jit(solution)/shard_map/ppermute | solution.py:538
  9.5 3.1 %collective-permute-start.7 = (bf16[128,1024]{1,0:T(8,128)(2,1)S(1)}, bf16[128,1024]{1,0:T(8,128)(2,1)S(1)}, u32[]{:S(2)}, u32[]{:S(2)}) collective-permute-start(bf16[128,1024]{1,0:T(8,128)(2,1)S(1)} %get-tuple-element.69.refs_4_), channel_id=1, source_target_pairs={{0,8},{2,10},{4,12},{6,14},{8,0},{10,2},{12,4},{14,6},{16,24},{18,... | collective-permute-start | bytes 786440 | tf_op jit(solution)/shard_map/ppermute | solution.py:538
  14.7 2.2 %shard_map.88 = (bf16[1024,512]{1,0:T(8,128)(2,1)S(1)}, bf16[1024,512]{1,0:T(8,128)(2,1)S(1)}, bf16[1024,512]{1,0:T(8,128)(2,1)S(1)}, bf16[512,1024]{1,0:T(8,128)(2,1)S(1)}) custom-call(bf16[1024,512]{1,0:T(8,128)(2,1)} %refs_0_.3, bf16[1024,512]{1,0:T(8,128)(2,1)} %refs_1_.1, bf16[1024,512]{1,0:T(8,128)(2,1)} %refs_2_.1, bf16[512,1024]{1,0:T(8,128)(2,1)} %refs_3_.1), custom_call_target="tpu_custom_call" | custom-call | flops 100000000 | bytes 8388608 | tf_op jit(solution)/shard_map/pallas_call | solution.py:37
  24.8 14.6 %collective-permute-done.refs_1_ = bf16[128,512]{1,0:T(8,128)(2,1)S(1)} collective-permute-done((bf16[128,512]{1,0:T(8,128)(2,1)S(1)}, bf16[128,512]{1,0:T(8,128)(2,1)S(1)}, u32[]{:S(2)}, u32[]{:S(2)}) %collective-permute-start) | collective-permute-done | bytes 131104 | tf_op jit(solution)/shard_map/ppermute | solution.py:526
  39.5 2.8 %shard_map.91 = (f32[4,128,1280]{2,1,0:T(8,128)S(1)}, f32[128,512]{1,0:T(8,128)S(1)}, bf16[136,512]{1,0:T(8,128)(2,1)S(1)}) custom-call(bf16[128,512]{1,0:T(8,128)(2,1)S(1)} %get-tuple-element.66.refs_0_, bf16[128,512]{1,0:T(8,128)(2,1)S(1)} %collective-permute-done.refs_1_, bf16[640,1024]{1,0:T(8,128)(2,1)S(1)} %get-tuple-element.72.kv_ref.refs_2_.refs_3_.refs_5_.kvm_ref, ...), custom_call_target="tpu_custom_call" | custom-call | flops 100000000 | bytes 8921088 | tf_op jit(solution)/shard_map/pallas_call | solution.py:37
  44.2 2.1 %collective-permute-start.10 = (bf16[136,512]{1,0:T(8,128)(2,1)S(1)}, bf16[136,512]{1,0:T(8,128)(2,1)S(1)}, u32[]{:S(2)}, u32[]{:S(2)}) collective-permute-start(bf16[136,512]{1,0:T(8,128)(2,1)S(1)} %get-tuple-element.78.refs_0_.packed_ref), channel_id=1, source_target_pairs={{0,8},{2,10},{4,12},{6,14},{8,0},{10,2},{12,4},{14,6},{16,24},{18,... | collective-permute-start | bytes 417800 | tf_op jit(solution)/shard_map/ppermute | solution.py:538
  46.9 2.3 %collective-permute-done.9.refs_0_ = bf16[136,512]{1,0:T(8,128)(2,1)S(1)} collective-permute-done((bf16[136,512]{1,0:T(8,128)(2,1)S(1)}, bf16[136,512]{1,0:T(8,128)(2,1)S(1)}, u32[]{:S(2)}, u32[]{:S(2)}) %collective-permute-start.9) | collective-permute-done | bytes 139296 | tf_op jit(solution)/shard_map/ppermute | solution.py:538
  57.2 7.7 %collective-permute-done.19.recv_ref = bf16[128,1024]{1,0:T(8,128)(2,1)S(1)} collective-permute-done((bf16[128,1024]{1,0:T(8,128)(2,1)S(1)}, bf16[128,1024]{1,0:T(8,128)(2,1)S(1)}, u32[]{:S(2)}, u32[]{:S(2)}) %collective-permute-start.19) | collective-permute-done | bytes 262176 | tf_op jit(solution)/shard_map/ppermute | solution.py:691
  66.1 2.6 %collective-permute-start.20 = (bf16[136,512]{1,0:T(8,128)(2,1)S(1)}, bf16[136,512]{1,0:T(8,128)(2,1)S(1)}, u32[]{:S(2)}, u32[]{:S(2)}) collective-permute-start(bf16[136,512]{1,0:T(8,128)(2,1)S(1)} %get-tuple-element.91.refs_0_.packed_ref), channel_id=1, source_target_pairs={{0,4},{2,6},{4,0},{6,2},{8,12},{10,14},{12,8},{14,10},{16,20},{18,... | collective-permute-start | bytes 417800 | tf_op jit(solution)/shard_map/ppermute | solution.py:538
  68.8 2.4 %collective-permute-start.21 = (bf16[136,512]{1,0:T(8,128)(2,1)S(1)}, bf16[136,512]{1,0:T(8,128)(2,1)S(1)}, u32[]{:S(2)}, u32[]{:S(2)}) collective-permute-start(bf16[136,512]{1,0:T(8,128)(2,1)S(1)} %get-tuple-element.91.refs_0_.packed_ref), channel_id=1, source_target_pairs={{0,8},{2,10},{4,12},{6,14},{8,0},{10,2},{12,4},{14,6},{16,24},{18,... | collective-permute-start | bytes 417800 | tf_op jit(solution)/shard_map/ppermute | solution.py:538
  71.7 2.4 %collective-permute-done.20.refs_0_ = bf16[136,512]{1,0:T(8,128)(2,1)S(1)} collective-permute-done((bf16[136,512]{1,0:T(8,128)(2,1)S(1)}, bf16[136,512]{1,0:T(8,128)(2,1)S(1)}, u32[]{:S(2)}, u32[]{:S(2)}) %collective-permute-start.20) | collective-permute-done | bytes 139296 | tf_op jit(solution)/shard_map/ppermute | solution.py:538
  75.2 3.6 %shard_map.101.ft_ref.refs_10_ = bf16[2,3,512,512]{3,2,1,0:T(8,128)(2,1)S(1)} custom-call(bf16[512,1024]{1,0:T(8,128)(2,1)S(1)} %get-tuple-element.77.refs_6_.wo_ref.w_ref, bf16[256,1024]{1,0:T(8,128)(2,1)S(1)} %collective-permute-done.29.mine_ref, bf16[256,1024]{1,0:T(8,128)(2,1)S(1)} %collective-permute-done.30.other_ref, ...), custom_call_target="tpu_custom_call" | custom-call | flops 100000000 | bytes 8392704 | tf_op jit(solution)/shard_map/pallas_call | solution.py:37
  84.5 5.4 %collective-permute-done.31.recv_ref = bf16[128,512]{1,0:T(8,128)(2,1)S(1)} collective-permute-done((bf16[128,512]{1,0:T(8,128)(2,1)S(1)}, bf16[128,512]{1,0:T(8,128)(2,1)S(1)}, u32[]{:S(2)}, u32[]{:S(2)}) %collective-permute-start.31) | collective-permute-done | bytes 131104 | tf_op jit(solution)/shard_map/ppermute | solution.py:526
  90.7 2.1 %collective-permute-start.32 = (bf16[136,512]{1,0:T(8,128)(2,1)S(1)}, bf16[136,512]{1,0:T(8,128)(2,1)S(1)}, u32[]{:S(2)}, u32[]{:S(2)}) collective-permute-start(bf16[136,512]{1,0:T(8,128)(2,1)S(1)} %shard_map.104.refs_0_.packed_ref), channel_id=1, source_target_pairs={{0,4},{2,6},{4,0},{6,2},{8,12},{10,14},{12,8},{14,10},{16,20},{18,... | collective-permute-start | bytes 417800 | tf_op jit(solution)/shard_map/ppermute | solution.py:538
  92.9 2.5 %collective-permute-start.33 = (bf16[136,512]{1,0:T(8,128)(2,1)S(1)}, bf16[136,512]{1,0:T(8,128)(2,1)S(1)}, u32[]{:S(2)}, u32[]{:S(2)}) collective-permute-start(bf16[136,512]{1,0:T(8,128)(2,1)S(1)} %shard_map.104.refs_0_.packed_ref), channel_id=1, source_target_pairs={{0,8},{2,10},{4,12},{6,14},{8,0},{10,2},{12,4},{14,6},{16,24},{18,... | collective-permute-start | bytes 417800 | tf_op jit(solution)/shard_map/ppermute | solution.py:538
  95.9 2.1 %collective-permute-done.32.refs_0_ = bf16[136,512]{1,0:T(8,128)(2,1)S(1)} collective-permute-done((bf16[136,512]{1,0:T(8,128)(2,1)S(1)}, bf16[136,512]{1,0:T(8,128)(2,1)S(1)}, u32[]{:S(2)}, u32[]{:S(2)}) %collective-permute-start.32) | collective-permute-done | bytes 139296 | tf_op jit(solution)/shard_map/ppermute | solution.py:538
  105.0 5.3 %collective-permute-done.41.recv_ref = bf16[128,512]{1,0:T(8,128)(2,1)S(1)} collective-permute-done((bf16[128,512]{1,0:T(8,128)(2,1)S(1)}, bf16[128,512]{1,0:T(8,128)(2,1)S(1)}, u32[]{:S(2)}, u32[]{:S(2)}) %collective-permute-start.41) | collective-permute-done | bytes 131104 | tf_op jit(solution)/shard_map/ppermute | solution.py:526
  111.2 2.1 %collective-permute-start.42 = (bf16[136,512]{1,0:T(8,128)(2,1)S(1)}, bf16[136,512]{1,0:T(8,128)(2,1)S(1)}, u32[]{:S(2)}, u32[]{:S(2)}) collective-permute-start(bf16[136,512]{1,0:T(8,128)(2,1)S(1)} %shard_map.109.refs_0_.packed_ref), channel_id=1, source_target_pairs={{0,4},{2,6},{4,0},{6,2},{8,12},{10,14},{12,8},{14,10},{16,20},{18,... | collective-permute-start | bytes 417800 | tf_op jit(solution)/shard_map/ppermute | solution.py:538
  113.3 2.5 %collective-permute-start.43 = (bf16[136,512]{1,0:T(8,128)(2,1)S(1)}, bf16[136,512]{1,0:T(8,128)(2,1)S(1)}, u32[]{:S(2)}, u32[]{:S(2)}) collective-permute-start(bf16[136,512]{1,0:T(8,128)(2,1)S(1)} %shard_map.109.refs_0_.packed_ref), channel_id=1, source_target_pairs={{0,8},{2,10},{4,12},{6,14},{8,0},{10,2},{12,4},{14,6},{16,24},{18,... | collective-permute-start | bytes 417800 | tf_op jit(solution)/shard_map/ppermute | solution.py:538
  116.3 2.0 %collective-permute-done.42.refs_0_ = bf16[136,512]{1,0:T(8,128)(2,1)S(1)} collective-permute-done((bf16[136,512]{1,0:T(8,128)(2,1)S(1)}, bf16[136,512]{1,0:T(8,128)(2,1)S(1)}, u32[]{:S(2)}, u32[]{:S(2)}) %collective-permute-start.42) | collective-permute-done | bytes 139296 | tf_op jit(solution)/shard_map/ppermute | solution.py:538
  130.2 2.7 %collective-permute-done.53.recv_ref = bf16[128,512]{1,0:T(8,128)(2,1)S(1)} collective-permute-done((bf16[128,512]{1,0:T(8,128)(2,1)S(1)}, bf16[128,512]{1,0:T(8,128)(2,1)S(1)}, u32[]{:S(2)}, u32[]{:S(2)}) %collective-permute-start.53) | collective-permute-done | bytes 131104 | tf_op jit(solution)/shard_map/ppermute | solution.py:526
  133.0 2.3 %collective-permute-done.51.recv_ref = bf16[128,512]{1,0:T(8,128)(2,1)S(1)} collective-permute-done((bf16[128,512]{1,0:T(8,128)(2,1)S(1)}, bf16[128,512]{1,0:T(8,128)(2,1)S(1)}, u32[]{:S(2)}, u32[]{:S(2)}) %collective-permute-start.51) | collective-permute-done | bytes 131104 | tf_op jit(solution)/shard_map/ppermute | solution.py:691
  135.7 10.5 %all_to_all.5.sums_ref = f32[32,1,128]{2,1,0:T(1,128)S(1)} all-to-all(f32[32,1,128]{2,1,0:T(1,128)S(1)} %get-tuple-element.128), channel_id=1, replica_groups=mesh['seq'=16,'tp'=2] {'seq','tp'}, dimensions={0} | all-to-all | bytes 32768 | tf_op jit(solution)/shard_map/all_to_all | solution.py:721
  (127 shorter events, 56.0 us)
Async XLA Ops:
  3.7 9.0 %collective-permute-start.1 = (bf16[128,512]{1,0:T(8,128)(2,1)}, bf16[128,512]{1,0:T(8,128)(2,1)S(1)}, u32[]{:S(2)}, u32[]{:S(2)}) collective-permute-start(bf16[128,512]{1,0:T(8,128)(2,1)} %state_ref.1), channel_id=1, source_target_pairs={{0,2},{2,0},{4,8},{6,10},{8,4},{10,6},{12,16},{14,18},{16,12},{18,... | collective-permute-start | bytes 393224 | tf_op jit(solution)/shard_map/ppermute | solution.py:538
  3.7 9.5 %collective-permute-start.3 = (bf16[128,512]{1,0:T(8,128)(2,1)}, bf16[128,512]{1,0:T(8,128)(2,1)S(1)}, u32[]{:S(2)}, u32[]{:S(2)}) collective-permute-start(bf16[128,512]{1,0:T(8,128)(2,1)} %state_ref.1), channel_id=1, source_target_pairs={{0,2},{2,0},{4,6},{6,4},{8,16},{10,18},{12,20},{14,22},{16,8},{18,... | collective-permute-start | bytes 393224 | tf_op jit(solution)/shard_map/ppermute | solution.py:538
  7.5 11.8 %collective-permute-start.6 = (bf16[128,1024]{1,0:T(8,128)(2,1)S(1)}, bf16[128,1024]{1,0:T(8,128)(2,1)S(1)}, u32[]{:S(2)}, u32[]{:S(2)}) collective-permute-start(bf16[128,1024]{1,0:T(8,128)(2,1)S(1)} %get-tuple-element.69.refs_4_), channel_id=1, source_target_pairs={{0,4},{2,6},{4,0},{6,2},{8,12},{10,14},{12,8},{14,10},{16,20},{18,... | collective-permute-start | bytes 786440 | tf_op jit(solution)/shard_map/ppermute | solution.py:538
  9.5 9.8 %collective-permute-start.7 = (bf16[128,1024]{1,0:T(8,128)(2,1)S(1)}, bf16[128,1024]{1,0:T(8,128)(2,1)S(1)}, u32[]{:S(2)}, u32[]{:S(2)}) collective-permute-start(bf16[128,1024]{1,0:T(8,128)(2,1)S(1)} %get-tuple-element.69.refs_4_), channel_id=1, source_target_pairs={{0,8},{2,10},{4,12},{6,14},{8,0},{10,2},{12,4},{14,6},{16,24},{18,... | collective-permute-start | bytes 786440 | tf_op jit(solution)/shard_map/ppermute | solution.py:538
  21.0 18.5 %collective-permute-start.8 = (bf16[640,1024]{1,0:T(8,128)(2,1)S(1)}, bf16[640,1024]{1,0:T(8,128)(2,1)S(1)}, u32[]{:S(2)}, u32[]{:S(2)}) collective-permute-start(bf16[640,1024]{1,0:T(8,128)(2,1)S(1)} %get-tuple-element.72.kv_ref.refs_2_.refs_3_.refs_5_.kvm_ref), channel_id=1, source_target_pairs={{0,2},{2,0},{4,6},{6,4},{8,10},{10,8},{12,14},{14,12},{16,18},{18,... | collective-permute-start | bytes 3932168 | tf_op jit(solution)/shard_map/ppermute | solution.py:521
  22.1 24.1 %collective-permute-start.13 = (bf16[640,512]{1,0:T(8,128)(2,1)S(1)}, bf16[640,512]{1,0:T(8,128)(2,1)S(1)}, u32[]{:S(2)}, u32[]{:S(2)}) collective-permute-start(bf16[640,512]{1,0:T(8,128)(2,1)S(1)} %get-tuple-element.75.refs_4_.qm_ref.refs_6_), channel_id=1, source_target_pairs={{0,2},{2,0},{4,6},{6,4},{8,10},{10,8},{12,14},{14,12},{16,18},{18,... | collective-permute-start | bytes 1966088 | tf_op jit(solution)/shard_map/ppermute | solution.py:521
  22.7 21.5 %collective-permute-start.29 = (bf16[256,1024]{1,0:T(8,128)(2,1)S(1)}, bf16[256,1024]{1,0:T(8,128)(2,1)S(1)}, u32[]{:S(2)}, u32[]{:S(2)}) collective-permute-start(bf16[256,1024]{1,0:T(8,128)(2,1)S(1)} %shard_map.100), channel_id=1, source_target_pairs={{1,0},{0,1},{3,2},{2,3},{5,4},{4,5},{7,6},{6,7},{9,8},{8,9},{11,10... | collective-permute-start | bytes 1572872 | tf_op jit(solution)/shard_map/ppermute | solution.py:526
  23.3 16.1 %collective-permute-start = (bf16[128,512]{1,0:T(8,128)(2,1)S(1)}, bf16[128,512]{1,0:T(8,128)(2,1)S(1)}, u32[]{:S(2)}, u32[]{:S(2)}) collective-permute-start(bf16[128,512]{1,0:T(8,128)(2,1)S(1)} %get-tuple-element.66.refs_0_), channel_id=1, source_target_pairs={{1,0},{0,1},{3,2},{2,3},{5,4},{4,5},{7,6},{6,7},{9,8},{8,9},{11,10... | collective-permute-start | bytes 393224 | tf_op jit(solution)/shard_map/ppermute | solution.py:526
  46.3 7.4 %collective-permute-start.16 = (bf16[136,512]{1,0:T(8,128)(2,1)S(1)}, bf16[136,512]{1,0:T(8,128)(2,1)S(1)}, u32[]{:S(2)}, u32[]{:S(2)}) collective-permute-start(bf16[136,512]{1,0:T(8,128)(2,1)S(1)} %collective-permute-done.14.refs_0_), channel_id=1, source_target_pairs={{0,2},{2,0},{4,6},{6,4},{8,10},{10,8},{12,14},{14,12},{16,18},{18,... | collective-permute-start | bytes 417800 | tf_op jit(solution)/shard_map/ppermute | solution.py:521
  50.2 21.0 %collective-permute-start.30 = (bf16[256,1024]{1,0:T(8,128)(2,1)S(1)}, bf16[256,1024]{1,0:T(8,128)(2,1)S(1)}, u32[]{:S(2)}, u32[]{:S(2)}) collective-permute-start(bf16[256,1024]{1,0:T(8,128)(2,1)S(1)} %collective-permute-done.29.mine_ref), channel_id=1, source_target_pairs={{0,2},{2,0},{4,6},{6,4},{8,10},{10,8},{12,14},{14,12},{16,18},{18,... | collective-permute-start | bytes 1572872 | tf_op jit(solution)/shard_map/ppermute | solution.py:521
  56.6 8.3 %collective-permute-start.19 = (bf16[128,1024]{1,0:T(8,128)(2,1)S(1)}, bf16[128,1024]{1,0:T(8,128)(2,1)S(1)}, u32[]{:S(2)}, u32[]{:S(2)}) collective-permute-start(bf16[128,1024]{1,0:T(8,128)(2,1)S(1)} %get-tuple-element.89), channel_id=1, source_target_pairs={{0,1},{1,0},{2,3},{3,2},{4,5},{5,4},{6,7},{7,6},{8,9},{9,8},{10,11... | collective-permute-start | bytes 786440 | tf_op jit(solution)/shard_map/ppermute | solution.py:691
  66.1 8.1 %collective-permute-start.20 = (bf16[136,512]{1,0:T(8,128)(2,1)S(1)}, bf16[136,512]{1,0:T(8,128)(2,1)S(1)}, u32[]{:S(2)}, u32[]{:S(2)}) collective-permute-start(bf16[136,512]{1,0:T(8,128)(2,1)S(1)} %get-tuple-element.91.refs_0_.packed_ref), channel_id=1, source_target_pairs={{0,4},{2,6},{4,0},{6,2},{8,12},{10,14},{12,8},{14,10},{16,20},{18,... | collective-permute-start | bytes 417800 | tf_op jit(solution)/shard_map/ppermute | solution.py:538
  71.2 9.4 %collective-permute-start.28 = (bf16[136,512]{1,0:T(8,128)(2,1)S(1)}, bf16[136,512]{1,0:T(8,128)(2,1)S(1)}, u32[]{:S(2)}, u32[]{:S(2)}) collective-permute-start(bf16[136,512]{1,0:T(8,128)(2,1)S(1)} %get-tuple-element.91.refs_0_.packed_ref), channel_id=1, source_target_pairs={{0,2},{2,0},{4,6},{6,4},{8,10},{10,8},{12,14},{14,12},{16,18},{18,... | collective-permute-start | bytes 417800 | tf_op jit(solution)/shard_map/ppermute | solution.py:521
  71.2 9.9 %collective-permute-start.26 = (bf16[136,512]{1,0:T(8,128)(2,1)S(1)}, bf16[136,512]{1,0:T(8,128)(2,1)S(1)}, u32[]{:S(2)}, u32[]{:S(2)}) collective-permute-start(bf16[136,512]{1,0:T(8,128)(2,1)S(1)} %collective-permute-done.24.refs_0_), channel_id=1, source_target_pairs={{0,2},{2,0},{4,6},{6,4},{8,10},{10,8},{12,14},{14,12},{16,18},{18,... | collective-permute-start | bytes 417800 | tf_op jit(solution)/shard_map/ppermute | solution.py:521
  71.7 9.4 %collective-permute-start.27 = (bf16[136,512]{1,0:T(8,128)(2,1)S(1)}, bf16[136,512]{1,0:T(8,128)(2,1)S(1)}, u32[]{:S(2)}, u32[]{:S(2)}) collective-permute-start(bf16[136,512]{1,0:T(8,128)(2,1)S(1)} %collective-permute-done.25.refs_1_), channel_id=1, source_target_pairs={{0,2},{2,0},{4,6},{6,4},{8,10},{10,8},{12,14},{14,12},{16,18},{18,... | collective-permute-start | bytes 417800 | tf_op jit(solution)/shard_map/ppermute | solution.py:521
  74.2 8.0 %collective-permute-start.22 = (bf16[136,512]{1,0:T(8,128)(2,1)S(1)}, bf16[136,512]{1,0:T(8,128)(2,1)S(1)}, u32[]{:S(2)}, u32[]{:S(2)}) collective-permute-start(bf16[136,512]{1,0:T(8,128)(2,1)S(1)} %collective-permute-done.20.refs_0_), channel_id=1, source_target_pairs={{0,2},{2,0},{4,6},{6,4},{8,10},{10,8},{12,14},{14,12},{16,18},{18,... | collective-permute-start | bytes 417800 | tf_op jit(solution)/shard_map/ppermute | solution.py:521
  90.7 7.2 %collective-permute-start.32 = (bf16[136,512]{1,0:T(8,128)(2,1)S(1)}, bf16[136,512]{1,0:T(8,128)(2,1)S(1)}, u32[]{:S(2)}, u32[]{:S(2)}) collective-permute-start(bf16[136,512]{1,0:T(8,128)(2,1)S(1)} %shard_map.104.refs_0_.packed_ref), channel_id=1, source_target_pairs={{0,4},{2,6},{4,0},{6,2},{8,12},{10,14},{12,8},{14,10},{16,20},{18,... | collective-permute-start | bytes 417800 | tf_op jit(solution)/shard_map/ppermute | solution.py:538
  111.2 7.2 %collective-permute-start.42 = (bf16[136,512]{1,0:T(8,128)(2,1)S(1)}, bf16[136,512]{1,0:T(8,128)(2,1)S(1)}, u32[]{:S(2)}, u32[]{:S(2)}) collective-permute-start(bf16[136,512]{1,0:T(8,128)(2,1)S(1)} %shard_map.109.refs_0_.packed_ref), channel_id=1, source_target_pairs={{0,4},{2,6},{4,0},{6,2},{8,12},{10,14},{12,8},{14,10},{16,20},{18,... | collective-permute-start | bytes 417800 | tf_op jit(solution)/shard_map/ppermute | solution.py:538
  115.7 7.9 %collective-permute-start.50 = (bf16[136,512]{1,0:T(8,128)(2,1)S(1)}, bf16[136,512]{1,0:T(8,128)(2,1)S(1)}, u32[]{:S(2)}, u32[]{:S(2)}) collective-permute-start(bf16[136,512]{1,0:T(8,128)(2,1)S(1)} %shard_map.109.refs_0_.packed_ref), channel_id=1, source_target_pairs={{0,2},{2,0},{4,6},{6,4},{8,10},{10,8},{12,14},{14,12},{16,18},{18,... | collective-permute-start | bytes 417800 | tf_op jit(solution)/shard_map/ppermute | solution.py:521
  115.8 9.2 %collective-permute-start.48 = (bf16[136,512]{1,0:T(8,128)(2,1)S(1)}, bf16[136,512]{1,0:T(8,128)(2,1)S(1)}, u32[]{:S(2)}, u32[]{:S(2)}) collective-permute-start(bf16[136,512]{1,0:T(8,128)(2,1)S(1)} %collective-permute-done.46.refs_0_), channel_id=1, source_target_pairs={{0,2},{2,0},{4,6},{6,4},{8,10},{10,8},{12,14},{14,12},{16,18},{18,... | collective-permute-start | bytes 417800 | tf_op jit(solution)/shard_map/ppermute | solution.py:521
  116.3 10.1 %collective-permute-start.49 = (bf16[136,512]{1,0:T(8,128)(2,1)S(1)}, bf16[136,512]{1,0:T(8,128)(2,1)S(1)}, u32[]{:S(2)}, u32[]{:S(2)}) collective-permute-start(bf16[136,512]{1,0:T(8,128)(2,1)S(1)} %collective-permute-done.47.refs_1_), channel_id=1, source_target_pairs={{0,2},{2,0},{4,6},{6,4},{8,10},{10,8},{12,14},{14,12},{16,18},{18,... | collective-permute-start | bytes 417800 | tf_op jit(solution)/shard_map/ppermute | solution.py:521
  118.3 9.1 %collective-permute-start.44 = (bf16[136,512]{1,0:T(8,128)(2,1)S(1)}, bf16[136,512]{1,0:T(8,128)(2,1)S(1)}, u32[]{:S(2)}, u32[]{:S(2)}) collective-permute-start(bf16[136,512]{1,0:T(8,128)(2,1)S(1)} %collective-permute-done.42.refs_0_), channel_id=1, source_target_pairs={{0,2},{2,0},{4,6},{6,4},{8,10},{10,8},{12,14},{14,12},{16,18},{18,... | collective-permute-start | bytes 417800 | tf_op jit(solution)/shard_map/ppermute | solution.py:521
  119.3 8.1 %collective-permute-start.45 = (bf16[136,512]{1,0:T(8,128)(2,1)S(1)}, bf16[136,512]{1,0:T(8,128)(2,1)S(1)}, u32[]{:S(2)}, u32[]{:S(2)}) collective-permute-start(bf16[136,512]{1,0:T(8,128)(2,1)S(1)} %collective-permute-done.43.refs_1_), channel_id=1, source_target_pairs={{0,2},{2,0},{4,6},{6,4},{8,10},{10,8},{12,14},{14,12},{16,18},{18,... | collective-permute-start | bytes 417800 | tf_op jit(solution)/shard_map/ppermute | solution.py:521
  125.0 7.9 %collective-permute-start.53 = (bf16[128,512]{1,0:T(8,128)(2,1)S(1)}, bf16[128,512]{1,0:T(8,128)(2,1)S(1)}, u32[]{:S(2)}, u32[]{:S(2)}) collective-permute-start(bf16[128,512]{1,0:T(8,128)(2,1)S(1)} %get-tuple-element.127), channel_id=1, source_target_pairs={{1,0},{0,1},{3,2},{2,3},{5,4},{4,5},{7,6},{6,7},{9,8},{8,9},{11,10... | collective-permute-start | bytes 393224 | tf_op jit(solution)/shard_map/ppermute | solution.py:526
  (34 other events, 177.4 us)

commit v8 on v7

--- a/solution.py
+++ b/solution.py
@@ -30,7 +30,7 @@
     return slice(h * HD, (h + 1) * HD)
 
 
-def kernel_call(body, outs, ins, scratch=(), hbm=0, flops=10**8, limit=12 << 20):
+def kernel_call(body, outs, ins, scratch=(), hbm=0, flops=10**8, limit=12 << 20, aliases=None):
     in_specs = [pl.BlockSpec(memory_space=pltpu.HBM)] * hbm
     in_specs += [pl.BlockSpec(memory_space=pltpu.VMEM)] * (len(ins) - hbm)
     moved = sum(math.prod(a.shape) * a.dtype.itemsize for a in list(ins) + list(outs))
@@ -40,6 +40,7 @@
         in_specs=in_specs,
         out_specs=[pl.BlockSpec(memory_space=pltpu.VMEM)] * len(outs),
         scratch_shapes=list(scratch),
+        input_output_aliases=aliases or {},
         compiler_params=pltpu.CompilerParams(vmem_limit_bytes=limit),
         cost_estimate=pl.CostEstimate(flops=flops, bytes_accessed=moved, transcendentals=0),
     )(*ins)
@@ -159,23 +160,36 @@
         normed_ref[:, sl] = piece
 
 
-def kv_body(raw, done, tps, *refs):
-    xs = refs[: raw * tps]
-    full = refs[raw * tps : raw * tps + done]
-    gain_ref, wk_ref, wv_ref, kv_ref, normed_ref = refs[raw * tps + done :]
+def kv_first_body(raw, done, *refs):
+    full = refs[:done]
+    wk_ref, wv_ref, kv_ref, normed_ref = refs[done:]
     rows = full[0].shape[0]
     width = wk_ref.shape[1]
-    at = feature_slices(tps, full[0].shape[1] // tps)
+    x = jnp.concatenate([r[...] for r in full], axis=0)
+    keys = mm(x, wk_ref[...]).astype(BF16)
+    values = mm(x, wv_ref[...]).astype(BF16)
+    for i, ref in enumerate(full):
+        b = i if i == 0 else i + raw
+        there, here = slice(b * rows, (b + 1) * rows), slice(i * rows, (i + 1) * rows)
+        normed_ref[there, :] = ref[...]
+        kv_ref[there, :width] = keys[here]
+        kv_ref[there, width:] = values[here]
+
+
+def kv_rest_body(raw, tps, *refs):
+    xs = refs[: raw * tps]
+    gain_ref, wk_ref, wv_ref, _, _, kv_ref, normed_ref = refs[raw * tps :]
+    rows, cols = xs[0].shape
+    width = wk_ref.shape[1]
+    at = feature_slices(tps, cols)
     for b in range(raw):
         _, pieces = norm_block(xs[b * tps : (b + 1) * tps], gain_ref, at)
         for sl, piece in zip(at, pieces):
             normed_ref[(b + 1) * rows : (b + 2) * rows, sl] = piece
-    for i, x in enumerate(full):
-        b = i if i == 0 else i + raw
-        normed_ref[b * rows : (b + 1) * rows, :] = x[...]
-    x = normed_ref[...]
-    kv_ref[:, :width] = mm(x, wk_ref[...]).astype(BF16)
-    kv_ref[:, width:] = mm(x, wv_ref[...]).astype(BF16)
+    new = slice(rows, (raw + 1) * rows)
+    x = normed_ref[new, :]
+    kv_ref[new, :width] = mm(x, wk_ref[...]).astype(BF16)
+    kv_ref[new, width:] = mm(x, wv_ref[...]).astype(BF16)
 
 
 def q_body(rows, normed_ref, wq_ref, kv_ref, q_ref, s_ref):
@@ -566,13 +580,19 @@
         limit=49 << 20,
     )
     cots = tp_blocks(cot_low)
+    shapes = [
+        sds(blocks * rows, 2 * width, dtype=BF16),
+        sds(blocks * rows, full, dtype=BF16),
+    ]
     kv_mine, normed = kernel_call(
-        functools.partial(kv_body, raw, len(done), tps),
-        [
-            sds(blocks * rows, 2 * width, dtype=BF16),
-            sds(blocks * rows, full, dtype=BF16),
-        ],
-        pieces + done + [gain, w_key, w_value],
+        functools.partial(kv_first_body, raw, len(done)), shapes, done + [w_key, w_value]
+    )
+    inputs = pieces + [gain, w_key, w_value]
+    kv_mine, normed = kernel_call(
+        functools.partial(kv_rest_body, raw, tps),
+        shapes,
+        inputs + [kv_mine, normed],
+        aliases={len(inputs): 0, len(inputs) + 1: 1},
     )
     kv_other = swap_core(kv_mine)
     q_mine, s_mine = kernel_call(

time: 148 us -> 156 us (1.054)
  starting transfers between devices: 41.1 us -> 52 us
  waiting for transfers between devices: 54.1 us -> 50.3 us
    ppermute x20, starting transfers between devices: 25.5 us -> 33.2 us  [hop(): return lax.ppermute(x, 'seq', pairs)]
    ppermute x9, waiting for transfers between devices: 31.2 us -> 28.8 us  [tp_blocks(): out.append(lax.ppermute(x, 'tp', [((i + k) % tps, i) for i in range(tps)]))]
    ppermute x9, starting transfers between devices: 10.6 us -> 12.2 us  [tp_blocks(): out.append(lax.ppermute(x, 'tp', [((i + k) % tps, i) for i in range(tps)]))]
    pallas_call x34 -> x35, Pallas kernels: 38.1 us -> 38.6 us  [kernel_call(): pl.pallas_call(body, out_shape=[jax.ShapeDtypeStruct(o.shape, o.dtype) fo...]
  transfers between devices with their start and end apart: 54 -> 54, of which waited for: 18 -> 18; matrix products, arithmetic and copies ran while one was open for 0% -> 0% of each run, Pallas kernels for 21% -> 20%
where the time goes in v8:
time: 156 us
  starting transfers between devices  52 us (33%)
  waiting for transfers between devices  50.3 us (32%)
  Pallas kernels  38.6 us (25%)
  blocking collectives  11 us (7%)
  local copies, waits for them, and re-layouts  2.55 us (2%)
    pallas_call x35, Pallas kernels, kernel_call(): pl.pallas_call(body, out_shape=[jax.ShapeDtypeStruct(o.shape, o.dtype) fo...  38.6 us
    ppermute x20, starting transfers between devices, hop(): return lax.ppermute(x, 'seq', pairs)  33.2 us
    ppermute x9, waiting for transfers between devices, tp_blocks(): out.append(lax.ppermute(x, 'tp', [((i + k) % tps, i) for i in range(tps)]))  28.8 us
    ppermute x20, waiting for transfers between devices, hop(): return lax.ppermute(x, 'seq', pairs)  12.4 us
    ppermute x9, starting transfers between devices, tp_blocks(): out.append(lax.ppermute(x, 'tp', [((i + k) % tps, i) for i in range(tps)]))  12.2 us
    all_to_all x1, blocking collectives, on_device(): sums = lax.all_to_all(sums, ('seq', 'tp'), 0, 0)  11 us
    ppermute x2, waiting for transfers between devices, on_device(): recv = lax.ppermute(send, 'tp', [(i, i ^ k) for i in range(tps)])  9.07 us
    ppermute x23, starting transfers between devices, swap_core(): return lax.ppermute(x, 'seq', [(i, i ^ 1) for i in range(seq)])  3.61 us
  transfers between devices with their start and end apart: 54, of which 18 were waited for; matrix products, arithmetic and copies ran while one was open for 0% of the time, Pallas kernels for 20%

profile of v8, /device:TPU:0, one launch (start us, length us, event | category | flops | bytes accessed | tf_op | source)
XLA Modules:
  0.0 155.5 jit_solution(18160235131905694949)
XLA Ops:
  0.6 3.0 %collective-permute-start.5 = (bf16[128,512]{1,0:T(8,128)(2,1)}, bf16[128,512]{1,0:T(8,128)(2,1)S(1)}, u32[]{:S(2)}, u32[]{:S(2)}) collective-permute-start(bf16[128,512]{1,0:T(8,128)(2,1)} %state_ref.1), channel_id=1, source_target_pairs={{1,0},{0,1},{3,2},{2,3},{5,4},{4,5},{7,6},{6,7},{9,8},{8,9},{11,10... | collective-permute-start | bytes 393224 | tf_op jit(solution)/shard_map/ppermute | solution.py:540
  7.5 1.8 %collective-permute-start.6 = (bf16[128,1024]{1,0:T(8,128)(2,1)S(1)}, bf16[128,1024]{1,0:T(8,128)(2,1)S(1)}, u32[]{:S(2)}, u32[]{:S(2)}) collective-permute-start(bf16[128,1024]{1,0:T(8,128)(2,1)S(1)} %get-tuple-element.73.refs_0_), channel_id=1, source_target_pairs={{0,4},{2,6},{4,0},{6,2},{8,12},{10,14},{12,8},{14,10},{16,20},{18,... | collective-permute-start | bytes 786440 | tf_op jit(solution)/shard_map/ppermute | solution.py:552
  14.3 2.2 %shard_map.87 = (bf16[1024,512]{1,0:T(8,128)(2,1)S(1)}, bf16[1024,512]{1,0:T(8,128)(2,1)S(1)}, bf16[1024,512]{1,0:T(8,128)(2,1)S(1)}, bf16[512,1024]{1,0:T(8,128)(2,1)S(1)}) custom-call(bf16[1024,512]{1,0:T(8,128)(2,1)} %refs_0_.3, bf16[1024,512]{1,0:T(8,128)(2,1)} %refs_1_.1, bf16[1024,512]{1,0:T(8,128)(2,1)} %refs_2_.1, bf16[512,1024]{1,0:T(8,128)(2,1)} %refs_3_.1), custom_call_target="tpu_custom_call" | custom-call | flops 100000000 | bytes 8388608 | tf_op jit(solution)/shard_map/pallas_call | solution.py:37
  18.7 2.0 %collective-permute-done.4.refs_3_ = bf16[128,512]{1,0:T(8,128)(2,1)S(1)} collective-permute-done((bf16[128,512]{1,0:T(8,128)(2,1)S(1)}, bf16[128,512]{1,0:T(8,128)(2,1)S(1)}, u32[]{:S(2)}, u32[]{:S(2)}) %collective-permute-start.4) | collective-permute-done | bytes 131104 | tf_op jit(solution)/shard_map/ppermute | solution.py:540
  25.4 14.6 %collective-permute-done.refs_1_ = bf16[128,512]{1,0:T(8,128)(2,1)S(1)} collective-permute-done((bf16[128,512]{1,0:T(8,128)(2,1)S(1)}, bf16[128,512]{1,0:T(8,128)(2,1)S(1)}, u32[]{:S(2)}, u32[]{:S(2)}) %collective-permute-start) | collective-permute-done | bytes 131104 | tf_op jit(solution)/shard_map/ppermute | solution.py:540
  40.0 2.8 %shard_map.92 = (f32[4,128,1280]{2,1,0:T(8,128)S(1)}, f32[128,512]{1,0:T(8,128)S(1)}, bf16[136,512]{1,0:T(8,128)(2,1)S(1)}) custom-call(bf16[128,512]{1,0:T(8,128)(2,1)S(1)} %get-tuple-element.68.refs_0_, bf16[128,512]{1,0:T(8,128)(2,1)S(1)} %collective-permute-done.refs_1_, bf16[640,1024]{1,0:T(8,128)(2,1)S(1)} %get-tuple-element.76.kv_ref.refs_2_.refs_3_.refs_5_.kvm_ref, ...), custom_call_target="tpu_custom_call" | custom-call | flops 100000000 | bytes 8921088 | tf_op jit(solution)/shard_map/pallas_call | solution.py:37
  43.4 7.4 %collective-permute-start.9 = (bf16[136,512]{1,0:T(8,128)(2,1)S(1)}, bf16[136,512]{1,0:T(8,128)(2,1)S(1)}, u32[]{:S(2)}, u32[]{:S(2)}) collective-permute-start(bf16[136,512]{1,0:T(8,128)(2,1)S(1)} %get-tuple-element.82.refs_0_.packed_ref), channel_id=1, source_target_pairs={{0,4},{2,6},{4,0},{6,2},{8,12},{10,14},{12,8},{14,10},{16,20},{18,... | collective-permute-start | bytes 417800 | tf_op jit(solution)/shard_map/ppermute | solution.py:552
  50.8 3.1 %collective-permute-start.10 = (bf16[136,512]{1,0:T(8,128)(2,1)S(1)}, bf16[136,512]{1,0:T(8,128)(2,1)S(1)}, u32[]{:S(2)}, u32[]{:S(2)}) collective-permute-start(bf16[136,512]{1,0:T(8,128)(2,1)S(1)} %get-tuple-element.82.refs_0_.packed_ref), channel_id=1, source_target_pairs={{0,8},{2,10},{4,12},{6,14},{8,0},{10,2},{12,4},{14,6},{16,24},{18,... | collective-permute-start | bytes 417800 | tf_op jit(solution)/shard_map/ppermute | solution.py:552
  64.8 6.8 %collective-permute-done.19.recv_ref = bf16[128,1024]{1,0:T(8,128)(2,1)S(1)} collective-permute-done((bf16[128,1024]{1,0:T(8,128)(2,1)S(1)}, bf16[128,1024]{1,0:T(8,128)(2,1)S(1)}, u32[]{:S(2)}, u32[]{:S(2)}) %collective-permute-start.19) | collective-permute-done | bytes 262176 | tf_op jit(solution)/shard_map/ppermute | solution.py:711
  72.9 3.0 %collective-permute-start.20 = (bf16[136,512]{1,0:T(8,128)(2,1)S(1)}, bf16[136,512]{1,0:T(8,128)(2,1)S(1)}, u32[]{:S(2)}, u32[]{:S(2)}) collective-permute-start(bf16[136,512]{1,0:T(8,128)(2,1)S(1)} %get-tuple-element.95.refs_0_.packed_ref), channel_id=1, source_target_pairs={{0,4},{2,6},{4,0},{6,2},{8,12},{10,14},{12,8},{14,10},{16,20},{18,... | collective-permute-start | bytes 417800 | tf_op jit(solution)/shard_map/ppermute | solution.py:552
  75.9 2.9 %collective-permute-start.21 = (bf16[136,512]{1,0:T(8,128)(2,1)S(1)}, bf16[136,512]{1,0:T(8,128)(2,1)S(1)}, u32[]{:S(2)}, u32[]{:S(2)}) collective-permute-start(bf16[136,512]{1,0:T(8,128)(2,1)S(1)} %get-tuple-element.95.refs_0_.packed_ref), channel_id=1, source_target_pairs={{0,8},{2,10},{4,12},{6,14},{8,0},{10,2},{12,4},{14,6},{16,24},{18,... | collective-permute-start | bytes 417800 | tf_op jit(solution)/shard_map/ppermute | solution.py:552
  81.9 3.7 %shard_map.102.ft_ref.refs_10_ = bf16[2,3,512,512]{3,2,1,0:T(8,128)(2,1)S(1)} custom-call(bf16[512,1024]{1,0:T(8,128)(2,1)S(1)} %get-tuple-element.81.refs_6_.wo_ref.w_ref, bf16[256,1024]{1,0:T(8,128)(2,1)S(1)} %collective-permute-done.29.mine_ref, bf16[256,1024]{1,0:T(8,128)(2,1)S(1)} %collective-permute-done.30.other_ref, ...), custom_call_target="tpu_custom_call" | custom-call | flops 100000000 | bytes 8392704 | tf_op jit(solution)/shard_map/pallas_call | solution.py:37
  89.0 1.8 %shard_map.104 = (f32[128,512]{1,0:T(8,128)S(1)}, bf16[128,512]{1,0:T(8,128)(2,1)S(1)}, bf16[128,512]{1,0:T(8,128)(2,1)S(1)}, bf16[128,512]{1,0:T(8,128)(2,1)S(1)}) custom-call(bf16[136,512]{1,0:T(8,128)(2,1)S(1)} %collective-permute-done.20.refs_0_, bf16[136,512]{1,0:T(8,128)(2,1)S(1)} %collective-permute-done.21.refs_1_, ...), custom_call_target="tpu_custom_call" | custom-call | flops 100000000 | bytes 9076736 | tf_op jit(solution)/shard_map/pallas_call | solution.py:37
  92.2 4.5 %collective-permute-done.31.recv_ref = bf16[128,512]{1,0:T(8,128)(2,1)S(1)} collective-permute-done((bf16[128,512]{1,0:T(8,128)(2,1)S(1)}, bf16[128,512]{1,0:T(8,128)(2,1)S(1)}, u32[]{:S(2)}, u32[]{:S(2)}) %collective-permute-start.31) | collective-permute-done | bytes 131104 | tf_op jit(solution)/shard_map/ppermute | solution.py:540
  97.5 3.0 %collective-permute-start.32 = (bf16[136,512]{1,0:T(8,128)(2,1)S(1)}, bf16[136,512]{1,0:T(8,128)(2,1)S(1)}, u32[]{:S(2)}, u32[]{:S(2)}) collective-permute-start(bf16[136,512]{1,0:T(8,128)(2,1)S(1)} %shard_map.105.refs_0_.packed_ref), channel_id=1, source_target_pairs={{0,4},{2,6},{4,0},{6,2},{8,12},{10,14},{12,8},{14,10},{16,20},{18,... | collective-permute-start | bytes 417800 | tf_op jit(solution)/shard_map/ppermute | solution.py:552
  100.5 2.6 %collective-permute-start.33 = (bf16[136,512]{1,0:T(8,128)(2,1)S(1)}, bf16[136,512]{1,0:T(8,128)(2,1)S(1)}, u32[]{:S(2)}, u32[]{:S(2)}) collective-permute-start(bf16[136,512]{1,0:T(8,128)(2,1)S(1)} %shard_map.105.refs_0_.packed_ref), channel_id=1, source_target_pairs={{0,8},{2,10},{4,12},{6,14},{8,0},{10,2},{12,4},{14,6},{16,24},{18,... | collective-permute-start | bytes 417800 | tf_op jit(solution)/shard_map/ppermute | solution.py:552
  112.9 4.5 %collective-permute-done.41.recv_ref = bf16[128,512]{1,0:T(8,128)(2,1)S(1)} collective-permute-done((bf16[128,512]{1,0:T(8,128)(2,1)S(1)}, bf16[128,512]{1,0:T(8,128)(2,1)S(1)}, u32[]{:S(2)}, u32[]{:S(2)}) %collective-permute-start.41) | collective-permute-done | bytes 131104 | tf_op jit(solution)/shard_map/ppermute | solution.py:540
  118.3 2.8 %collective-permute-start.42 = (bf16[136,512]{1,0:T(8,128)(2,1)S(1)}, bf16[136,512]{1,0:T(8,128)(2,1)S(1)}, u32[]{:S(2)}, u32[]{:S(2)}) collective-permute-start(bf16[136,512]{1,0:T(8,128)(2,1)S(1)} %shard_map.110.refs_0_.packed_ref), channel_id=1, source_target_pairs={{0,4},{2,6},{4,0},{6,2},{8,12},{10,14},{12,8},{14,10},{16,20},{18,... | collective-permute-start | bytes 417800 | tf_op jit(solution)/shard_map/ppermute | solution.py:552
  121.1 2.1 %collective-permute-start.43 = (bf16[136,512]{1,0:T(8,128)(2,1)S(1)}, bf16[136,512]{1,0:T(8,128)(2,1)S(1)}, u32[]{:S(2)}, u32[]{:S(2)}) collective-permute-start(bf16[136,512]{1,0:T(8,128)(2,1)S(1)} %shard_map.110.refs_0_.packed_ref), channel_id=1, source_target_pairs={{0,8},{2,10},{4,12},{6,14},{8,0},{10,2},{12,4},{14,6},{16,24},{18,... | collective-permute-start | bytes 417800 | tf_op jit(solution)/shard_map/ppermute | solution.py:552
  129.3 1.9 %shard_map.113.refs_12_ = f32[128,1024]{1,0:T(8,128)S(1)} custom-call(bf16[136,512]{1,0:T(8,128)(2,1)S(1)} %shard_map.110.refs_0_.packed_ref, f32[128,512]{1,0:T(8,128)S(1)} %get-tuple-element.90.att_ref, f32[4,128,1280]{2,1,0:T(8,128)S(1)} %get-tuple-element.91.p_ref, bf16[640,1024]{1,0:T(8,128)(2,1)S(1)} %get-tuple-element.76.kv_ref.refs_2_.refs_3_.refs_5_.kvm_ref, ...), custom_call_target="tpu_custom_call" | custom-call | flops 100000000 | bytes 7217152 | tf_op jit(solution)/shard_map/pallas_call | solution.py:37
  135.1 1.8 %shard_map.114 = (f32[128,512]{1,0:T(8,128)S(1)}, bf16[128,512]{1,0:T(8,128)(2,1)S(1)}) custom-call(bf16[136,512]{1,0:T(8,128)(2,1)S(1)} %collective-permute-done.42.refs_0_, bf16[136,512]{1,0:T(8,128)(2,1)S(1)} %collective-permute-done.43.refs_1_, bf16[136,512]{1,0:T(8,128)(2,1)S(1)} %collective-permute-done.44.refs_2_, ...), custom_call_target="tpu_custom_call" | custom-call | flops 100000000 | bytes 7766016 | tf_op jit(solution)/shard_map/pallas_call | solution.py:37
  138.5 2.1 %collective-permute-done.53.recv_ref = bf16[128,512]{1,0:T(8,128)(2,1)S(1)} collective-permute-done((bf16[128,512]{1,0:T(8,128)(2,1)S(1)}, bf16[128,512]{1,0:T(8,128)(2,1)S(1)}, u32[]{:S(2)}, u32[]{:S(2)}) %collective-permute-start.53) | collective-permute-done | bytes 131104 | tf_op jit(solution)/shard_map/ppermute | solution.py:540
  140.6 2.2 %collective-permute-done.51.recv_ref = bf16[128,512]{1,0:T(8,128)(2,1)S(1)} collective-permute-done((bf16[128,512]{1,0:T(8,128)(2,1)S(1)}, bf16[128,512]{1,0:T(8,128)(2,1)S(1)}, u32[]{:S(2)}, u32[]{:S(2)}) %collective-permute-start.51) | collective-permute-done | bytes 131104 | tf_op jit(solution)/shard_map/ppermute | solution.py:711
  143.3 11.0 %all_to_all.5.sums_ref = f32[32,1,128]{2,1,0:T(1,128)S(1)} all-to-all(f32[32,1,128]{2,1,0:T(1,128)S(1)} %get-tuple-element.132), channel_id=1, replica_groups=mesh['seq'=16,'tp'=2] {'seq','tp'}, dimensions={0} | all-to-all | bytes 32768 | tf_op jit(solution)/shard_map/all_to_all | solution.py:741
  (128 shorter events, 60.7 us)
Async XLA Ops:
  7.5 9.0 %collective-permute-start.6 = (bf16[128,1024]{1,0:T(8,128)(2,1)S(1)}, bf16[128,1024]{1,0:T(8,128)(2,1)S(1)}, u32[]{:S(2)}, u32[]{:S(2)}) collective-permute-start(bf16[128,1024]{1,0:T(8,128)(2,1)S(1)} %get-tuple-element.73.refs_0_), channel_id=1, source_target_pairs={{0,4},{2,6},{4,0},{6,2},{8,12},{10,14},{12,8},{14,10},{16,20},{18,... | collective-permute-start | bytes 786440 | tf_op jit(solution)/shard_map/ppermute | solution.py:552
  9.4 8.3 %collective-permute-start.7 = (bf16[128,1024]{1,0:T(8,128)(2,1)S(1)}, bf16[128,1024]{1,0:T(8,128)(2,1)S(1)}, u32[]{:S(2)}, u32[]{:S(2)}) collective-permute-start(bf16[128,1024]{1,0:T(8,128)(2,1)S(1)} %get-tuple-element.73.refs_0_), channel_id=1, source_target_pairs={{0,8},{2,10},{4,12},{6,14},{8,0},{10,2},{12,4},{14,6},{16,24},{18,... | collective-permute-start | bytes 786440 | tf_op jit(solution)/shard_map/ppermute | solution.py:552
  21.5 18.5 %collective-permute-start.8 = (bf16[640,1024]{1,0:T(8,128)(2,1)S(1)}, bf16[640,1024]{1,0:T(8,128)(2,1)S(1)}, u32[]{:S(2)}, u32[]{:S(2)}) collective-permute-start(bf16[640,1024]{1,0:T(8,128)(2,1)S(1)} %get-tuple-element.76.kv_ref.refs_2_.refs_3_.refs_5_.kvm_ref), channel_id=1, source_target_pairs={{0,2},{2,0},{4,6},{6,4},{8,10},{10,8},{12,14},{14,12},{16,18},{18,... | collective-permute-start | bytes 3932168 | tf_op jit(solution)/shard_map/ppermute | solution.py:535
  22.7 31.2 %collective-permute-start.13 = (bf16[640,512]{1,0:T(8,128)(2,1)S(1)}, bf16[640,512]{1,0:T(8,128)(2,1)S(1)}, u32[]{:S(2)}, u32[]{:S(2)}) collective-permute-start(bf16[640,512]{1,0:T(8,128)(2,1)S(1)} %get-tuple-element.79.refs_4_.qm_ref.refs_6_), channel_id=1, source_target_pairs={{0,2},{2,0},{4,6},{6,4},{8,10},{10,8},{12,14},{14,12},{16,18},{18,... | collective-permute-start | bytes 1966088 | tf_op jit(solution)/shard_map/ppermute | solution.py:535
  23.3 27.5 %collective-permute-start.29 = (bf16[256,1024]{1,0:T(8,128)(2,1)S(1)}, bf16[256,1024]{1,0:T(8,128)(2,1)S(1)}, u32[]{:S(2)}, u32[]{:S(2)}) collective-permute-start(bf16[256,1024]{1,0:T(8,128)(2,1)S(1)} %shard_map.101), channel_id=1, source_target_pairs={{1,0},{0,1},{3,2},{2,3},{5,4},{4,5},{7,6},{6,7},{9,8},{8,9},{11,10... | collective-permute-start | bytes 1572872 | tf_op jit(solution)/shard_map/ppermute | solution.py:540
  24.8 15.2 %collective-permute-start = (bf16[128,512]{1,0:T(8,128)(2,1)S(1)}, bf16[128,512]{1,0:T(8,128)(2,1)S(1)}, u32[]{:S(2)}, u32[]{:S(2)}) collective-permute-start(bf16[128,512]{1,0:T(8,128)(2,1)S(1)} %get-tuple-element.68.refs_0_), channel_id=1, source_target_pairs={{1,0},{0,1},{3,2},{2,3},{5,4},{4,5},{7,6},{6,7},{9,8},{8,9},{11,10... | collective-permute-start | bytes 393224 | tf_op jit(solution)/shard_map/ppermute | solution.py:540
  42.8 11.1 %collective-permute-start.14 = (bf16[136,512]{1,0:T(8,128)(2,1)S(1)}, bf16[136,512]{1,0:T(8,128)(2,1)S(1)}, u32[]{:S(2)}, u32[]{:S(2)}) collective-permute-start(bf16[136,512]{1,0:T(8,128)(2,1)S(1)} %get-tuple-element.82.refs_0_.packed_ref), channel_id=1, source_target_pairs={{0,2},{2,0},{4,8},{6,10},{8,4},{10,6},{12,16},{14,18},{16,12},{18,... | collective-permute-start | bytes 417800 | tf_op jit(solution)/shard_map/ppermute | solution.py:552
  42.9 11.6 %collective-permute-start.15 = (bf16[136,512]{1,0:T(8,128)(2,1)S(1)}, bf16[136,512]{1,0:T(8,128)(2,1)S(1)}, u32[]{:S(2)}, u32[]{:S(2)}) collective-permute-start(bf16[136,512]{1,0:T(8,128)(2,1)S(1)} %get-tuple-element.82.refs_0_.packed_ref), channel_id=1, source_target_pairs={{0,2},{2,0},{4,6},{6,4},{8,16},{10,18},{12,20},{14,22},{16,8},{18,... | collective-permute-start | bytes 417800 | tf_op jit(solution)/shard_map/ppermute | solution.py:552
  43.4 12.3 %collective-permute-start.9 = (bf16[136,512]{1,0:T(8,128)(2,1)S(1)}, bf16[136,512]{1,0:T(8,128)(2,1)S(1)}, u32[]{:S(2)}, u32[]{:S(2)}) collective-permute-start(bf16[136,512]{1,0:T(8,128)(2,1)S(1)} %get-tuple-element.82.refs_0_.packed_ref), channel_id=1, source_target_pairs={{0,4},{2,6},{4,0},{6,2},{8,12},{10,14},{12,8},{14,10},{16,20},{18,... | collective-permute-start | bytes 417800 | tf_op jit(solution)/shard_map/ppermute | solution.py:552
  57.0 21.9 %collective-permute-start.30 = (bf16[256,1024]{1,0:T(8,128)(2,1)S(1)}, bf16[256,1024]{1,0:T(8,128)(2,1)S(1)}, u32[]{:S(2)}, u32[]{:S(2)}) collective-permute-start(bf16[256,1024]{1,0:T(8,128)(2,1)S(1)} %collective-permute-done.29.mine_ref), channel_id=1, source_target_pairs={{0,2},{2,0},{4,6},{6,4},{8,10},{10,8},{12,14},{14,12},{16,18},{18,... | collective-permute-start | bytes 1572872 | tf_op jit(solution)/shard_map/ppermute | solution.py:535
  63.3 8.3 %collective-permute-start.19 = (bf16[128,1024]{1,0:T(8,128)(2,1)S(1)}, bf16[128,1024]{1,0:T(8,128)(2,1)S(1)}, u32[]{:S(2)}, u32[]{:S(2)}) collective-permute-start(bf16[128,1024]{1,0:T(8,128)(2,1)S(1)} %get-tuple-element.93), channel_id=1, source_target_pairs={{0,1},{1,0},{2,3},{3,2},{4,5},{5,4},{6,7},{7,6},{8,9},{9,8},{10,11... | collective-permute-start | bytes 786440 | tf_op jit(solution)/shard_map/ppermute | solution.py:711
  72.9 7.8 %collective-permute-start.20 = (bf16[136,512]{1,0:T(8,128)(2,1)S(1)}, bf16[136,512]{1,0:T(8,128)(2,1)S(1)}, u32[]{:S(2)}, u32[]{:S(2)}) collective-permute-start(bf16[136,512]{1,0:T(8,128)(2,1)S(1)} %get-tuple-element.95.refs_0_.packed_ref), channel_id=1, source_target_pairs={{0,4},{2,6},{4,0},{6,2},{8,12},{10,14},{12,8},{14,10},{16,20},{18,... | collective-permute-start | bytes 417800 | tf_op jit(solution)/shard_map/ppermute | solution.py:552
  78.8 8.4 %collective-permute-start.28 = (bf16[136,512]{1,0:T(8,128)(2,1)S(1)}, bf16[136,512]{1,0:T(8,128)(2,1)S(1)}, u32[]{:S(2)}, u32[]{:S(2)}) collective-permute-start(bf16[136,512]{1,0:T(8,128)(2,1)S(1)} %get-tuple-element.95.refs_0_.packed_ref), channel_id=1, source_target_pairs={{0,2},{2,0},{4,6},{6,4},{8,10},{10,8},{12,14},{14,12},{16,18},{18,... | collective-permute-start | bytes 417800 | tf_op jit(solution)/shard_map/ppermute | solution.py:535
  78.9 9.0 %collective-permute-start.26 = (bf16[136,512]{1,0:T(8,128)(2,1)S(1)}, bf16[136,512]{1,0:T(8,128)(2,1)S(1)}, u32[]{:S(2)}, u32[]{:S(2)}) collective-permute-start(bf16[136,512]{1,0:T(8,128)(2,1)S(1)} %collective-permute-done.24.refs_0_), channel_id=1, source_target_pairs={{0,2},{2,0},{4,6},{6,4},{8,10},{10,8},{12,14},{14,12},{16,18},{18,... | collective-permute-start | bytes 417800 | tf_op jit(solution)/shard_map/ppermute | solution.py:535
  79.4 8.5 %collective-permute-start.27 = (bf16[136,512]{1,0:T(8,128)(2,1)S(1)}, bf16[136,512]{1,0:T(8,128)(2,1)S(1)}, u32[]{:S(2)}, u32[]{:S(2)}) collective-permute-start(bf16[136,512]{1,0:T(8,128)(2,1)S(1)} %collective-permute-done.25.refs_1_), channel_id=1, source_target_pairs={{0,2},{2,0},{4,6},{6,4},{8,10},{10,8},{12,14},{14,12},{16,18},{18,... | collective-permute-start | bytes 417800 | tf_op jit(solution)/shard_map/ppermute | solution.py:535
  80.7 8.2 %collective-permute-start.22 = (bf16[136,512]{1,0:T(8,128)(2,1)S(1)}, bf16[136,512]{1,0:T(8,128)(2,1)S(1)}, u32[]{:S(2)}, u32[]{:S(2)}) collective-permute-start(bf16[136,512]{1,0:T(8,128)(2,1)S(1)} %collective-permute-done.20.refs_0_), channel_id=1, source_target_pairs={{0,2},{2,0},{4,6},{6,4},{8,10},{10,8},{12,14},{14,12},{16,18},{18,... | collective-permute-start | bytes 417800 | tf_op jit(solution)/shard_map/ppermute | solution.py:535
  97.5 7.4 %collective-permute-start.32 = (bf16[136,512]{1,0:T(8,128)(2,1)S(1)}, bf16[136,512]{1,0:T(8,128)(2,1)S(1)}, u32[]{:S(2)}, u32[]{:S(2)}) collective-permute-start(bf16[136,512]{1,0:T(8,128)(2,1)S(1)} %shard_map.105.refs_0_.packed_ref), channel_id=1, source_target_pairs={{0,4},{2,6},{4,0},{6,2},{8,12},{10,14},{12,8},{14,10},{16,20},{18,... | collective-permute-start | bytes 417800 | tf_op jit(solution)/shard_map/ppermute | solution.py:552
  118.3 7.2 %collective-permute-start.42 = (bf16[136,512]{1,0:T(8,128)(2,1)S(1)}, bf16[136,512]{1,0:T(8,128)(2,1)S(1)}, u32[]{:S(2)}, u32[]{:S(2)}) collective-permute-start(bf16[136,512]{1,0:T(8,128)(2,1)S(1)} %shard_map.110.refs_0_.packed_ref), channel_id=1, source_target_pairs={{0,4},{2,6},{4,0},{6,2},{8,12},{10,14},{12,8},{14,10},{16,20},{18,... | collective-permute-start | bytes 417800 | tf_op jit(solution)/shard_map/ppermute | solution.py:552
  123.3 8.0 %collective-permute-start.50 = (bf16[136,512]{1,0:T(8,128)(2,1)S(1)}, bf16[136,512]{1,0:T(8,128)(2,1)S(1)}, u32[]{:S(2)}, u32[]{:S(2)}) collective-permute-start(bf16[136,512]{1,0:T(8,128)(2,1)S(1)} %shard_map.110.refs_0_.packed_ref), channel_id=1, source_target_pairs={{0,2},{2,0},{4,6},{6,4},{8,10},{10,8},{12,14},{14,12},{16,18},{18,... | collective-permute-start | bytes 417800 | tf_op jit(solution)/shard_map/ppermute | solution.py:535
  123.3 9.9 %collective-permute-start.48 = (bf16[136,512]{1,0:T(8,128)(2,1)S(1)}, bf16[136,512]{1,0:T(8,128)(2,1)S(1)}, u32[]{:S(2)}, u32[]{:S(2)}) collective-permute-start(bf16[136,512]{1,0:T(8,128)(2,1)S(1)} %collective-permute-done.46.refs_0_), channel_id=1, source_target_pairs={{0,2},{2,0},{4,6},{6,4},{8,10},{10,8},{12,14},{14,12},{16,18},{18,... | collective-permute-start | bytes 417800 | tf_op jit(solution)/shard_map/ppermute | solution.py:535
  123.8 10.2 %collective-permute-start.49 = (bf16[136,512]{1,0:T(8,128)(2,1)S(1)}, bf16[136,512]{1,0:T(8,128)(2,1)S(1)}, u32[]{:S(2)}, u32[]{:S(2)}) collective-permute-start(bf16[136,512]{1,0:T(8,128)(2,1)S(1)} %collective-permute-done.47.refs_1_), channel_id=1, source_target_pairs={{0,2},{2,0},{4,6},{6,4},{8,10},{10,8},{12,14},{14,12},{16,18},{18,... | collective-permute-start | bytes 417800 | tf_op jit(solution)/shard_map/ppermute | solution.py:535
  125.5 9.6 %collective-permute-start.44 = (bf16[136,512]{1,0:T(8,128)(2,1)S(1)}, bf16[136,512]{1,0:T(8,128)(2,1)S(1)}, u32[]{:S(2)}, u32[]{:S(2)}) collective-permute-start(bf16[136,512]{1,0:T(8,128)(2,1)S(1)} %collective-permute-done.42.refs_0_), channel_id=1, source_target_pairs={{0,2},{2,0},{4,6},{6,4},{8,10},{10,8},{12,14},{14,12},{16,18},{18,... | collective-permute-start | bytes 417800 | tf_op jit(solution)/shard_map/ppermute | solution.py:535
  126.9 8.1 %collective-permute-start.45 = (bf16[136,512]{1,0:T(8,128)(2,1)S(1)}, bf16[136,512]{1,0:T(8,128)(2,1)S(1)}, u32[]{:S(2)}, u32[]{:S(2)}) collective-permute-start(bf16[136,512]{1,0:T(8,128)(2,1)S(1)} %collective-permute-done.43.refs_1_), channel_id=1, source_target_pairs={{0,2},{2,0},{4,6},{6,4},{8,10},{10,8},{12,14},{14,12},{16,18},{18,... | collective-permute-start | bytes 417800 | tf_op jit(solution)/shard_map/ppermute | solution.py:535
  133.3 7.3 %collective-permute-start.53 = (bf16[128,512]{1,0:T(8,128)(2,1)S(1)}, bf16[128,512]{1,0:T(8,128)(2,1)S(1)}, u32[]{:S(2)}, u32[]{:S(2)}) collective-permute-start(bf16[128,512]{1,0:T(8,128)(2,1)S(1)} %get-tuple-element.131), channel_id=1, source_target_pairs={{1,0},{0,1},{3,2},{2,3},{5,4},{4,5},{7,6},{6,7},{9,8},{8,9},{11,10... | collective-permute-start | bytes 393224 | tf_op jit(solution)/shard_map/ppermute | solution.py:540
  (34 other events, 175.6 us)
